TPU v7x, 32 devices: a whole 2x2x4 slice. The times are simulated.
32 devices in a mesh: fsdp: 8 (over z, y), tp: 4 (over x, core).
Axes of the slice: x: 2, y: 2, z: 4, core: 2. Of those that a mesh axis runs over, the one named last changes fastest.
Arguments:
- hidden_in: bfloat16 [32768, 1024], P(('fsdp', 'tp')), may hold values from -8 to 8
- cotangent: bfloat16 [32768, 1024], P(('fsdp', 'tp')), may hold values from -6 to 6
- norm1_gain: bfloat16 [1024], replicated, may hold values from 0.5 to 1.5
- norm1_bias: bfloat16 [1024], replicated, may hold values from -3 to 3
- w_query: bfloat16 [1024, 1024], P('fsdp', 'tp'), may hold values from -0.25 to 0.25
- w_key: bfloat16 [1024, 1024], P('fsdp', 'tp'), may hold values from -0.1875 to 0.1875
- w_value: bfloat16 [1024, 1024], P('fsdp', 'tp'), may hold values from -0.1875 to 0.1875
- w_out: bfloat16 [1024, 1024], P('tp', 'fsdp'), may hold values from -1.5 to 1.5
- norm2_gain: bfloat16 [1024], replicated, may hold values from 0.5 to 1.5
- norm2_bias: bfloat16 [1024], replicated, may hold values from -3 to 3
- w_fc1: bfloat16 [1024, 4096], P('fsdp', 'tp'), may hold values from -0.1875 to 0.1875
- bias_fc1: bfloat16 [4096], P('tp'), may hold values from -3 to 3
- w_fc2: bfloat16 [4096, 1024], P('tp', 'fsdp'), may hold values from -0.09375 to 0.09375
- bias_fc2: bfloat16 [1024], replicated, may hold values from -3 to 3
- segments: int32 [8, 4096], P('fsdp'), may hold values from 0 to 9, as said below
- random_blocks: int32 [8, 16, 62, 3], P('fsdp', 'tp'), may hold values from 1 to 62, as said below
Outputs:
- layer_out: bfloat16 [32768, 1024], P(('fsdp', 'tp'))
- grad_input: float32 [32768, 1024], P(('fsdp', 'tp'))
- grad_norm1_gain: float32 [1024], replicated
- grad_norm1_bias: float32 [1024], replicated
- grad_w_query: float32 [1024, 1024], P('fsdp', 'tp')
- grad_w_key: float32 [1024, 1024], P('fsdp', 'tp')
- grad_w_value: float32 [1024, 1024], P('fsdp', 'tp')
- grad_w_out: float32 [1024, 1024], P('tp', 'fsdp')
- grad_norm2_gain: float32 [1024], replicated
- grad_norm2_bias: float32 [1024], replicated
- grad_w_fc1: float32 [1024, 4096], P('fsdp', 'tp')
- grad_bias_fc1: float32 [4096], P('tp')
- grad_w_fc2: float32 [4096, 1024], P('tp', 'fsdp')
- grad_bias_fc2: float32 [1024], replicated
- residual_rms: float32 [4], replicated
Inputs may be any that keep to these rules, and one draw needn't show every extreme that they name: `segments`: in each row the segment numbers never fall over the non-padding tokens, all of 1 to 9 occur, and the row ends with 1 to 512 padding tokens of segment 0. `random_blocks`: for the query block b of row b - 1, the 3 numbers are distinct and none equals b - 1, b or b + 1.
All inputs are finite; a program needn't handle non-finite values.
Results may differ from a plain program's by a relative error of at most 0.012.
The roundings to bfloat16 on the way count: a program that leaves them out, or rounds other values in their place, can miss the bound.
Values may be sent and summed in bfloat16 or wider, within the bound.
No kernel may reach another device: no remote copies, remote signals or barrier semaphores. Data moves between devices by JAX's collectives and lax.ppermute only.
A program may use at most 448 MiB of HBM per device.

v0:
```python
from functools import partial

import jax
import jax.numpy as jnp
from jax import lax
from jax.sharding import PartitionSpec as P

HEAD_DIM = 64
BLOCK = 64


eps_norm = 1e-05
neg_large = -1e30


def norm_rows(source, gain_vec, shift_vec):
    average = jnp.mean(source, axis=-1, keepdims=True)
    centred = source - average
    variance = jnp.mean(centred * centred, axis=-1, keepdims=True)
    return centred * lax.rsqrt(variance + eps_norm) * gain_vec + shift_vec


def gelu_tanh(values):
    return jax.nn.gelu(values, approximate=True)


def product(left, right):
    return jnp.dot(left, right, preferred_element_type=jnp.float32)


def inner_rows(left, right):
    return lax.dot_general(
        left, right, (((0,), (0,)), ((), ())), preferred_element_type=jnp.float32
    )


def inner_cols(left, right):
    return lax.dot_general(
        left, right, (((1,), (1,)), ((), ())), preferred_element_type=jnp.float32
    )


def attn_spread(source):
    return lax.all_gather(source, "tp", axis=0, tiled=True)


def attn_collect(terms):
    return lax.psum_scatter(terms, "tp", scatter_dimension=0, tiled=True)


def ffn_spread(source):
    return lax.all_gather(source, "tp", axis=0, tiled=True)


def ffn_collect(terms):
    return lax.psum_scatter(terms, "tp", scatter_dimension=0, tiled=True)


def head_blocks(flat, heads_local):
    return flat.reshape(flat.shape[0] // BLOCK, BLOCK, heads_local, -1).transpose(2, 0, 1, 3)


def head_flat(blocks):
    heads_local, nblocks, block_len, head_width = blocks.shape
    return blocks.transpose(1, 2, 0, 3).reshape(nblocks * block_len, heads_local * head_width)


def take_blocks(blocks, index):
    return blocks[index]


def add_blocks(terms, index, nblocks):
    return jnp.zeros((nblocks,) + terms.shape[1:], jnp.float32).at[index].add(terms)


def block_layout(seq_segs, random_local):
    heads_local, count_mid, rand_count = random_local.shape
    seq_len = seq_segs.shape[0]
    nblocks = count_mid + 2
    middle_ids = jnp.arange(1, nblocks - 1, dtype=jnp.int32)
    window_ids = middle_ids[:, None] + jnp.arange(-1, 2, dtype=jnp.int32)[None, :]
    global_ids = jnp.broadcast_to(jnp.array([0, nblocks - 1], jnp.int32)[None, :], (count_mid, 2))
    fixed_ids = jnp.concatenate([window_ids, global_ids], 1)
    slot_idx = jnp.concatenate(
        [jnp.broadcast_to(fixed_ids[None], (heads_local, count_mid, 5)), random_local], 2
    )
    window_live = (window_ids != 0) & (window_ids != nblocks - 1)
    slot_live = jnp.concatenate([window_live, jnp.ones((count_mid, 2 + rand_count), jnp.bool_)], 1)
    slot_count = 5 + rand_count
    block_segs = seq_segs.reshape(nblocks, BLOCK)
    key_segs = block_segs[slot_idx].reshape(heads_local, count_mid, slot_count * BLOCK)
    query_segs = block_segs[1:-1]
    key_live = jnp.repeat(slot_live, BLOCK, axis=1)
    same_doc = (
        (query_segs[None, :, :, None] == key_segs[:, :, None, :])
        & (key_segs[:, :, None, :] != 0)
        & key_live[None, :, None, :]
    )
    slot_pos = jnp.arange(slot_count * BLOCK, dtype=jnp.int32)
    self_pos = slot_pos[None, :] == jnp.arange(BLOCK, dtype=jnp.int32)[:, None] + BLOCK
    mid_mask = same_doc | self_pos[None, None]
    positions = jnp.arange(seq_len, dtype=jnp.int32)
    glob_pos = jnp.concatenate([positions[:BLOCK], positions[seq_len - BLOCK :]])
    glob_segs = jnp.concatenate([seq_segs[:BLOCK], seq_segs[seq_len - BLOCK :]])
    glob_mask = (glob_segs[:, None] == seq_segs[None, :]) & (seq_segs[None, :] != 0) | (
        glob_pos[:, None] == positions[None, :]
    )
    return (slot_idx, mid_mask, glob_mask)


def prepare(queries, key_rows, value_rows, seq_segs, random_local):
    heads_local, count_mid, rand_count = random_local.shape
    seq_len = seq_segs.shape[0]
    slot_idx, mid_mask, glob_mask = block_layout(seq_segs, random_local)
    query_blk = head_blocks(queries, heads_local)
    key_blk = head_blocks(key_rows, heads_local)
    value_blk = head_blocks(value_rows, heads_local)
    span = (5 + rand_count) * BLOCK
    key_sel = jax.vmap(take_blocks)(key_blk, slot_idx).reshape(heads_local, count_mid, span, -1)
    value_sel = jax.vmap(take_blocks)(value_blk, slot_idx).reshape(heads_local, count_mid, span, -1)
    query_mid = query_blk[:, 1:-1]
    query_glob = jnp.concatenate([query_blk[:, 0], query_blk[:, -1]], 1)
    key_all = key_blk.reshape(heads_local, seq_len, -1)
    value_all = value_blk.reshape(heads_local, seq_len, -1)
    score_mid = jnp.einsum(
        "hnqd,hnkd->hnqk", query_mid, key_sel, preferred_element_type=jnp.float32
    )
    score_mid = jnp.where(mid_mask, score_mid, neg_large)
    score_glob = jnp.einsum("hqd,hkd->hqk", query_glob, key_all, preferred_element_type=jnp.float32)
    score_glob = jnp.where(glob_mask[None], score_glob, neg_large)
    return (
        query_mid,
        key_sel,
        value_sel,
        query_glob,
        key_all,
        value_all,
        score_mid,
        score_glob,
        slot_idx,
    )


def assemble(mid_blocks, glob_rows):
    first_rows = glob_rows[:, None, :BLOCK]
    last_rows = glob_rows[:, None, BLOCK:]
    return head_flat(jnp.concatenate([first_rows, mid_blocks, last_rows], 1))


def attend(queries, key_rows, value_rows, seq_segs, random_local):
    (
        query_mid,
        key_sel,
        value_sel,
        query_glob,
        key_all,
        value_all,
        score_mid,
        score_glob,
        slot_idx,
    ) = prepare(queries, key_rows, value_rows, seq_segs, random_local)
    max_mid = jnp.max(score_mid, axis=-1, keepdims=True)
    exp_mid = jnp.exp(score_mid - max_mid)
    sum_mid = jnp.sum(exp_mid, axis=-1, keepdims=True)
    prob_mid = (exp_mid / sum_mid).astype(jnp.bfloat16)
    out_mid = jnp.einsum("hnqk,hnkd->hnqd", prob_mid, value_sel, preferred_element_type=jnp.float32)
    max_glob = jnp.max(score_glob, axis=-1, keepdims=True)
    exp_glob = jnp.exp(score_glob - max_glob)
    sum_glob = jnp.sum(exp_glob, axis=-1, keepdims=True)
    prob_glob = (exp_glob / sum_glob).astype(jnp.bfloat16)
    out_glob = jnp.einsum("hqk,hkd->hqd", prob_glob, value_all, preferred_element_type=jnp.float32)
    return (
        assemble(out_mid, out_glob).astype(jnp.bfloat16),
        (max_mid, sum_mid, max_glob, sum_glob),
    )


def attend_back(queries, key_rows, value_rows, grad_context, softmax_kept, seq_segs, random_local):
    (
        query_mid,
        key_sel,
        value_sel,
        query_glob,
        key_all,
        value_all,
        score_mid,
        score_glob,
        slot_idx,
    ) = prepare(queries, key_rows, value_rows, seq_segs, random_local)
    max_mid, sum_mid, max_glob, sum_glob = softmax_kept
    heads_local = random_local.shape[0]
    seq_len = seq_segs.shape[0]
    nblocks = seq_len // BLOCK
    head_width = key_sel.shape[-1]
    grad_blk = head_blocks(grad_context, heads_local)
    grad_mid = grad_blk[:, 1:-1]
    grad_glob = jnp.concatenate([grad_blk[:, 0], grad_blk[:, -1]], 1)
    prob_mid = jnp.exp(score_mid - max_mid) / sum_mid
    dv_sel = jnp.einsum(
        "hnqk,hnqd->hnkd",
        prob_mid.astype(jnp.bfloat16),
        grad_mid,
        preferred_element_type=jnp.float32,
    )
    dprob_mid = jnp.einsum(
        "hnqd,hnkd->hnqk", grad_mid, value_sel, preferred_element_type=jnp.float32
    )
    dscore_mid = (
        prob_mid * (dprob_mid - jnp.sum(prob_mid * dprob_mid, axis=-1, keepdims=True))
    ).astype(jnp.bfloat16)
    dq_mid = jnp.einsum("hnqk,hnkd->hnqd", dscore_mid, key_sel, preferred_element_type=jnp.float32)
    dk_sel = jnp.einsum(
        "hnqk,hnqd->hnkd", dscore_mid, query_mid, preferred_element_type=jnp.float32
    )
    prob_glob = jnp.exp(score_glob - max_glob) / sum_glob
    dv_glob = jnp.einsum(
        "hqk,hqd->hkd",
        prob_glob.astype(jnp.bfloat16),
        grad_glob,
        preferred_element_type=jnp.float32,
    )
    dprob_glob = jnp.einsum(
        "hqd,hkd->hqk", grad_glob, value_all, preferred_element_type=jnp.float32
    )
    dscore_glob = (
        prob_glob * (dprob_glob - jnp.sum(prob_glob * dprob_glob, axis=-1, keepdims=True))
    ).astype(jnp.bfloat16)
    dq_glob = jnp.einsum("hqk,hkd->hqd", dscore_glob, key_all, preferred_element_type=jnp.float32)
    dk_glob = jnp.einsum(
        "hqk,hqd->hkd", dscore_glob, query_glob, preferred_element_type=jnp.float32
    )
    spread_back = partial(add_blocks, nblocks=nblocks)
    flat_idx = slot_idx.reshape(heads_local, -1)
    dk_blocks = jax.vmap(spread_back)(dk_sel.reshape(heads_local, -1, BLOCK, head_width), flat_idx)
    dv_blocks = jax.vmap(spread_back)(dv_sel.reshape(heads_local, -1, BLOCK, head_width), flat_idx)
    grad_keys = head_flat(dk_blocks + dk_glob.reshape(heads_local, nblocks, BLOCK, head_width))
    grad_values = head_flat(dv_blocks + dv_glob.reshape(heads_local, nblocks, BLOCK, head_width))
    grad_queries = assemble(dq_mid, dq_glob)
    return (
        grad_queries.astype(jnp.bfloat16),
        grad_keys.astype(jnp.bfloat16),
        grad_values.astype(jnp.bfloat16),
    )


def on_device(
    hidden_in,
    cotangent,
    norm1_gain,
    norm1_bias,
    w_query,
    w_key,
    w_value,
    w_out,
    norm2_gain,
    norm2_bias,
    w_fc1,
    bias_fc1,
    w_fc2,
    bias_fc2,
    segments,
    random_blocks,
):
    rows_dev = hidden_in.shape[0]
    width_model = hidden_in.shape[1]
    tp_rank = lax.axis_index("tp")
    seq_segs = segments[0]
    random_local = random_blocks[0]
    own_segs = lax.dynamic_slice_in_dim(seq_segs, tp_rank * rows_dev, rows_dev)
    valid_rows = (own_segs != 0).astype(jnp.float32)[:, None]
    gain_first = norm1_gain.astype(jnp.float32)
    shift_first = norm1_bias.astype(jnp.float32)
    gain_second = norm2_gain.astype(jnp.float32)
    shift_second = norm2_bias.astype(jnp.float32)
    bias_down = bias_fc2.astype(jnp.float32)
    residual_in = hidden_in.astype(jnp.float32)
    scale_query = HEAD_DIM ** (-0.5)
    w_q, w_k, w_v, w_o = (
        lax.all_gather(w_query, "fsdp", axis=0, tiled=True),
        lax.all_gather(w_key, "fsdp", axis=0, tiled=True),
        lax.all_gather(w_value, "fsdp", axis=0, tiled=True),
        lax.all_gather(w_out, "fsdp", axis=1, tiled=True),
    )
    normed_first, norm_first_back = jax.vjp(norm_rows, residual_in, gain_first, shift_first)
    full_first = attn_spread(normed_first.astype(jnp.bfloat16))
    queries = (product(full_first, w_q) * scale_query).astype(jnp.bfloat16)
    key_rows = product(full_first, w_k).astype(jnp.bfloat16)
    value_rows = product(full_first, w_v).astype(jnp.bfloat16)
    context, softmax_kept = attend(queries, key_rows, value_rows, seq_segs, random_local)
    attn_branch = attn_collect(product(context, w_o))
    middle = residual_in + attn_branch
    normed_second, norm_second_back = jax.vjp(norm_rows, middle, gain_second, shift_second)
    normed_low = normed_second.astype(jnp.bfloat16)
    w_up, w_down = (
        lax.all_gather(w_fc1, "fsdp", axis=0, tiled=True),
        lax.all_gather(w_fc2, "fsdp", axis=1, tiled=True),
    )
    ffn_input = ffn_spread(normed_low)
    pre_act = product(ffn_input, w_up) + bias_fc1.astype(jnp.float32)
    hidden_act, gelu_back = jax.vjp(gelu_tanh, pre_act)
    hidden_low = hidden_act.astype(jnp.bfloat16)
    down_terms = product(hidden_low, w_down)
    ffn_branch = ffn_collect(down_terms) + bias_down
    output_rows = middle + ffn_branch
    square_sums = jnp.stack(
        [
            jnp.sum(valid_rows * branch * branch)
            for branch in (residual_in, attn_branch, middle, ffn_branch)
        ]
    )
    valid_count = jnp.sum(valid_rows)
    square_sums, valid_count = lax.psum((square_sums, valid_count), ("fsdp", "tp"))
    grad_branch = cotangent.astype(jnp.float32)
    grad_bias_down = jnp.sum(grad_branch, axis=0)
    grad_ffn_rows = ffn_spread(cotangent)
    grad_hidden = inner_cols(grad_ffn_rows, w_down)
    grad_pre = gelu_back(grad_hidden)[0].astype(jnp.bfloat16)
    grad_w_down = inner_rows(hidden_low, grad_ffn_rows)
    grad_w_up = inner_rows(ffn_input, grad_pre)
    grad_bias_up = jnp.sum(grad_pre, axis=0, dtype=jnp.float32)
    normed_terms = inner_cols(grad_pre, w_up)
    width_local = bias_fc1.shape[0]
    grad_normed_second = ffn_collect(normed_terms)
    grad_bias_up = lax.dynamic_update_slice_in_dim(
        jnp.zeros((width_local * lax.axis_size("tp"),), jnp.float32),
        grad_bias_up,
        tp_rank * width_local,
        0,
    )
    grad_w_up, grad_w_down = (
        lax.psum_scatter(grad_w_up, "fsdp", scatter_dimension=0, tiled=True),
        lax.psum_scatter(grad_w_down, "fsdp", scatter_dimension=1, tiled=True),
    )
    grad_mid_norm, grad_gain_second, grad_shift_second = norm_second_back(grad_normed_second)
    grad_middle = grad_branch + grad_mid_norm
    grad_attn_rows = attn_spread(grad_middle.astype(jnp.bfloat16))
    grad_context = inner_cols(grad_attn_rows, w_o).astype(jnp.bfloat16)
    grad_w_o = inner_rows(context, grad_attn_rows)
    grad_queries, grad_keys, grad_values = attend_back(
        queries, key_rows, value_rows, grad_context, softmax_kept, seq_segs, random_local
    )
    grad_queries = grad_queries * scale_query
    input_terms = (
        inner_cols(grad_queries, w_q) + inner_cols(grad_keys, w_k) + inner_cols(grad_values, w_v)
    )
    grad_normed_first = attn_collect(input_terms)
    grad_w_q = inner_rows(full_first, grad_queries)
    grad_w_k = inner_rows(full_first, grad_keys)
    grad_w_v = inner_rows(full_first, grad_values)
    grad_w_q, grad_w_k, grad_w_v, grad_w_o = (
        lax.psum_scatter(grad_w_q, "fsdp", scatter_dimension=0, tiled=True),
        lax.psum_scatter(grad_w_k, "fsdp", scatter_dimension=0, tiled=True),
        lax.psum_scatter(grad_w_v, "fsdp", scatter_dimension=0, tiled=True),
        lax.psum_scatter(grad_w_o, "fsdp", scatter_dimension=1, tiled=True),
    )
    grad_in_norm, grad_gain_first, grad_shift_first = norm_first_back(grad_normed_first)
    grad_input = grad_middle + grad_in_norm
    (
        grad_gain_first,
        grad_shift_first,
        grad_gain_second,
        grad_shift_second,
        grad_bias_up,
        grad_bias_down,
    ) = lax.psum(
        (
            grad_gain_first,
            grad_shift_first,
            grad_gain_second,
            grad_shift_second,
            grad_bias_up,
            grad_bias_down,
        ),
        ("fsdp", "tp"),
    )
    grad_bias_local = lax.dynamic_slice_in_dim(grad_bias_up, tp_rank * width_local, width_local)
    residual_rms = jnp.sqrt(square_sums / (valid_count * width_model))
    return (
        output_rows.astype(jnp.bfloat16),
        grad_input,
        grad_gain_first,
        grad_shift_first,
        grad_w_q,
        grad_w_k,
        grad_w_v,
        grad_w_o,
        grad_gain_second,
        grad_shift_second,
        grad_w_up,
        grad_bias_local,
        grad_w_down,
        grad_bias_down,
        residual_rms,
    )


def solution(mesh):
    in_specs = (
        P(("fsdp", "tp"), None),
        P(("fsdp", "tp"), None),
        P(),
        P(),
        P("fsdp", "tp"),
        P("fsdp", "tp"),
        P("fsdp", "tp"),
        P("tp", "fsdp"),
        P(),
        P(),
        P("fsdp", "tp"),
        P("tp"),
        P("tp", "fsdp"),
        P(),
        P("fsdp", None),
        P("fsdp", "tp", None, None),
    )
    out_specs = (
        P(("fsdp", "tp"), None),
        P(("fsdp", "tp"), None),
        P(),
        P(),
        P("fsdp", "tp"),
        P("fsdp", "tp"),
        P("fsdp", "tp"),
        P("tp", "fsdp"),
        P(),
        P(),
        P("fsdp", "tp"),
        P("tp"),
        P("tp", "fsdp"),
        P(),
        P(),
    )
    return jax.shard_map(
        on_device, mesh=mesh, in_specs=in_specs, out_specs=out_specs, check_vma=False
    )
```

profile of v0, /device:TPU:0, one launch (start us, length us, event | category | flops | bytes accessed | tf_op | source)
XLA Modules:
  0.0 2378.1 jit_solution(15552342759166836100)
XLA Ops:
  26.9 35.5 %all_gather.31 = bf16[1024,256]{1,0:T(8,128)(2,1)} all-gather(bf16[128,256]{1,0:T(8,128)(2,1)S(1)} %copy-done.39), channel_id=1, replica_groups=mesh['fsdp'=8,'tp'=4] {'fsdp'}, dimensions={0}, use_global_device_ids=true | all-gather | bytes 589824 | tf_op jit(solution)/shard_map/all_gather | solution.py:279
  62.4 33.5 %all_gather.32 = bf16[1024,256]{1,0:T(8,128)(2,1)} all-gather(bf16[128,256]{1,0:T(8,128)(2,1)S(1)} %copy-done.40), channel_id=1, replica_groups=mesh['fsdp'=8,'tp'=4] {'fsdp'}, dimensions={0}, use_global_device_ids=true | all-gather | bytes 589824 | tf_op jit(solution)/shard_map/all_gather | solution.py:280
  95.9 31.7 %all_gather.33 = bf16[1024,256]{1,0:T(8,128)(2,1)S(1)} all-gather(bf16[128,256]{1,0:T(8,128)(2,1)S(1)} %copy-done.41), channel_id=1, replica_groups=mesh['fsdp'=8,'tp'=4] {'fsdp'}, dimensions={0}, use_global_device_ids=true | all-gather | bytes 589824 | tf_op jit(solution)/shard_map/all_gather | solution.py:281
  127.5 28.1 %all_gather.34 = bf16[256,1024]{1,0:T(8,128)(2,1)} all-gather(bf16[256,128]{1,0:T(8,128)(2,1)S(1)} %copy-done.42), channel_id=1, replica_groups=mesh['fsdp'=8,'tp'=4] {'fsdp'}, dimensions={1}, use_global_device_ids=true | all-gather | bytes 589824 | tf_op jit(solution)/shard_map/all_gather | solution.py:282
  195.0 7.4 copy.115
  203.3 8.4 fusion.75
  218.4 30.9 %gather_fusion.1 = bf16[1984,64,64]{2,1,0:T(8,128)(2,1)} fusion(bf16[4,64,64,64]{3,2,1,0:T(8,128)(2,1)} %bitcast.129, s32[1984]{0:T(1024)S(1)} %reshape.502), kind=kCustom, calls=%fused_computation.1 | custom fusion | bytes 32521728 | tf_op jit(solution)/shard_map/vmap()/gather | solution.py:69
  249.3 30.6 %gather_fusion.2 = bf16[1984,64,64]{2,1,0:T(8,128)(2,1)} fusion(bf16[4,64,64,64]{3,2,1,0:T(8,128)(2,1)} %bitcast.132, s32[1984]{0:T(1024)S(1)} %reshape.502), kind=kCustom, calls=%fused_computation.2 | custom fusion | bytes 32521728 | tf_op jit(solution)/shard_map/vmap()/gather | solution.py:69
  279.9 30.4 %fusion.76 = (f32[4,62,64]{2,1,0:T(8,128)S(1)}, f32[4,62,64,512]{3,2,1,0:T(8,128)}) fusion(s32[4,62,512]{2,1,0:T(8,128)S(1)} %eq.116, s32[62,64]{1,0:T(8,128)S(1)} %eq.114, pred[64,512]{1,0:T(8,128)(4,1)S(1)} %iota_compare_fusion.1, pred[62,512]{1,0:T(8,128)(4,1)S(1)} %and.58, pred[4,62,512]{2,1,0:T(8,128)(4,1)S(1)} %broadcast_compare_fusion, ...), kind=kOutput, calls=%fused_computation.168 | convolution fusion | flops 1097073152 | bytes 69853696 | tf_op jit(solution)/shard_map/sub | solution.py:163
  310.3 23.9 %fusion.48 = bf16[4,62,64,64]{3,2,1,0:T(8,128)(2,1)} fusion(bf16[4,62,512,64]{3,2,1,0:T(8,128)(2,1)} %bitcast.140, f32[4,62,64,512]{3,2,1,0:T(8,128)} %get-tuple-element.67, f32[4,62,64]{2,1,0:T(8,128)S(1)} %get-tuple-element.66), kind=kOutput, calls=%fused_computation.92 | convolution fusion | flops 1057456128 | bytes 50853888 | tf_op jit(solution)/shard_map/hnqk,hnkd->hnqd/dot_general | solution.py:166
  350.7 8.2 fusion.81
  359.6 123.5 %reduce-scatter.11.cloned.1.call-done = f32[1024,1024]{1,0:T(8,128)} async-done(((f32[4096,1024]{1,0:T(8,128)}), f32[1024,1024]{1,0:T(8,128)}) %reduce-scatter.11.cloned.1.call-update) | async-done | bytes 4194320 | tf_op jit(solution)/shard_map/reduce_scatter | solution.py:48
  491.3 56.8 %all-gather.9.cloned.1.call-done = bf16[4096,1024]{1,0:T(8,128)(2,1)} async-done(((bf16[1024,1024]{1,0:T(8,128)(2,1)}), bf16[4096,1024]{1,0:T(8,128)(2,1)}) %all-gather.9.cloned.1.call-update) | async-done | bytes 8388624 | tf_op jit(solution)/shard_map/all_gather | solution.py:52
  548.1 16.1 fusion.82
  564.2 36.3 %all-gather.13.cloned.1.call-done = bf16[1024,1024]{1,0:T(8,128)(2,1)} async-done(((bf16[1024,128]{1,0:T(8,128)(2,1)}), bf16[1024,1024]{1,0:T(8,128)(2,1)}) %all-gather.13.cloned.1.call-update) | async-done | bytes 2097168 | tf_op jit(solution)/shard_map/all_gather | solution.py:296
  600.5 57.9 %all-gather.15.cloned.1.call-done = bf16[4096,1024]{1,0:T(8,128)(2,1)} async-done(((bf16[1024,1024]{1,0:T(8,128)(2,1)}), bf16[4096,1024]{1,0:T(8,128)(2,1)}) %all-gather.15.cloned.1.call-update) | async-done | bytes 8388624 | tf_op jit(solution)/shard_map/all_gather | solution.py:52
  658.4 26.5 %convert_reduce_fusion = (f32[1024]{0:T(1024)}, bf16[4096,1024]{1,0:T(8,128)(2,1)S(1)}, bf16[4096,1024]{1,0:T(8,128)(2,1)}) fusion(f32[4096,1024]{1,0:T(8,128)} %fusion.82, f32[1024]{0:T(1024)S(1)} %convert_element_type.132, bf16[4096,1024]{1,0:T(8,128)(2,1)} %all-gather.15.cloned.1.call-done, bf16[1024,1024]{1,0:T(8,128)(2,1)} %all-gather.13.cloned.1.call-done), kind=kOutput, calls=%fused_computation.20 | convolution fusion | flops 8694791168 | bytes 44048384 | tf_op jit(solution)/shard_map/dot_general | solution.py:38
  688.1 13.9 fusion.84
  703.5 123.7 %reduce-scatter.15.cloned.1.call-done = f32[1024,1024]{1,0:T(8,128)} async-done(((f32[4096,1024]{1,0:T(8,128)}), f32[1024,1024]{1,0:T(8,128)}) %reduce-scatter.15.cloned.1.call-update) | async-done | bytes 4194320 | tf_op jit(solution)/shard_map/reduce_scatter | solution.py:56
  840.8 16.1 fusion.83
  857.0 41.0 %all-gather.17.cloned.1.call-done = bf16[4096,1024]{1,0:T(8,128)(2,1)} async-done(((bf16[1024,1024]{1,0:T(8,128)(2,1)}), bf16[4096,1024]{1,0:T(8,128)(2,1)}) %all-gather.17.cloned.1.call-update) | async-done | bytes 8388624 | tf_op jit(solution)/shard_map/all_gather | solution.py:44
  907.1 7.8 copy.132
  915.8 10.0 multiply_reduce_fusion.1
  931.1 35.7 %multiply_reduce_fusion = (f32[4,62,64]{2,1,0:T(8,128)S(1)}, f32[4,62,64,512]{3,2,1,0:T(8,128)}) fusion(f32[4,62,64,512]{3,2,1,0:T(8,128)} %get-tuple-element.67, f32[4,62,64]{2,1,0:T(8,128)S(1)} %copy-done.33, bf16[4,62,512,64]{3,2,1,0:T(8,128)(2,1)} %bitcast.141, bf16[4,64,64,64]{2,3,0,1:T(8,128)(2,1)} %bitcast.149), kind=kOutput, calls=%fused_computation.8 | convolution fusion | flops 1064550912 | bytes 101707776 | tf_op jit(solution)/shard_map/hnqd,hnkd->hnqk/dot_general | solution.py:205
  966.7 27.7 %multiply_convert_fusion = bf16[4,62,64,512]{3,2,1,0:T(8,128)(2,1)} fusion(f32[4,62,64,512]{3,2,1,0:T(8,128)} %get-tuple-element.71, f32[4,62,64]{2,1,0:T(8,128)S(1)} %get-tuple-element.70, f32[4,62,64,512]{3,2,1,0:T(8,128)} %get-tuple-element.67, f32[4,62,64]{2,1,0:T(8,128)S(1)} %copy-done.33), kind=kLoop, calls=%fused_computation.7 | loop fusion | flops 32505856 | bytes 81391616 | tf_op jit(solution)/shard_map/convert_element_type | solution.py:210
  994.4 17.9 convolution_convert_fusion.3
  1028.2 8.5 fusion.51
  1036.8 33.1 %fusion.16 = f32[4,62,512,64]{3,2,1,0:T(8,128)} fusion(f32[4,62,64,512]{3,2,1,0:T(8,128)} %get-tuple-element.67, f32[4,62,64]{2,1,0:T(8,128)S(1)} %copy-done.33, bf16[4,64,64,64]{2,3,0,1:T(8,128)(2,1)S(1)} %bitcast.150), kind=kOutput, calls=%fused_computation.39 | convolution fusion | flops 1056440320 | bytes 69206016 | tf_op jit(solution)/shard_map/reshape | solution.py:235
  1069.9 303.6 %scatter_fusion.1 = f32[256,64,64]{2,1,0:T(8,128)} fusion(f32[256,64,64]{2,1,0:T(8,128)} %bitcast.126, s32[1984]{0:T(1024)S(1)} %copy-done.36, f32[1984,64,64]{2,1,0:T(8,128)} %bitcast.136), kind=kCustom, calls=%fused_computation.4 | custom fusion | flops 8126464 | bytes 97525504
  1400.4 29.3 %fusion.43 = f32[4,62,512,64]{3,2,1,0:T(8,128)} fusion(bf16[4,62,64,512]{3,2,1,0:T(8,128)(2,1)} %multiply_convert_fusion, bf16[4,64,64,64]{2,3,0,1:T(8,128)(2,1)} %bitcast.139), kind=kOutput, calls=%fused_computation.87 | convolution fusion | flops 1040187392 | bytes 52822016 | tf_op jit(solution)/shard_map/reshape | solution.py:234
  1429.7 304.1 %scatter_fusion = f32[256,64,64]{2,1,0:T(8,128)} fusion(f32[256,64,64]{2,1,0:T(8,128)} %bitcast.125, s32[1984]{0:T(1024)S(1)} %copy-done.36, f32[1984,64,64]{2,1,0:T(8,128)} %bitcast.127), kind=kCustom, calls=%fused_computation.3 | custom fusion | flops 8126464 | bytes 97525504
  1753.7 8.1 fusion.85
  1761.8 8.1 fusion.86
  1770.0 18.8 add_add_fusion
  1788.8 15.3 fusion.91
  1804.2 18.5 fusion.92
  1822.7 7.3 fusion.90
  1837.4 7.4 fusion.89
  1845.3 7.7 fusion.88
  1853.1 61.8 %reduce-scatter.17.cloned.1.call-done = f32[1024,1024]{1,0:T(8,128)} async-done(((f32[4096,1024]{1,0:T(8,128)}), f32[1024,1024]{1,0:T(8,128)}) %reduce-scatter.17.cloned.1.call-update) | async-done | bytes 4194320 | tf_op jit(solution)/shard_map/reduce_scatter | solution.py:48
  1914.9 9.7 fusion.70
  1934.2 42.1 %all-reduce.1 = (f32[1024]{0:T(1024)}, f32[1024]{0:T(1024)}, f32[1024]{0:T(1024)}, f32[1024]{0:T(1024)}, f32[4096]{0:T(1024)S(1)}, /*index=5*/f32[1024]{0:T(1024)}, f32[4]{0:T(128)S(1)}, f32[]{:T(128)}) all-reduce(f32[1024]{0:T(1024)S(1)} %get-tuple-element.17, ...), channel_id=1, replica_groups=mesh['fsdp'=8,'tp'=4] {'fsdp','tp'}, use_global_device_ids=true, to_apply=%region_21.22 | all-reduce | flops 9221 | bytes 73768 | tf_op jit(solution)/shard_map/psum | solution.py:365
  1978.0 30.4 %reduce-scatter.27.cloned.1.call-done = f32[128,1024]{1,0:T(8,128)} async-done(((f32[1024,1024]{1,0:T(8,128)}), f32[128,1024]{1,0:T(8,128)}) %reduce-scatter.27.cloned.1.call-update) | async-done | bytes 524304 | tf_op jit(solution)/shard_map/reduce_scatter | solution.py:331
  2008.4 92.5 %reduce-scatter.29.cloned.1.call-done = f32[1024,128]{1,0:T(8,128)} async-done(((f32[1024,1024]{1,0:T(8,128)}), f32[1024,128]{1,0:T(8,128)}) %reduce-scatter.29.cloned.1.call-update) | async-done | bytes 524304 | tf_op jit(solution)/shard_map/reduce_scatter | solution.py:332
  2101.0 68.4 %reduce-scatter.25.cloned.1.call-done = f32[256,128]{1,0:T(8,128)} async-done(((f32[256,1024]{1,0:T(8,128)}), f32[256,128]{1,0:T(8,128)}) %reduce-scatter.25.cloned.1.call-update) | async-done | bytes 131088 | tf_op jit(solution)/shard_map/reduce_scatter | solution.py:354
  2169.4 67.1 %reduce-scatter.19.cloned.1.call-done = f32[128,256]{1,0:T(8,128)} async-done(((f32[1024,256]{1,0:T(8,128)}), f32[128,256]{1,0:T(8,128)}) %reduce-scatter.19.cloned.1.call-update) | async-done | bytes 131088 | tf_op jit(solution)/shard_map/reduce_scatter | solution.py:351
  2236.5 66.9 %reduce-scatter.23.cloned.1.call-done = f32[128,256]{1,0:T(8,128)} async-done(((f32[1024,256]{1,0:T(8,128)}), f32[128,256]{1,0:T(8,128)}) %reduce-scatter.23.cloned.1.call-update) | async-done | bytes 131088 | tf_op jit(solution)/shard_map/reduce_scatter | solution.py:353
  2303.4 67.1 %reduce-scatter.21.cloned.1.call-done = f32[128,256]{1,0:T(8,128)} async-done(((f32[1024,256]{1,0:T(8,128)}), f32[128,256]{1,0:T(8,128)}) %reduce-scatter.21.cloned.1.call-update) | async-done | bytes 131088 | tf_op jit(solution)/shard_map/reduce_scatter | solution.py:352
  (283 shorter events, 205.5 us)
Async XLA Ops:
  8.0 7.0 copy-start.3
  8.0 149.1 %all-gather.7.cloned.1.call-start = ((), (), s32[]{:S(2)}) async-start(), calls=%async_computation.10 | async-start | bytes 10485760 | tf_op jit(solution)/shard_map/all_gather | solution.py:44
  17.2 465.9 %reduce-scatter.11.cloned.1.call-start = ((), (), s32[]{:S(2)}) async-start(), calls=%async_computation.11 | async-start | bytes 20971520 | tf_op jit(solution)/shard_map/reduce_scatter | solution.py:48
  20.6 41.8 %copy-start.40 = (bf16[128,256]{1,0:T(8,128)(2,1)S(1)}, bf16[128,256]{1,0:T(8,128)(2,1)}, u32[]{:S(2)}) copy-start(bf16[128,256]{1,0:T(8,128)(2,1)} %param.23) | copy-start | bytes 196612
  20.6 75.3 %copy-start.41 = (bf16[128,256]{1,0:T(8,128)(2,1)S(1)}, bf16[128,256]{1,0:T(8,128)(2,1)}, u32[]{:S(2)}) copy-start(bf16[128,256]{1,0:T(8,128)(2,1)} %param.24) | copy-start | bytes 196612
  20.6 106.9 %copy-start.42 = (bf16[256,128]{1,0:T(8,128)(2,1)S(1)}, bf16[256,128]{1,0:T(8,128)(2,1)}, u32[]{:S(2)}) copy-start(bf16[256,128]{1,0:T(8,128)(2,1)} %param.25) | copy-start | bytes 196612
  127.5 35.3 %copy-start.17 = (bf16[1024,256]{1,0:T(8,128)(2,1)}, bf16[1024,256]{1,0:T(8,128)(2,1)S(1)}, u32[]{:S(2)}) copy-start(bf16[1024,256]{1,0:T(8,128)(2,1)S(1)} %all_gather.33) | copy-start | bytes 1572868
  195.0 8.3 copy-start.24
  203.3 8.5 copy-start.26
  203.3 8.5 copy-start.28
  310.3 23.9 %copy-start.32 = (f32[4,62,64]{2,1,0:T(8,128)}, f32[4,62,64]{2,1,0:T(8,128)S(1)}, u32[]{:S(2)}) copy-start(f32[4,62,64]{2,1,0:T(8,128)S(1)} %get-tuple-element.66) | copy-start | bytes 190468
  350.7 8.2 copy-start.15
  358.9 124.2 %copy-start.4 = (bf16[1024,1024]{1,0:T(8,128)(2,1)S(1)}, bf16[1024,1024]{1,0:T(8,128)(2,1)}, u32[]{:S(2)}) copy-start(bf16[1024,1024]{1,0:T(8,128)(2,1)} %param.18) | copy-start | bytes 6291460
  358.9 132.3 %all-gather.11.cloned.1.call-start = ((), (), s32[]{:S(2)}) async-start(), calls=%async_computation.13 | async-start | bytes 2359296 | tf_op jit(solution)/shard_map/all_gather | solution.py:295
  359.5 188.6 %all-gather.9.cloned.1.call-start = ((), (), s32[]{:S(2)}) async-start(), calls=%async_computation.12 | async-start | bytes 10485760 | tf_op jit(solution)/shard_map/all_gather | solution.py:52
  489.9 110.6 %all-gather.13.cloned.1.call-start = ((), (), s32[]{:S(2)}) async-start(), calls=%async_computation.14 | async-start | bytes 2359296 | tf_op jit(solution)/shard_map/all_gather | solution.py:296
  490.4 168.0 %all-gather.15.cloned.1.call-start = ((), (), s32[]{:S(2)}) async-start(), calls=%async_computation.16 | async-start | bytes 10485760 | tf_op jit(solution)/shard_map/all_gather | solution.py:52
  491.2 336.0 %reduce-scatter.15.cloned.1.call-start = ((), (), s32[]{:S(2)}) async-start(), calls=%async_computation.17 | async-start | bytes 20971520 | tf_op jit(solution)/shard_map/reduce_scatter | solution.py:56
  702.1 195.9 %all-gather.17.cloned.1.call-start = ((), (), s32[]{:S(2)}) async-start(), calls=%async_computation.18 | async-start | bytes 10485760 | tf_op jit(solution)/shard_map/all_gather | solution.py:44
  703.5 130.4 %copy-start.45 = (f32[1,1024]{1,0:T(1,128)}, f32[1,1024]{1,0:T(1,128)S(1)}, u32[]{:S(2)}) copy-start(f32[1,1024]{1,0:T(1,128)S(1)} %get-tuple-element.35) | copy-start | bytes 12292
  827.2 6.7 copy-start.12
  839.6 1013.5 %reduce-scatter.13.cloned.1.call-start = ((), (), s32[]{:S(2)}) async-start(), calls=%async_computation.15 | async-start | bytes 20971520 | tf_op jit(solution)/shard_map/reduce_scatter | solution.py:56
  856.9 1058.0 %reduce-scatter.17.cloned.1.call-start = ((), (), s32[]{:S(2)}) async-start(), calls=%async_computation.19 | async-start | bytes 20971520 | tf_op jit(solution)/shard_map/reduce_scatter | solution.py:48
  907.1 8.7 copy-start.58
  915.8 10.0 slice-start
  915.8 10.7 slice-start.1
  1028.2 8.5 copy-start.16
  1036.8 33.1 %copy-start.36 = (s32[1984]{0:T(1024)S(1)}, s32[1984]{0:T(1024)}, u32[]{:S(2)}) copy-start(s32[1984]{0:T(1024)} %reshape.514) | copy-start | bytes 23812
  1746.9 6.8 copy-start.13
  1746.9 6.8 copy-start.22
  1753.7 8.2 copy-start.14
  1753.7 8.2 copy-start.20
  1761.8 8.1 copy-start.18
  1788.8 219.7 %reduce-scatter.27.cloned.1.call-start = ((), (), s32[]{:S(2)}) async-start(), calls=%async_computation.24 | async-start | bytes 4718592 | tf_op jit(solution)/shard_map/reduce_scatter | solution.py:331
  1804.1 296.9 %reduce-scatter.29.cloned.1.call-start = ((), (), s32[]{:S(2)}) async-start(), calls=%async_computation.25 | async-start | bytes 4718592 | tf_op jit(solution)/shard_map/reduce_scatter | solution.py:332
  1822.7 346.7 %reduce-scatter.25.cloned.1.call-start = ((), (), s32[]{:S(2)}) async-start(), calls=%async_computation.23 | async-start | bytes 1179648 | tf_op jit(solution)/shard_map/reduce_scatter | solution.py:354
  1830.1 406.4 %reduce-scatter.19.cloned.1.call-start = ((), (), s32[]{:S(2)}) async-start(), calls=%async_computation.20 | async-start | bytes 1179648 | tf_op jit(solution)/shard_map/reduce_scatter | solution.py:351
  1837.1 7.8 copy-start.62
  1837.1 7.8 copy-start.56
  1837.2 466.2 %reduce-scatter.23.cloned.1.call-start = ((), (), s32[]{:S(2)}) async-start(), calls=%async_computation.22 | async-start | bytes 1179648 | tf_op jit(solution)/shard_map/reduce_scatter | solution.py:353
  1844.9 525.6 %reduce-scatter.21.cloned.1.call-start = ((), (), s32[]{:S(2)}) async-start(), calls=%async_computation.21 | async-start | bytes 1179648 | tf_op jit(solution)/shard_map/reduce_scatter | solution.py:352
  1845.3 69.6 %copy-start.5 = (bf16[1024,1024]{1,0:T(8,128)(2,1)S(1)}, bf16[1024,1024]{1,0:T(8,128)(2,1)}, u32[]{:S(2)}) copy-start(bf16[1024,1024]{1,0:T(8,128)(2,1)} %param.18) | copy-start | bytes 6291460
  1845.3 69.6 %copy-start.31 = (f32[1024]{0:T(1024)S(1)}, f32[1024]{0:T(1024)}, u32[]{:S(2)}) copy-start(f32[1024]{0:T(1024)} %copy-done.30) | copy-start | bytes 12292
  1845.3 69.6 %copy-start.35 = (f32[1024]{0:T(1024)S(1)}, f32[1024]{0:T(1024)}, u32[]{:S(2)}) copy-start(f32[1024]{0:T(1024)} %copy-done.34) | copy-start | bytes 12292
  1845.3 69.6 %copy-start.46 = (f32[1,1024]{1,0:T(1,128)S(1)}, f32[1,1024]{1,0:T(1,128)}, u32[]{:S(2)}) copy-start(f32[1,1024]{1,0:T(1,128)} %copy-done.45) | copy-start | bytes 12292
  1853.0 75.2 %copy-start.50 = (f32[1024]{0:T(1024)S(1)}, f32[1024]{0:T(1024)}, u32[]{:S(2)}) copy-start(f32[1024]{0:T(1024)} %copy-done.49) | copy-start | bytes 12292
  1853.1 75.2 %copy-start.44 = (f32[1024]{0:T(1024)S(1)}, f32[1024]{0:T(1024)}, u32[]{:S(2)}) copy-start(f32[1024]{0:T(1024)} %copy-done.43) | copy-start | bytes 12292
  1914.9 13.4 copy-start.7
  (36 other events, 134.7 us)
Sparse Core Ops, SparseCore 0:
  17.3 60.9 all-gather.6
  359.0 123.9 reduce-scatter.10
  839.7 58.2 all-gather.16
  900.4 125.0 reduce-scatter.12
  1788.9 125.9 reduce-scatter.16
  1918.9 89.4 reduce-scatter.26
  2012.6 88.3 reduce-scatter.28
  2105.0 64.3 reduce-scatter.24
  2173.4 63.0 reduce-scatter.18
  2240.3 63.0 reduce-scatter.22
  2307.4 63.0 reduce-scatter.20
Sparse Core Ops, SparseCore 1:
  361.5 47.9 all-gather.10
  489.9 58.1 all-gather.8
  550.0 50.4 all-gather.12
  602.1 56.3 all-gather.14
  702.2 124.9 reduce-scatter.14
where the time goes:
time: 2390 us; the launch traced here: 2380 us
  waiting for transfers between devices  896 us (37%)
  other arithmetic  705 us (29%)
  matrix products  414 us (17%)
  local copies, waits for them, and re-layouts  175 us (7%)
  blocking collectives  171 us (7%)
    unnamed x7, other arithmetic  609 us
    reduce_scatter x2, waiting for transfers between devices, attn_collect(): return lax.psum_scatter(terms, 'tp', scatter_dimension=0, tiled=True)  185 us
    reduce_scatter x2, waiting for transfers between devices, ffn_collect(): return lax.psum_scatter(terms, 'tp', scatter_dimension=0, tiled=True)  124 us
    all_gather x2, waiting for transfers between devices, ffn_spread(): return lax.all_gather(source, 'tp', axis=0, tiled=True)  115 us
    reduce_scatter x1, waiting for transfers between devices, on_device(): lax.psum_scatter(grad_w_down, 'fsdp', scatter_dimension=1, tiled=True)  92.5 us
    dot_general x6, matrix products, inner_cols(): lax.dot_general(left, right, (((1,), (1,)), ((), ())), preferred_element_...  81.3 us
    reduce_scatter x1, waiting for transfers between devices, on_device(): lax.psum_scatter(grad_w_o, 'fsdp', scatter_dimension=1, tiled=True)  68.4 us
    reduce_scatter x1, waiting for transfers between devices, on_device(): lax.psum_scatter(grad_w_q, 'fsdp', scatter_dimension=0, tiled=True)  67.1 us
  transfers between devices with their start and end apart: 16, of which 13 were waited for; matrix products, arithmetic and copies ran while one was open for 43% of the time, Pallas kernels for 0%

commit v1 on v0

v1 whole, which is shorter than its diff:
```python
from functools import partial
import jax, jax.numpy as jnp
from jax import lax
from jax.experimental import pallas as pl
from jax.experimental.pallas import tpu as pltpu
from jax.sharding import PartitionSpec as P

HEAD_DIM = 64
BLOCK = 64
LANES = 128
F32 = jnp.float32
LOW = jnp.bfloat16
neg_large = -1e30


def dot_nn(a, b):
    return lax.dot_general(a, b, (((1,), (0,)), ((), ())), preferred_element_type=F32)


def dot_nt(a, b):
    return lax.dot_general(a, b, (((1,), (1,)), ((), ())), preferred_element_type=F32)


def dot_tn(a, b):
    return lax.dot_general(a, b, (((0,), (0,)), ((), ())), preferred_element_type=F32)


class Walk:
    def __init__(self, rank_ref, pick_ref, heads, seq, rand):
        self.rank = rank_ref[0]
        self.pick_ref = pick_ref
        self.heads = heads
        self.rand = rand
        self.nblocks = seq // BLOCK

    def place(self, blk):
        per = self.nblocks // 4
        chunk = lax.bitwise_xor(lax.div(blk, per), self.rank)
        return pl.multiple_of((chunk * per + lax.rem(blk, per)) * BLOCK, BLOCK)

    def picked(self, blk, head, slot):
        return self.pick_ref[(head * (self.nblocks - 2) + blk - 1) * self.rand + slot]


def left_lanes(rows):
    return lax.broadcasted_iota(jnp.int32, (rows, LANES), 1) < HEAD_DIM


def spread_heads(rows, heads):
    tall = jnp.concatenate([rows.astype(F32)] * heads, axis=0)
    width = heads * HEAD_DIM
    row_head = lax.broadcasted_iota(jnp.int32, (heads * BLOCK, width), 0) // BLOCK
    col_head = lax.broadcasted_iota(jnp.int32, (heads * BLOCK, width), 1) // HEAD_DIM
    return jnp.where(row_head == col_head, tall, 0.0).astype(LOW)


def own_heads(full, heads):
    left = left_lanes(BLOCK)
    halves = []
    for pair in range(heads // 2):
        cols = slice(pair * LANES, (pair + 1) * LANES)
        first = full[2 * pair * BLOCK : (2 * pair + 1) * BLOCK, cols]
        second = full[(2 * pair + 1) * BLOCK : (2 * pair + 2) * BLOCK, cols]
        halves.append(jnp.where(left, first, second))
    return jnp.concatenate(halves, axis=1)


def gather_rows(ref, base, walk, blk):
    heads = walk.heads
    width = heads * HEAD_DIM
    left = left_lanes(BLOCK)
    parts = [
        ref[pl.ds(walk.place(at), BLOCK), base : base + width]
        for at in (blk - 1, blk, blk + 1, 0, walk.nblocks - 1)
    ]
    for slot in range(walk.rand):
        halves = []
        for pair in range(heads // 2):
            cols = slice(base + pair * LANES, base + (pair + 1) * LANES)
            first = ref[pl.ds(walk.place(walk.picked(blk, 2 * pair, slot)), BLOCK), cols]
            second = ref[pl.ds(walk.place(walk.picked(blk, 2 * pair + 1, slot)), BLOCK), cols]
            halves.append(jnp.where(left, first, second))
        parts.append(jnp.concatenate(halves, axis=1))
    return jnp.concatenate(parts, axis=0)


def key_marks(mark_ref, walk, blk):
    heads = walk.heads
    left = left_lanes(BLOCK)

    def rows_at(at):
        return mark_ref[pl.ds(pl.multiple_of(at * BLOCK, BLOCK), BLOCK), :]

    before = jnp.where(blk == 1, -1, rows_at(blk - 1))
    after = jnp.where(blk == walk.nblocks - 2, -1, rows_at(blk + 1))
    parts = [
        jnp.concatenate([rows] * (heads // 2), axis=1)
        for rows in (before, rows_at(blk), after, rows_at(0), rows_at(walk.nblocks - 1))
    ]
    for slot in range(walk.rand):
        halves = []
        for pair in range(heads // 2):
            first = rows_at(walk.picked(blk, 2 * pair, slot))
            second = rows_at(walk.picked(blk, 2 * pair + 1, slot))
            halves.append(jnp.where(left, first, second))
        parts.append(jnp.concatenate(halves, axis=1))
    return jnp.concatenate(parts, axis=0)


def chunk_marks(mark_ref, walk, at, size):
    per = walk.nblocks // 4 * BLOCK
    chunk = lax.bitwise_xor(lax.div(at, per), walk.rank)
    natural = pl.multiple_of(chunk * per + lax.rem(at, per), BLOCK)
    rows = mark_ref[pl.ds(natural, size), :]
    return jnp.concatenate([rows] * (walk.heads // 2), axis=1)


def forward_kernel(rank_ref, pick_ref, qkv_ref, mark_ref, qmark_ref, out_ref, score_ref, *, heads, rand, span):
    seq = qkv_ref.shape[0]
    width = heads * HEAD_DIM
    walk = Walk(rank_ref, pick_ref, heads, seq, rand)

    def middle(blk):
        query = spread_heads(qkv_ref[pl.ds(walk.place(blk), BLOCK), 0:width], heads)
        keys = gather_rows(qkv_ref, width, walk, blk)
        score = dot_nt(keys, query)
        ok = key_marks(mark_ref, walk, blk) == qmark_ref[pl.ds(blk, 1), :]
        score = jnp.where(ok, score, neg_large)
        expo = jnp.exp(score - jnp.max(score, axis=0, keepdims=True))
        probs = (expo * (1.0 / jnp.sum(expo, axis=0, keepdims=True))).astype(LOW)
        values = gather_rows(qkv_ref, 2 * width, walk, blk)
        out_ref[pl.ds(walk.place(blk), BLOCK), :] = own_heads(dot_tn(probs, values), heads).astype(LOW)

    def pair(step, carry):
        middle(2 * step + 1)
        middle(2 * step + 2)
        return carry

    lax.fori_loop(0, (walk.nblocks - 2) // 2, pair, 0)

    for blk in (0, walk.nblocks - 1):
        query = spread_heads(qkv_ref[pl.ds(walk.place(blk), BLOCK), 0:width], heads)
        qmark = qmark_ref[blk : blk + 1, :]

        def scores_at(step, top):
            at = pl.multiple_of(step * span, span)
            score = dot_nt(qkv_ref[pl.ds(at, span), width : 2 * width], query)
            score = jnp.where(chunk_marks(mark_ref, walk, at, span) == qmark, score, neg_large)
            score_ref[pl.ds(at, span), :] = score
            return jnp.maximum(top, jnp.max(score, axis=0, keepdims=True))

        def expo_at(step, total, top):
            at = pl.multiple_of(step * span, span)
            expo = jnp.exp(score_ref[pl.ds(at, span), :] - top)
            score_ref[pl.ds(at, span), :] = expo
            return total + jnp.sum(expo, axis=0, keepdims=True)

        def value_at(step, total, scale):
            at = pl.multiple_of(step * span, span)
            probs = (score_ref[pl.ds(at, span), :] * scale).astype(LOW)
            return total + dot_tn(probs, qkv_ref[pl.ds(at, span), 2 * width : 3 * width])

        top = jnp.full((1, heads * BLOCK), neg_large, F32)
        top = lax.fori_loop(0, seq // span, scores_at, top)
        total = lax.fori_loop(0, seq // span, partial(expo_at, top=top), jnp.zeros_like(top))
        full = lax.fori_loop(0, seq // span, partial(value_at, scale=1.0 / total), jnp.zeros((heads * BLOCK, width), F32))
        out_ref[pl.ds(walk.place(blk), BLOCK), :] = own_heads(full, heads).astype(LOW)


def backward_kernel(rank_ref, pick_ref, qkv_ref, grad_ref, mark_ref, qmark_ref, out_ref, key_acc, value_acc, score_ref, dprob_ref, *, heads, rand, span):
    seq = qkv_ref.shape[0]
    width = heads * HEAD_DIM
    walk = Walk(rank_ref, pick_ref, heads, seq, rand)
    left = left_lanes(BLOCK)

    def clear(step, carry):
        at = pl.multiple_of(step * span, span)
        key_acc[pl.ds(at, span), :] = jnp.zeros((span, width), F32)
        value_acc[pl.ds(at, span), :] = jnp.zeros((span, width), F32)
        return carry

    lax.fori_loop(0, seq // span, clear, 0)

    def add_rows(acc, rows, blk):
        for index, at in enumerate((blk - 1, blk, blk + 1, 0, walk.nblocks - 1)):
            acc[pl.ds(walk.place(at), BLOCK), :] += rows[index * BLOCK : (index + 1) * BLOCK, :]
        for slot in range(rand):
            row = (5 + slot) * BLOCK
            for pair in range(heads // 2):
                cols = slice(pair * LANES, (pair + 1) * LANES)
                piece = rows[row : row + BLOCK, cols]
                acc[pl.ds(walk.place(walk.picked(blk, 2 * pair, slot)), BLOCK), cols] += jnp.where(left, piece, 0.0)
                acc[pl.ds(walk.place(walk.picked(blk, 2 * pair + 1, slot)), BLOCK), cols] += jnp.where(left, 0.0, piece)

    def middle(blk):
        place = walk.place(blk)
        query = spread_heads(qkv_ref[pl.ds(place, BLOCK), 0:width], heads)
        grad = spread_heads(grad_ref[pl.ds(place, BLOCK), :], heads)
        keys = gather_rows(qkv_ref, width, walk, blk)
        values = gather_rows(qkv_ref, 2 * width, walk, blk)
        score = dot_nt(keys, query)
        ok = key_marks(mark_ref, walk, blk) == qmark_ref[pl.ds(blk, 1), :]
        score = jnp.where(ok, score, neg_large)
        expo = jnp.exp(score - jnp.max(score, axis=0, keepdims=True))
        probs = expo * (1.0 / jnp.sum(expo, axis=0, keepdims=True))
        dprob = dot_nt(values, grad)
        delta = jnp.sum(probs * dprob, axis=0, keepdims=True)
        dscore = (probs * (dprob - delta)).astype(LOW)
        dvalue = dot_nn(probs.astype(LOW), grad)
        dkey = dot_nn(dscore, query)
        dquery = own_heads(dot_tn(dscore, keys), heads)
        out_ref[pl.ds(place, BLOCK), 0:width] = dquery.astype(LOW)
        return dkey, dvalue

    def pair(step, carry):
        dkey_a, dvalue_a = middle(2 * step + 1)
        dkey_b, dvalue_b = middle(2 * step + 2)
        add_rows(key_acc, dkey_a, 2 * step + 1)
        add_rows(value_acc, dvalue_a, 2 * step + 1)
        add_rows(key_acc, dkey_b, 2 * step + 2)
        add_rows(value_acc, dvalue_b, 2 * step + 2)
        return carry

    lax.fori_loop(0, (walk.nblocks - 2) // 2, pair, 0)

    for blk in (0, walk.nblocks - 1):
        place = walk.place(blk)
        query = spread_heads(qkv_ref[pl.ds(place, BLOCK), 0:width], heads)
        grad = spread_heads(grad_ref[pl.ds(place, BLOCK), :], heads)
        qmark = qmark_ref[blk : blk + 1, :]

        def scores_at(step, top):
            at = pl.multiple_of(step * span, span)
            score = dot_nt(qkv_ref[pl.ds(at, span), width : 2 * width], query)
            score = jnp.where(chunk_marks(mark_ref, walk, at, span) == qmark, score, neg_large)
            score_ref[pl.ds(at, span), :] = score
            dprob_ref[pl.ds(at, span), :] = dot_nt(qkv_ref[pl.ds(at, span), 2 * width : 3 * width], grad)
            return jnp.maximum(top, jnp.max(score, axis=0, keepdims=True))

        def expo_at(step, carry, top):
            total, weighted = carry
            at = pl.multiple_of(step * span, span)
            expo = jnp.exp(score_ref[pl.ds(at, span), :] - top)
            score_ref[pl.ds(at, span), :] = expo
            return (
                total + jnp.sum(expo, axis=0, keepdims=True),
                weighted + jnp.sum(expo * dprob_ref[pl.ds(at, span), :], axis=0, keepdims=True),
            )

        def grads_at(step, dquery, scale, delta):
            at = pl.multiple_of(step * span, span)
            probs = score_ref[pl.ds(at, span), :] * scale
            dscore = (probs * (dprob_ref[pl.ds(at, span), :] - delta)).astype(LOW)
            value_acc[pl.ds(at, span), :] += dot_nn(probs.astype(LOW), grad)
            key_acc[pl.ds(at, span), :] += dot_nn(dscore, query)
            return dquery + dot_tn(dscore, qkv_ref[pl.ds(at, span), width : 2 * width])

        top = jnp.full((1, heads * BLOCK), neg_large, F32)
        top = lax.fori_loop(0, seq // span, scores_at, top)
        total, weighted = lax.fori_loop(0, seq // span, partial(expo_at, top=top), (jnp.zeros_like(top), jnp.zeros_like(top)))
        scale = 1.0 / total
        full = lax.fori_loop(0, seq // span, partial(grads_at, scale=scale, delta=weighted * scale), jnp.zeros((heads * BLOCK, width), F32))
        out_ref[pl.ds(place, BLOCK), 0:width] = own_heads(full, heads).astype(LOW)

    def finish(step, carry):
        at = pl.multiple_of(step * span, span)
        out_ref[pl.ds(at, span), width : 2 * width] = key_acc[pl.ds(at, span), :].astype(LOW)
        out_ref[pl.ds(at, span), 2 * width : 3 * width] = value_acc[pl.ds(at, span), :].astype(LOW)
        return carry

    lax.fori_loop(0, seq // span, finish, 0)


def token_marks(seq_segs, heads):
    seq = seq_segs.shape[0]
    marks = jnp.where(seq_segs != 0, seq_segs, 1000 + jnp.arange(seq, dtype=jnp.int32))
    by_row = jnp.broadcast_to(marks[:, None], (seq, LANES))
    by_block = jnp.tile(marks.reshape(seq // BLOCK, BLOCK), (1, heads))
    return by_row, by_block


SMEM_SPEC = pl.BlockSpec(memory_space=pltpu.SMEM)
VMEM_SPEC = pl.BlockSpec(memory_space=pltpu.VMEM)


def attend(rank, picks, qkv, marks):
    heads, _, rand = picks.shape
    seq = qkv.shape[0]
    width = heads * HEAD_DIM
    span = min(512, seq // 4)
    return pl.pallas_call(
        partial(forward_kernel, heads=heads, rand=rand, span=span),
        out_shape=jax.ShapeDtypeStruct((seq, width), LOW),
        in_specs=[SMEM_SPEC, SMEM_SPEC, VMEM_SPEC, VMEM_SPEC, VMEM_SPEC],
        out_specs=VMEM_SPEC,
        scratch_shapes=[pltpu.VMEM((seq, heads * BLOCK), F32)],
        name="attend",
    )(rank, picks.reshape(-1), qkv, *marks)


def attend_back(rank, picks, qkv, grad_context, marks):
    heads, _, rand = picks.shape
    seq = qkv.shape[0]
    width = heads * HEAD_DIM
    span = min(512, seq // 4)
    return pl.pallas_call(
        partial(backward_kernel, heads=heads, rand=rand, span=span),
        out_shape=jax.ShapeDtypeStruct((seq, 3 * width), LOW),
        in_specs=[SMEM_SPEC, SMEM_SPEC, VMEM_SPEC, VMEM_SPEC, VMEM_SPEC, VMEM_SPEC],
        out_specs=VMEM_SPEC,
        scratch_shapes=[pltpu.VMEM((seq, width), F32)] * 2 + [pltpu.VMEM((seq, heads * BLOCK), F32)] * 2,
        name="attend_back",
    )(rank, picks.reshape(-1), qkv, grad_context, *marks)


eps_norm = 1e-05


def norm_rows(source, gain_vec, shift_vec):
    average = jnp.mean(source, axis=-1, keepdims=True)
    centred = source - average
    variance = jnp.mean(centred * centred, axis=-1, keepdims=True)
    return centred * lax.rsqrt(variance + eps_norm) * gain_vec + shift_vec


def gelu_tanh(values):
    return jax.nn.gelu(values, approximate=True)


def swap(values, axis, mask):
    count = lax.axis_size(axis)
    return lax.ppermute(values, axis, [(i, i ^ mask) for i in range(count)])


def spread_rows(shard):
    count = lax.axis_size("fsdp")
    spot = lax.axis_index("fsdp")
    rows, cols = shard.shape
    held = shard[None]
    mask = count // 2
    while mask:
        other = swap(held, "fsdp", mask)
        upper = (spot & mask) != 0
        held = jnp.where(upper, jnp.stack([other, held], 1), jnp.stack([held, other], 1))
        held = held.reshape(-1, rows, cols)
        mask //= 2
    return held.reshape(-1, cols)


def collect_rows(terms):
    count = lax.axis_size("fsdp")
    spot = lax.axis_index("fsdp")
    rows, cols = terms.shape
    held = terms
    mask = 1
    while mask < count:
        held = held.reshape(-1, 2, rows // count, cols)
        bit = jnp.where((spot & mask) != 0, 1, 0)
        kept = lax.dynamic_index_in_dim(held, bit, 1, keepdims=False)
        sent = lax.dynamic_index_in_dim(held, 1 - bit, 1, keepdims=False)
        held = kept + swap(sent.astype(LOW), "fsdp", mask).astype(F32)
        mask *= 2
    return held.reshape(-1, cols)


def total_over(values, axes):
    for axis in axes:
        mask = 1
        while mask < lax.axis_size(axis):
            values = values + swap(values, axis, mask)
            mask *= 2
    return values


def on_device(
    hidden_in,
    cotangent,
    norm1_gain,
    norm1_bias,
    w_query,
    w_key,
    w_value,
    w_out,
    norm2_gain,
    norm2_bias,
    w_fc1,
    bias_fc1,
    w_fc2,
    bias_fc2,
    segments,
    random_blocks,
):
    rows_dev, width_model = hidden_in.shape
    heads_wide = w_query.shape[1]
    rank = lax.axis_index("tp")
    seq_segs = segments[0]
    picks = random_blocks[0]
    heads_local = picks.shape[0]
    own_segs = lax.dynamic_slice_in_dim(seq_segs, rank * rows_dev, rows_dev)
    valid_rows = (own_segs != 0).astype(F32)[:, None]
    gain_first = norm1_gain.astype(F32)
    shift_first = norm1_bias.astype(F32)
    gain_second = norm2_gain.astype(F32)
    shift_second = norm2_bias.astype(F32)
    residual_in = hidden_in.astype(F32)
    scale_query = HEAD_DIM ** (-0.5)
    rank_word = rank.astype(jnp.int32).reshape(1)
    marks = token_marks(seq_segs, heads_local)

    w_qkv = spread_rows(jnp.concatenate([w_query * jnp.asarray(scale_query, LOW), w_key, w_value], 1))
    wo_own = spread_rows(w_out.T)
    wo_far = swap(wo_own, "tp", 2)
    wo_all = jnp.concatenate([wo_own, swap(wo_own, "tp", 1), wo_far, swap(wo_far, "tp", 1)], 1)
    w_up = [spread_rows(w_fc1), spread_rows(swap(w_fc1, "tp", 2))]
    w_down_local = w_fc2.T
    w_down = [spread_rows(w_down_local), spread_rows(swap(w_down_local, "tp", 2))]
    bias_up = [bias_fc1.astype(F32), swap(bias_fc1, "tp", 2).astype(F32)]

    normed_first, norm_first_back = jax.vjp(norm_rows, residual_in, gain_first, shift_first)
    first_own = normed_first.astype(LOW)
    first_far = swap(first_own, "tp", 2)
    first_all = jnp.concatenate(
        [first_own, swap(first_own, "tp", 1), first_far, swap(first_far, "tp", 1)], 0
    )
    qkv = dot_nn(first_all, w_qkv).astype(LOW)
    context = attend(rank_word, picks, qkv, marks)
    context_cat = jnp.concatenate(
        [context[:rows_dev]]
        + [swap(context[k * rows_dev : (k + 1) * rows_dev], "tp", k) for k in (1, 2, 3)],
        1,
    )
    attn_branch = dot_nt(context_cat, wo_all)
    middle = residual_in + attn_branch
    normed_second, norm_second_back = jax.vjp(norm_rows, middle, gain_second, shift_second)
    second_own = normed_second.astype(LOW)

    second_two = jnp.concatenate([second_own, swap(second_own, "tp", 1)], 0)
    grad_two = jnp.concatenate([cotangent, swap(cotangent, "tp", 1)], 0)
    hidden = []
    grad_pre = []
    for half in range(2):
        pre_act = dot_nn(second_two, w_up[half]) + bias_up[half]
        hidden_act, gelu_back = jax.vjp(gelu_tanh, pre_act)
        hidden.append(hidden_act.astype(LOW))
        grad_pre.append(gelu_back(dot_nn(grad_two, w_down[half]))[0].astype(LOW))
    second_terms = (dot_nt(grad_pre[0], w_up[0]) + dot_nt(grad_pre[1], w_up[1]))
    grad_normed_second = second_terms[:rows_dev] + swap(second_terms[rows_dev:].astype(LOW), "tp", 1).astype(F32)
    grad_branch = cotangent.astype(F32)
    grad_mid_norm, grad_gain_second, grad_shift_second = norm_second_back(grad_normed_second)
    grad_middle = grad_branch + grad_mid_norm

    grad_attn = grad_middle.astype(LOW)
    grad_context_cat = dot_nn(grad_attn, wo_all).astype(LOW)
    grad_context = jnp.concatenate(
        [grad_context_cat[:, :heads_wide]]
        + [swap(grad_context_cat[:, k * heads_wide : (k + 1) * heads_wide], "tp", k) for k in (1, 2, 3)],
        0,
    )

    down_terms = dot_nt(hidden[0], w_down[0]) + dot_nt(hidden[1], w_down[1])
    ffn_branch = (
        down_terms[:rows_dev]
        + swap(down_terms[rows_dev:].astype(LOW), "tp", 1).astype(F32)
        + bias_fc2.astype(F32)
    )
    output_rows = middle + ffn_branch
    up_terms = [collect_rows(dot_tn(second_two, grad_pre[half])) for half in range(2)]
    down_grads = [collect_rows(dot_tn(grad_two, hidden[half])) for half in range(2)]
    grad_w_up = up_terms[0] + swap(up_terms[1].astype(LOW), "tp", 2).astype(F32)
    grad_w_down = (down_grads[0] + swap(down_grads[1].astype(LOW), "tp", 2).astype(F32)).T
    bias_terms = [jnp.sum(grad_pre[half], axis=0, dtype=F32) for half in range(2)]
    grad_bias_up = bias_terms[0] + swap(bias_terms[1], "tp", 2)
    out_terms = dot_tn(grad_attn, context_cat)
    out_near = [out_terms[:, k * heads_wide : (k + 1) * heads_wide] for k in range(4)]
    out_chip = [
        out_near[k] + swap(out_near[k + 1].astype(LOW), "tp", 1).astype(F32) for k in (0, 2)
    ]
    out_sum = out_chip[0] + swap(out_chip[1].astype(LOW), "tp", 2).astype(F32)
    grad_w_o = collect_rows(out_sum).T

    grad_qkv = attend_back(rank_word, picks, qkv, grad_context, marks)
    far_terms = dot_nt(grad_qkv[2 * rows_dev :], w_qkv)
    near_terms = dot_nt(grad_qkv[: 2 * rows_dev], w_qkv)
    far_sum = far_terms[:rows_dev] + swap(far_terms[rows_dev:].astype(LOW), "tp", 1).astype(F32)
    grad_normed_first = (
        near_terms[:rows_dev]
        + swap(near_terms[rows_dev:].astype(LOW), "tp", 1).astype(F32)
        + swap(far_sum.astype(LOW), "tp", 2).astype(F32)
    )
    grad_w_qkv = collect_rows(dot_tn(first_all, grad_qkv))
    grad_w_q = grad_w_qkv[:, :heads_wide] * scale_query
    grad_w_k = grad_w_qkv[:, heads_wide : 2 * heads_wide]
    grad_w_v = grad_w_qkv[:, 2 * heads_wide :]
    grad_in_norm, grad_gain_first, grad_shift_first = norm_first_back(grad_normed_first)
    grad_input = grad_middle + grad_in_norm

    square_sums = jnp.stack(
        [
            jnp.sum(valid_rows * branch * branch)
            for branch in (residual_in, attn_branch, middle, ffn_branch)
        ]
        + [jnp.sum(valid_rows)]
    )
    early = jnp.concatenate(
        [grad_gain_second, grad_shift_second, jnp.sum(grad_branch, axis=0), square_sums]
    )
    early = total_over(early, ("tp",))
    early_size = early.shape[0]
    early = total_over(jnp.concatenate([early, grad_bias_up]), ("fsdp",))
    late = total_over(jnp.concatenate([grad_gain_first, grad_shift_first]), ("tp", "fsdp"))
    square_sums = early[3 * width_model : early_size]
    residual_rms = jnp.sqrt(square_sums[:4] / (square_sums[4] * width_model))
    return (
        output_rows.astype(LOW),
        grad_input,
        late[:width_model],
        late[width_model:],
        grad_w_q,
        grad_w_k,
        grad_w_v,
        grad_w_o,
        early[:width_model],
        early[width_model : 2 * width_model],
        grad_w_up,
        early[early_size:],
        grad_w_down,
        early[2 * width_model : 3 * width_model],
        residual_rms,
    )


def solution(mesh):
    in_specs = (
        P(("fsdp", "tp"), None),
        P(("fsdp", "tp"), None),
        P(),
        P(),
        P("fsdp", "tp"),
        P("fsdp", "tp"),
        P("fsdp", "tp"),
        P("tp", "fsdp"),
        P(),
        P(),
        P("fsdp", "tp"),
        P("tp"),
        P("tp", "fsdp"),
        P(),
        P("fsdp", None),
        P("fsdp", "tp", None, None),
    )
    out_specs = (
        P(("fsdp", "tp"), None),
        P(("fsdp", "tp"), None),
        P(),
        P(),
        P("fsdp", "tp"),
        P("fsdp", "tp"),
        P("fsdp", "tp"),
        P("tp", "fsdp"),
        P(),
        P(),
        P("fsdp", "tp"),
        P("tp"),
        P("tp", "fsdp"),
        P(),
        P(),
    )
    return jax.shard_map(
        on_device, mesh=mesh, in_specs=in_specs, out_specs=out_specs, check_vma=False
    )
```

time: 2390 us -> 799 us (0.33)
  other arithmetic: 705 us -> 82.5 us
  waiting for transfers between devices: 896 us -> 289 us
  matrix products: 414 us -> 155 us
  blocking collectives: 171 us -> 0 us
  Pallas kernels: 0 us -> 128 us
  local copies, waits for them, and re-layouts: 175 us -> 62.1 us
  starting transfers between devices: 0.88 us -> 70.3 us
    reduce_scatter x10 -> x0, waiting for transfers between devices: 701 us -> none  [the longest x2 185 us: attn_collect(): return lax.psum_scatter(terms, 'tp', scatter_dimension=0, tiled=True)]
    unnamed x7 -> x1, other arithmetic: 609 us -> 0.68 us
    ppermute x0 -> x74, waiting for transfers between devices: none -> 289 us  [swap(): return lax.ppermute(values, axis, [(i, i ^ mask) for i in range(count)])]
    all_gather x6 -> x0, waiting for transfers between devices: 192 us -> none  [the longest x2 115 us: ffn_spread(): return lax.all_gather(source, 'tp', axis=0, tiled=True)]
    dot_general x24 -> x19, matrix products: 297 us -> 155 us  [the longest x6 64.3 us: dot_nn(): lax.dot_general(a, b, (((1,), (0,)), ((), ())), preferred_element_type=F32)]
    all_gather x4 -> x0, blocking collectives: 129 us -> none  [the longest x1 35.5 us: on_device(): lax.all_gather(w_query, 'fsdp', axis=0, tiled=True)]
    pallas_call x0 -> x2, Pallas kernels: none -> 128 us  [the longest x1 74.1 us: attend_back(): pl.pallas_call(partial(backward_kernel, heads=heads, rand=rand, span=span...]
    ppermute x0 -> x74, starting transfers between devices: none -> 70.3 us  [swap(): return lax.ppermute(values, axis, [(i, i ^ mask) for i in range(count)])]
  transfers between devices with their start and end apart: 16 -> 74, of which waited for: 13 -> 26; matrix products, arithmetic and copies ran while one was open for 43% -> 29% of each run, Pallas kernels for 0% -> 16%
where the time goes in v1:
time: 799 us; the launch traced here: 790 us
  waiting for transfers between devices  289 us (36%)
  matrix products  155 us (19%)
  Pallas kernels  128 us (16%)
  other arithmetic  82.5 us (10%)
  starting transfers between devices  70.3 us (9%)
  local copies, waits for them, and re-layouts  62.1 us (8%)
    ppermute x74, waiting for transfers between devices, swap(): return lax.ppermute(values, axis, [(i, i ^ mask) for i in range(count)])  289 us
    pallas_call x1, Pallas kernels, attend_back(): pl.pallas_call(partial(backward_kernel, heads=heads, rand=rand, span=span...  74.1 us
    ppermute x74, starting transfers between devices, swap(): return lax.ppermute(values, axis, [(i, i ^ mask) for i in range(count)])  70.3 us
    dot_general x6, matrix products, dot_nn(): lax.dot_general(a, b, (((1,), (0,)), ((), ())), preferred_element_type=F32)  64.3 us
    pallas_call x1, Pallas kernels, attend(): pl.pallas_call(partial(forward_kernel, heads=heads, rand=rand, span=span)...  54.2 us
    dot_general x7, matrix products, dot_nt(): lax.dot_general(a, b, (((1,), (1,)), ((), ())), preferred_element_type=F32)  49.3 us
    dot_general x6, matrix products, dot_tn(): lax.dot_general(a, b, (((0,), (0,)), ((), ())), preferred_element_type=F32)  41 us
    unnamed x150, local copies, waits for them, and re-layouts  32.3 us
  transfers between devices with their start and end apart: 74, of which 26 were waited for; matrix products, arithmetic and copies ran while one was open for 29% of the time, Pallas kernels for 16%

profile of v1, /device:TPU:0, one launch (start us, length us, event | category | flops | bytes accessed | tf_op | source)
XLA Modules:
  0.0 789.6 jit_solution(14133940530384525476)
XLA Ops:
  11.0 45.9 %collective-permute-done.1 = bf16[1024,1024]{0,1:T(8,128)(2,1)} collective-permute-done((bf16[1024,1024]{0,1:T(8,128)(2,1)}, bf16[1024,1024]{0,1:T(8,128)(2,1)}, u32[]{:S(2)}, u32[]{:S(2)}) %collective-permute-start.1) | collective-permute-done | bytes 2097184 | tf_op jit(solution)/shard_map/ppermute | solution.py:332
  60.1 11.4 %collective-permute-done.3 = bf16[1,128,768]{2,1,0:T(8,128)(2,1)S(1)} collective-permute-done((bf16[1,128,768]{2,1,0:T(8,128)(2,1)S(1)}, bf16[1,128,768]{2,1,0:T(8,128)(2,1)S(1)}, u32[]{:S(2)}, u32[]{:S(2)}) %collective-permute-start.3) | collective-permute-done | bytes 196640 | tf_op jit(solution)/shard_map/ppermute | solution.py:332
  77.5 11.7 %collective-permute-done.4 = bf16[2,128,768]{2,1,0:T(8,128)(2,1)S(1)} collective-permute-done((bf16[2,128,768]{2,1,0:T(8,128)(2,1)S(1)}, bf16[2,128,768]{2,1,0:T(8,128)(2,1)S(1)}, u32[]{:S(2)}, u32[]{:S(2)}) %collective-permute-start.4) | collective-permute-done | bytes 393248 | tf_op jit(solution)/shard_map/ppermute | solution.py:332
  97.3 14.4 %collective-permute-done.11 = bf16[4,128,256]{2,1,0:T(8,128)(2,1)S(1)} collective-permute-done((bf16[4,128,256]{2,1,0:T(8,128)(2,1)}, bf16[4,128,256]{2,1,0:T(8,128)(2,1)S(1)}, u32[]{:S(2)}, u32[]{:S(2)}) %collective-permute-start.11) | collective-permute-done | bytes 262176 | tf_op jit(solution)/shard_map/ppermute | solution.py:332
  134.4 14.5 %convolution_convert_fusion.qkv_ref = bf16[4096,768]{1,0:T(8,128)(2,1)} fusion(bf16[1024,768]{1,0:T(8,128)(2,1)S(1)} %bitcast.245, bf16[1024,1024]{0,1:T(8,128)(2,1)} %collective-permute-done.2, bf16[1024,1024]{0,1:T(8,128)(2,1)} %collective-permute-done.1, bf16[1024,1024]{0,1:T(8,128)(2,1)} %collective-permute-done, bf16[1024,1024]{0,1:T(8,128)(2,1)} %fusion.21), kind=kOutput, calls=%fused_computation.28 | convolution fusion | flops 6479151104 | bytes 16252928 | tf_op jit(solution)/shard_map/dot_general | solution.py:17
  151.8 54.2 %attend.1 = bf16[4096,256]{1,0:T(8,128)(2,1)} custom-call(s32[1]{0:T(128)} %bitcast.rank_ref, s32[744]{0:T(1024)} %reshape_squeeze.4.pick_ref, bf16[4096,768]{1,0:T(8,128)(2,1)} %convolution_convert_fusion.qkv_ref, s32[4096,128]{1,0:T(8,128)} %broadcast_in_dim.23.mark_ref, s32[64,256]{1,0:T(8,128)} %tile.9.qmark_ref), custom_call_target="tpu_custom_call" | custom-call | tf_op jit(solution)/shard_map/attend/pallas_call | solution.py:291
  218.3 4.0 collective-permute-done.8
  222.4 11.4 %collective-permute-done.7 = bf16[1024,256]{1,0:T(8,128)(2,1)S(1)} collective-permute-done((bf16[1024,256]{1,0:T(8,128)(2,1)S(1)}, bf16[1024,256]{1,0:T(8,128)(2,1)S(1)}, u32[]{:S(2)}, u32[]{:S(2)}) %collective-permute-start.7) | collective-permute-done | bytes 524320 | tf_op jit(solution)/shard_map/ppermute | solution.py:332
  235.4 5.6 fusion.81
  251.7 7.2 collective-permute-done.29
  264.4 3.9 copy.65
  272.6 9.9 %collective-permute-done.21 = bf16[4,128,1024]{2,1,0:T(8,128)(2,1)} collective-permute-done((bf16[4,128,1024]{2,1,0:T(8,128)(2,1)S(1)}, bf16[4,128,1024]{2,1,0:T(8,128)(2,1)}, u32[]{:S(2)}, u32[]{:S(2)}) %collective-permute-start.21) | collective-permute-done | bytes 1048608 | tf_op jit(solution)/shard_map/ppermute | solution.py:332
  284.6 20.4 %collective-permute-done.25 = bf16[4,128,1024]{2,1,0:T(8,128)(2,1)} collective-permute-done((bf16[4,128,1024]{2,1,0:T(8,128)(2,1)S(1)}, bf16[4,128,1024]{2,1,0:T(8,128)(2,1)}, u32[]{:S(2)}, u32[]{:S(2)}) %collective-permute-start.25) | collective-permute-done | bytes 1048608 | tf_op jit(solution)/shard_map/ppermute | solution.py:332
  307.1 19.2 %collective-permute-done.30 = bf16[4,128,1024]{2,1,0:T(8,128)(2,1)} collective-permute-done((bf16[4,128,1024]{2,1,0:T(8,128)(2,1)}, bf16[4,128,1024]{2,1,0:T(8,128)(2,1)}, u32[]{:S(2)}, u32[]{:S(2)}) %collective-permute-start.30) | collective-permute-done | bytes 1048608 | tf_op jit(solution)/shard_map/ppermute | solution.py:332
  331.0 9.5 %fusion.73 = f32[2048,1024]{1,0:T(8,128)} fusion(bf16[1024,1024]{1,0:T(8,128)(2,1)S(1)} %bitcast.235, bf16[1024,1024]{0,1:T(8,128)(2,1)} %collective-permute-done.15, bf16[1024,1024]{0,1:T(8,128)(2,1)} %add_convert_fusion.1), kind=kOutput, calls=%fused_computation.198 | convolution fusion | flops 4303355904 | bytes 14680064 | tf_op jit(solution)/shard_map/dot_general | solution.py:17
  340.5 13.4 %convert_reduce_fusion.1 = (f32[1024]{0:T(1024)S(1)}, bf16[2048,1024]{1,0:T(8,128)(2,1)}, bf16[2048,1024]{1,0:T(8,128)(2,1)S(1)}) fusion(f32[2048,1024]{1,0:T(8,128)} %fusion.73, f32[1024]{0:T(1024)S(1)} %convert_element_type.298, bf16[2048,1024]{1,0:T(8,128)(2,1)S(1)} %constant_dynamic-update-slice_fusion, bf16[1024,1024]{1,0:T(8,128)(2,1)S(1)} %bitcast.239), kind=kOutput, calls=%fused_computation.20 | convolution fusion | flops 4347395072 | bytes 23076864 | tf_op jit(solution)/shard_map/dot_general | solution.py:17
  353.9 4.6 fusion.91
  358.6 6.7 fusion.89
  365.3 9.3 %fusion.72 = f32[2048,1024]{1,0:T(8,128)} fusion(bf16[1024,1024]{1,0:T(8,128)(2,1)S(1)} %bitcast.233, bf16[1024,1024]{0,1:T(8,128)(2,1)} %collective-permute-done.15, bf16[1024,1024]{0,1:T(8,128)(2,1)} %add_convert_fusion.1), kind=kOutput, calls=%fused_computation.197 | convolution fusion | flops 4303355904 | bytes 14680064 | tf_op jit(solution)/shard_map/dot_general | solution.py:17
  374.6 7.4 fusion.75
  384.6 13.9 %convert_reduce_fusion = (f32[1024]{0:T(1024)S(1)}, bf16[2048,1024]{1,0:T(8,128)(2,1)}) fusion(f32[2048,1024]{1,0:T(8,128)} %fusion.72, f32[1024]{0:T(1024)S(1)} %convert_element_type.300, bf16[2048,1024]{1,0:T(8,128)(2,1)S(1)} %constant_dynamic-update-slice_fusion, bf16[1024,1024]{1,0:T(8,128)(2,1)S(1)} %bitcast.237), kind=kOutput, calls=%fused_computation.19 | convolution fusion | flops 4343200768 | bytes 18882560 | tf_op jit(solution)/shard_map/dot_general | solution.py:17
  400.0 7.7 fusion.70
  411.8 6.8 fusion.90
  418.6 6.4 fusion.71
  428.3 10.5 %convolution_add_fusion.1 = f32[2048,1024]{0,1:T(8,128)S(1)} fusion(f32[2048,1024]{0,1:T(8,128)} %fusion.89, bf16[1024,1024]{1,0:T(8,128)(2,1)S(1)} %bitcast.238, f32[2048,1024]{1,0:T(8,128)} %fusion.72, f32[1024]{0:T(1024)S(1)} %convert_element_type.300), kind=kOutput, calls=%fused_computation.70 | convolution fusion | flops 4318035968 | bytes 27267072 | tf_op jit(solution)/shard_map/dot_general | solution.py:21
  438.8 8.8 %convolution_add_fusion = f32[2048,1024]{0,1:T(8,128)S(1)} fusion(f32[2048,1024]{0,1:T(8,128)} %fusion.90, bf16[2048,1024]{1,0:T(8,128)(2,1)} %get-tuple-element.58, bf16[1024,1024]{1,0:T(8,128)(2,1)S(1)} %bitcast.234), kind=kOutput, calls=%fused_computation.69 | convolution fusion | flops 4297064448 | bytes 23068672 | tf_op jit(solution)/shard_map/dot_general | solution.py:21
  461.2 16.5 %collective-permute-done.67 = bf16[4,128,1024]{2,1,0:T(8,128)(2,1)} collective-permute-done((bf16[4,128,1024]{2,1,0:T(8,128)(2,1)S(1)}, bf16[4,128,1024]{2,1,0:T(8,128)(2,1)}, u32[]{:S(2)}, u32[]{:S(2)}) %collective-permute-start.67) | collective-permute-done | bytes 1048608 | tf_op jit(solution)/shard_map/ppermute | solution.py:332
  482.0 18.7 %collective-permute-done.61 = bf16[2,128,1024]{2,1,0:T(8,128)(2,1)S(1)} collective-permute-done((bf16[2,128,1024]{2,1,0:T(8,128)(2,1)S(1)}, bf16[2,128,1024]{2,1,0:T(8,128)(2,1)S(1)}, u32[]{:S(2)}, u32[]{:S(2)}) %collective-permute-start.61) | collective-permute-done | bytes 524320 | tf_op jit(solution)/shard_map/ppermute | solution.py:332
  501.6 8.2 %collective-permute-done.68 = bf16[2,128,1024]{2,1,0:T(8,128)(2,1)S(1)} collective-permute-done((bf16[2,128,1024]{2,1,0:T(8,128)(2,1)S(1)}, bf16[2,128,1024]{2,1,0:T(8,128)(2,1)S(1)}, u32[]{:S(2)}, u32[]{:S(2)}) %collective-permute-start.68) | collective-permute-done | bytes 524320 | tf_op jit(solution)/shard_map/ppermute | solution.py:332
  510.7 12.5 %collective-permute-done.65 = bf16[1,128,1024]{2,1,0:T(8,128)(2,1)S(1)} collective-permute-done((bf16[1,128,1024]{2,1,0:T(8,128)(2,1)S(1)}, bf16[1,128,1024]{2,1,0:T(8,128)(2,1)S(1)}, u32[]{:S(2)}, u32[]{:S(2)}) %collective-permute-start.65) | collective-permute-done | bytes 262176 | tf_op jit(solution)/shard_map/ppermute | solution.py:332
  525.3 7.7 multiply_reduce_fusion
  537.0 3.6 convolution_convert_fusion.1
  542.7 4.4 fusion.88
  548.0 7.0 collective-permute-done.36
  555.1 11.2 %collective-permute-done.35 = bf16[1024,256]{1,0:T(8,128)(2,1)S(1)} collective-permute-done((bf16[1024,256]{1,0:T(8,128)(2,1)S(1)}, bf16[1024,256]{1,0:T(8,128)(2,1)S(1)}, u32[]{:S(2)}, u32[]{:S(2)}) %collective-permute-start.35) | collective-permute-done | bytes 524320 | tf_op jit(solution)/shard_map/ppermute | solution.py:332
  567.9 74.1 %attend_back.1 = bf16[4096,768]{1,0:T(8,128)(2,1)} custom-call(s32[1]{0:T(128)} %bitcast.rank_ref, s32[744]{0:T(1024)} %reshape_squeeze.4.pick_ref, bf16[4096,768]{1,0:T(8,128)(2,1)} %convolution_convert_fusion.qkv_ref, bf16[4096,256]{1,0:T(8,128)(2,1)} %pad_maximum_fusion.4.grad_ref, s32[4096,128]{1,0:T(8,128)} %broadcast_in_dim.23.mark_ref, ...), custom_call_target="tpu_custom_call" | custom-call | tf_op jit(solution)/shard_map/attend_back/pallas_call | solution.py:306
  642.0 5.9 fusion.32
  648.8 10.5 %fusion.37 = f32[1024,768]{1,0:T(8,128)} fusion(bf16[4096,768]{1,0:T(8,128)(2,1)S(1)} %copy-done.8, bf16[1024,1024]{0,1:T(8,128)(2,1)} %collective-permute-done.2, bf16[1024,1024]{0,1:T(8,128)(2,1)} %collective-permute-done.1, bf16[1024,1024]{0,1:T(8,128)(2,1)} %collective-permute-done, bf16[1024,1024]{0,1:T(8,128)(2,1)} %fusion.21), kind=kOutput, calls=%fused_computation.95 | convolution fusion | flops 6476005376 | bytes 17825792 | tf_op jit(solution)/shard_map/dot_general | solution.py:25
  659.4 5.0 fusion.34
  672.8 3.8 fusion.29
  680.6 7.0 collective-permute-done.50
  692.1 5.5 collective-permute-done.51
  699.8 37.2 %collective-permute-done.73 = bf16[128,1024]{1,0:T(8,128)(2,1)S(1)} collective-permute-done((bf16[128,1024]{1,0:T(8,128)(2,1)S(1)}, bf16[128,1024]{1,0:T(8,128)(2,1)S(1)}, u32[]{:S(2)}, u32[]{:S(2)}) %collective-permute-start.73) | collective-permute-done | bytes 262176 | tf_op jit(solution)/shard_map/ppermute | solution.py:332
  738.1 3.9 copy.80
  743.6 4.3 fusion.27
  748.0 3.8 fusion.22
  751.9 4.0 convert_reduce_fusion.3
  776.5 5.3 copy.81
  (405 shorter events, 187.6 us)
Async XLA Ops:
  8.1 48.9 %collective-permute-start.1 = (bf16[1024,1024]{0,1:T(8,128)(2,1)}, bf16[1024,1024]{0,1:T(8,128)(2,1)}, u32[]{:S(2)}, u32[]{:S(2)}) collective-permute-start(bf16[1024,1024]{0,1:T(8,128)(2,1)} %fusion.21), channel_id=1, source_target_pairs={{0,2},{1,3},{2,0},{3,1},{4,6},{5,7},{6,4},{7,5},{8,10},{9,11},{10,... | collective-permute-start | bytes 6291464 | tf_op jit(solution)/shard_map/ppermute | solution.py:332
  11.0 120.2 %collective-permute-start = (bf16[1024,1024]{0,1:T(8,128)(2,1)}, bf16[1024,1024]{0,1:T(8,128)(2,1)}, u32[]{:S(2)}, u32[]{:S(2)}) collective-permute-start(bf16[1024,1024]{0,1:T(8,128)(2,1)} %fusion.21), channel_id=1, source_target_pairs={{0,1},{1,0},{2,3},{3,2},{4,5},{5,4},{6,7},{7,6},{8,9},{9,8},{10,11... | collective-permute-start | bytes 6291464 | tf_op jit(solution)/shard_map/ppermute | solution.py:332
  57.0 76.9 %collective-permute-start.2 = (bf16[1024,1024]{0,1:T(8,128)(2,1)}, bf16[1024,1024]{0,1:T(8,128)(2,1)}, u32[]{:S(2)}, u32[]{:S(2)}) collective-permute-start(bf16[1024,1024]{0,1:T(8,128)(2,1)} %collective-permute-done.1), channel_id=1, source_target_pairs={{0,1},{1,0},{2,3},{3,2},{4,5},{5,4},{6,7},{7,6},{8,9},{9,8},{10,11... | collective-permute-start | bytes 6291464 | tf_op jit(solution)/shard_map/ppermute | solution.py:332
  72.0 23.8 %collective-permute-start.16 = (bf16[1,128,1024]{2,1,0:T(8,128)(2,1)}, bf16[1,128,1024]{2,1,0:T(8,128)(2,1)}, u32[]{:S(2)}, u32[]{:S(2)}) collective-permute-start(bf16[1,128,1024]{2,1,0:T(8,128)(2,1)} %bitcast.21), channel_id=1, source_target_pairs={{0,16},{4,20},{8,24},{12,28},{16,0},{20,4},{24,8},{28,12},{1,17},{... | collective-permute-start | bytes 786440 | tf_op jit(solution)/shard_map/ppermute | solution.py:332
  89.3 37.6 %collective-permute-start.5 = (bf16[4,128,768]{2,1,0:T(8,128)(2,1)S(1)}, bf16[4,128,768]{2,1,0:T(8,128)(2,1)}, u32[]{:S(2)}, u32[]{:S(2)}) collective-permute-start(bf16[4,128,768]{2,1,0:T(8,128)(2,1)S(1)} %bitcast.219), channel_id=1, source_target_pairs={{0,4},{4,0},{8,12},{12,8},{16,20},{20,16},{24,28},{28,24},{1,5},{5... | collective-permute-start | bytes 2359304 | tf_op jit(solution)/shard_map/ppermute | solution.py:332
  91.6 20.1 %collective-permute-start.11 = (bf16[4,128,256]{2,1,0:T(8,128)(2,1)}, bf16[4,128,256]{2,1,0:T(8,128)(2,1)S(1)}, u32[]{:S(2)}, u32[]{:S(2)}) collective-permute-start(bf16[4,128,256]{2,1,0:T(8,128)(2,1)} %bitcast.17), channel_id=1, source_target_pairs={{0,4},{4,0},{8,12},{12,8},{16,20},{20,16},{24,28},{28,24},{1,5},{5... | collective-permute-start | bytes 786440 | tf_op jit(solution)/shard_map/ppermute | solution.py:332
  95.8 30.9 %collective-permute-start.22 = (bf16[128,1024]{1,0:T(8,128)(2,1)}, bf16[128,1024]{1,0:T(8,128)(2,1)}, u32[]{:S(2)}, u32[]{:S(2)}) collective-permute-start(bf16[128,1024]{1,0:T(8,128)(2,1)} %param.26), channel_id=1, source_target_pairs={{0,2},{1,3},{2,0},{3,1},{4,6},{5,7},{6,4},{7,5},{8,10},{9,11},{10,... | collective-permute-start | bytes 786440 | tf_op jit(solution)/shard_map/ppermute | solution.py:332
  123.9 83.9 %collective-permute-start.19 = (bf16[1,128,1024]{2,1,0:T(8,128)(2,1)S(1)}, bf16[1,128,1024]{2,1,0:T(8,128)(2,1)}, u32[]{:S(2)}, u32[]{:S(2)}) collective-permute-start(bf16[1,128,1024]{2,1,0:T(8,128)(2,1)S(1)} %bitcast.230), channel_id=1, source_target_pairs={{0,16},{4,20},{8,24},{12,28},{16,0},{20,4},{24,8},{28,12},{1,17},{... | collective-permute-start | bytes 786440 | tf_op jit(solution)/shard_map/ppermute | solution.py:332
  126.7 81.6 %collective-permute-start.28 = (bf16[1,128,1024]{2,1,0:T(8,128)(2,1)S(1)}, bf16[1,128,1024]{2,1,0:T(8,128)(2,1)}, u32[]{:S(2)}, u32[]{:S(2)}) collective-permute-start(bf16[1,128,1024]{2,1,0:T(8,128)(2,1)S(1)} %bitcast.249), channel_id=1, source_target_pairs={{0,16},{4,20},{8,24},{12,28},{16,0},{20,4},{24,8},{28,12},{1,17},{... | collective-permute-start | bytes 786440 | tf_op jit(solution)/shard_map/ppermute | solution.py:332
  126.8 82.7 %collective-permute-start.23 = (bf16[1,128,1024]{2,1,0:T(8,128)(2,1)}, bf16[1,128,1024]{2,1,0:T(8,128)(2,1)}, u32[]{:S(2)}, u32[]{:S(2)}) collective-permute-start(bf16[1,128,1024]{2,1,0:T(8,128)(2,1)} %bitcast.40), channel_id=1, source_target_pairs={{0,16},{4,20},{8,24},{12,28},{16,0},{20,4},{24,8},{28,12},{1,17},{... | collective-permute-start | bytes 786440 | tf_op jit(solution)/shard_map/ppermute | solution.py:332
  131.3 78.8 %collective-permute-start.17 = (bf16[2,128,1024]{2,1,0:T(8,128)(2,1)}, bf16[2,128,1024]{2,1,0:T(8,128)(2,1)S(1)}, u32[]{:S(2)}, u32[]{:S(2)}) collective-permute-start(bf16[2,128,1024]{2,1,0:T(8,128)(2,1)} %maximum_select_fusion.11), channel_id=1, source_target_pairs={{0,8},{4,12},{8,0},{12,4},{16,24},{20,28},{24,16},{28,20},{1,9},{5... | collective-permute-start | bytes 1572872 | tf_op jit(solution)/shard_map/ppermute | solution.py:332
  133.8 74.0 %collective-permute-start.13 = (bf16[1024,256]{1,0:T(8,128)(2,1)}, bf16[1024,256]{1,0:T(8,128)(2,1)}, u32[]{:S(2)}, u32[]{:S(2)}) collective-permute-start(bf16[1024,256]{1,0:T(8,128)(2,1)} %bitcast.20), channel_id=1, source_target_pairs={{0,2},{1,3},{2,0},{3,1},{4,6},{5,7},{6,4},{7,5},{8,10},{9,11},{10,... | collective-permute-start | bytes 1572872 | tf_op jit(solution)/shard_map/ppermute | solution.py:332
  209.5 24.3 %collective-permute-start.7 = (bf16[1024,256]{1,0:T(8,128)(2,1)S(1)}, bf16[1024,256]{1,0:T(8,128)(2,1)S(1)}, u32[]{:S(2)}, u32[]{:S(2)}) collective-permute-start(bf16[1024,256]{1,0:T(8,128)(2,1)S(1)} %get-tuple-element.79), channel_id=1, source_target_pairs={{0,2},{1,3},{2,0},{3,1},{4,6},{5,7},{6,4},{7,5},{8,10},{9,11},{10,... | collective-permute-start | bytes 1572872 | tf_op jit(solution)/shard_map/ppermute | solution.py:332
  210.1 23.8 %collective-permute-start.6 = (bf16[1024,256]{1,0:T(8,128)(2,1)S(1)}, bf16[1024,256]{1,0:T(8,128)(2,1)S(1)}, u32[]{:S(2)}, u32[]{:S(2)}) collective-permute-start(bf16[1024,256]{1,0:T(8,128)(2,1)S(1)} %get-tuple-element.80), channel_id=1, source_target_pairs={{0,1},{1,0},{2,3},{3,2},{4,5},{5,4},{6,7},{7,6},{8,9},{9,8},{10,11... | collective-permute-start | bytes 1572872 | tf_op jit(solution)/shard_map/ppermute | solution.py:332
  216.7 27.2 %collective-permute-start.26 = (bf16[1024]{0:T(1024)(128)(2,1)S(1)}, bf16[1024]{0:T(1024)(128)(2,1)S(1)}, u32[]{:S(2)}, u32[]{:S(2)}) collective-permute-start(bf16[1024]{0:T(1024)(128)(2,1)S(1)} %copy-done.57), channel_id=1, source_target_pairs={{0,2},{1,3},{2,0},{3,1},{4,6},{5,7},{6,4},{7,5},{8,10},{9,11},{10,... | collective-permute-start | bytes 6152 | tf_op jit(solution)/shard_map/ppermute | solution.py:332
  218.2 111.0 %collective-permute-start.32 = (bf16[1024,1024]{1,0:T(8,128)(2,1)}, bf16[1024,1024]{1,0:T(8,128)(2,1)}, u32[]{:S(2)}, u32[]{:S(2)}) collective-permute-start(bf16[1024,1024]{1,0:T(8,128)(2,1)} %param.17), channel_id=1, source_target_pairs={{0,1},{1,0},{2,3},{3,2},{4,5},{5,4},{6,7},{7,6},{8,9},{9,8},{10,11... | collective-permute-start | bytes 6291464 | tf_op jit(solution)/shard_map/ppermute | solution.py:332
  222.3 23.6 %collective-permute-start.20 = (bf16[2,128,1024]{2,1,0:T(8,128)(2,1)S(1)}, bf16[2,128,1024]{2,1,0:T(8,128)(2,1)S(1)}, u32[]{:S(2)}, u32[]{:S(2)}) collective-permute-start(bf16[2,128,1024]{2,1,0:T(8,128)(2,1)S(1)} %maximum_select_fusion.13), channel_id=1, source_target_pairs={{0,8},{4,12},{8,0},{12,4},{16,24},{20,28},{24,16},{28,20},{1,9},{5... | collective-permute-start | bytes 1572872 | tf_op jit(solution)/shard_map/ppermute | solution.py:332
  233.9 29.0 %collective-permute-start.18 = (bf16[4,128,1024]{2,1,0:T(8,128)(2,1)S(1)}, bf16[4,128,1024]{2,1,0:T(8,128)(2,1)S(1)}, u32[]{:S(2)}, u32[]{:S(2)}) collective-permute-start(bf16[4,128,1024]{2,1,0:T(8,128)(2,1)S(1)} %bitcast.211), channel_id=1, source_target_pairs={{0,4},{4,0},{8,12},{12,8},{16,20},{20,16},{24,28},{28,24},{1,5},{5... | collective-permute-start | bytes 3145736 | tf_op jit(solution)/shard_map/ppermute | solution.py:332
  245.9 85.1 %collective-permute-start.15 = (bf16[1024,1024]{0,1:T(8,128)(2,1)}, bf16[1024,1024]{0,1:T(8,128)(2,1)}, u32[]{:S(2)}, u32[]{:S(2)}) collective-permute-start(bf16[1024,1024]{0,1:T(8,128)(2,1)} %add_convert_fusion.1), channel_id=1, source_target_pairs={{0,1},{1,0},{2,3},{3,2},{4,5},{5,4},{6,7},{7,6},{8,9},{9,8},{10,11... | collective-permute-start | bytes 6291464 | tf_op jit(solution)/shard_map/ppermute | solution.py:332
  248.6 33.9 %collective-permute-start.21 = (bf16[4,128,1024]{2,1,0:T(8,128)(2,1)S(1)}, bf16[4,128,1024]{2,1,0:T(8,128)(2,1)}, u32[]{:S(2)}, u32[]{:S(2)}) collective-permute-start(bf16[4,128,1024]{2,1,0:T(8,128)(2,1)S(1)} %bitcast.213), channel_id=1, source_target_pairs={{0,4},{4,0},{8,12},{12,8},{16,20},{20,16},{24,28},{28,24},{1,5},{5... | collective-permute-start | bytes 3145736 | tf_op jit(solution)/shard_map/ppermute | solution.py:332
  258.9 46.0 %collective-permute-start.25 = (bf16[4,128,1024]{2,1,0:T(8,128)(2,1)S(1)}, bf16[4,128,1024]{2,1,0:T(8,128)(2,1)}, u32[]{:S(2)}, u32[]{:S(2)}) collective-permute-start(bf16[4,128,1024]{2,1,0:T(8,128)(2,1)S(1)} %bitcast.215), channel_id=1, source_target_pairs={{0,4},{4,0},{8,12},{12,8},{16,20},{20,16},{24,28},{28,24},{1,5},{5... | collective-permute-start | bytes 3145736 | tf_op jit(solution)/shard_map/ppermute | solution.py:332
  263.9 62.4 %collective-permute-start.30 = (bf16[4,128,1024]{2,1,0:T(8,128)(2,1)}, bf16[4,128,1024]{2,1,0:T(8,128)(2,1)}, u32[]{:S(2)}, u32[]{:S(2)}) collective-permute-start(bf16[4,128,1024]{2,1,0:T(8,128)(2,1)} %bitcast.53), channel_id=1, source_target_pairs={{0,4},{4,0},{8,12},{12,8},{16,20},{20,16},{24,28},{28,24},{1,5},{5... | collective-permute-start | bytes 3145736 | tf_op jit(solution)/shard_map/ppermute | solution.py:332
  383.1 68.4 %collective-permute-start.70 = (bf16[4,128,1024]{2,1,0:T(8,128)(2,1)}, bf16[4,128,1024]{2,1,0:T(8,128)(2,1)}, u32[]{:S(2)}, u32[]{:S(2)}) collective-permute-start(bf16[4,128,1024]{2,1,0:T(8,128)(2,1)} %fusion.39), channel_id=1, source_target_pairs={{0,4},{4,0},{8,12},{12,8},{16,20},{20,16},{24,28},{28,24},{1,5},{5... | collective-permute-start | bytes 3145736 | tf_op jit(solution)/shard_map/ppermute | solution.py:332
  398.5 52.4 %collective-permute-start.56 = (f32[1024]{0:T(1024)S(1)}, f32[1024]{0:T(1024)S(1)}, u32[]{:S(2)}, u32[]{:S(2)}) collective-permute-start(f32[1024]{0:T(1024)S(1)} %get-tuple-element.57), channel_id=1, source_target_pairs={{0,2},{1,3},{2,0},{3,1},{4,6},{5,7},{6,4},{7,5},{8,10},{9,11},{10,... | collective-permute-start | bytes 12296 | tf_op jit(solution)/shard_map/ppermute | solution.py:332
  408.9 44.9 %collective-permute-start.63 = (bf16[4,128,1024]{2,1,0:T(8,128)(2,1)}, bf16[4,128,1024]{2,1,0:T(8,128)(2,1)}, u32[]{:S(2)}, u32[]{:S(2)}) collective-permute-start(bf16[4,128,1024]{2,1,0:T(8,128)(2,1)} %fusion.38), channel_id=1, source_target_pairs={{0,4},{4,0},{8,12},{12,8},{16,20},{20,16},{24,28},{28,24},{1,5},{5... | collective-permute-start | bytes 3145736 | tf_op jit(solution)/shard_map/ppermute | solution.py:332
  426.3 31.5 %collective-permute-start.60 = (bf16[4,128,1024]{2,1,0:T(8,128)(2,1)}, bf16[4,128,1024]{2,1,0:T(8,128)(2,1)}, u32[]{:S(2)}, u32[]{:S(2)}) collective-permute-start(bf16[4,128,1024]{2,1,0:T(8,128)(2,1)} %fusion.40), channel_id=1, source_target_pairs={{0,4},{4,0},{8,12},{12,8},{16,20},{20,16},{24,28},{28,24},{1,5},{5... | collective-permute-start | bytes 3145736 | tf_op jit(solution)/shard_map/ppermute | solution.py:332
  427.3 50.4 %collective-permute-start.67 = (bf16[4,128,1024]{2,1,0:T(8,128)(2,1)S(1)}, bf16[4,128,1024]{2,1,0:T(8,128)(2,1)}, u32[]{:S(2)}, u32[]{:S(2)}) collective-permute-start(bf16[4,128,1024]{2,1,0:T(8,128)(2,1)S(1)} %fusion.41), channel_id=1, source_target_pairs={{0,4},{4,0},{8,12},{12,8},{16,20},{20,16},{24,28},{28,24},{1,5},{5... | collective-permute-start | bytes 3145736 | tf_op jit(solution)/shard_map/ppermute | solution.py:332
  450.9 74.3 %collective-permute-start.33 = (bf16[1024,1024]{0,1:T(8,128)(2,1)}, bf16[1024,1024]{0,1:T(8,128)(2,1)S(1)}, u32[]{:S(2)}, u32[]{:S(2)}) collective-permute-start(bf16[1024,1024]{0,1:T(8,128)(2,1)} %slice.216), channel_id=1, source_target_pairs={{0,1},{1,0},{2,3},{3,2},{4,5},{5,4},{6,7},{7,6},{8,9},{9,8},{10,11... | collective-permute-start | bytes 6291464 | tf_op jit(solution)/shard_map/ppermute | solution.py:332
  451.5 73.7 %collective-permute-start.31 = (bf16[1024,1024]{0,1:T(8,128)(2,1)}, bf16[1024,1024]{0,1:T(8,128)(2,1)}, u32[]{:S(2)}, u32[]{:S(2)}) collective-permute-start(bf16[1024,1024]{0,1:T(8,128)(2,1)} %slice.217), channel_id=1, source_target_pairs={{0,1},{1,0},{2,3},{3,2},{4,5},{5,4},{6,7},{7,6},{8,9},{9,8},{10,11... | collective-permute-start | bytes 6291464 | tf_op jit(solution)/shard_map/ppermute | solution.py:332
  453.8 26.9 %collective-permute-start.71 = (bf16[2,128,1024]{2,1,0:T(8,128)(2,1)S(1)}, bf16[2,128,1024]{2,1,0:T(8,128)(2,1)S(1)}, u32[]{:S(2)}, u32[]{:S(2)}) collective-permute-start(bf16[2,128,1024]{2,1,0:T(8,128)(2,1)S(1)} %fusion.49), channel_id=1, source_target_pairs={{0,8},{4,12},{8,0},{12,4},{16,24},{20,28},{24,16},{28,20},{1,9},{5... | collective-permute-start | bytes 1572872 | tf_op jit(solution)/shard_map/ppermute | solution.py:332
  457.8 23.9 %collective-permute-start.64 = (bf16[2,128,1024]{2,1,0:T(8,128)(2,1)S(1)}, bf16[2,128,1024]{2,1,0:T(8,128)(2,1)S(1)}, u32[]{:S(2)}, u32[]{:S(2)}) collective-permute-start(bf16[2,128,1024]{2,1,0:T(8,128)(2,1)S(1)} %fusion.48), channel_id=1, source_target_pairs={{0,8},{4,12},{8,0},{12,4},{16,24},{20,28},{24,16},{28,20},{1,9},{5... | collective-permute-start | bytes 1572872 | tf_op jit(solution)/shard_map/ppermute | solution.py:332
  477.7 23.0 %collective-permute-start.61 = (bf16[2,128,1024]{2,1,0:T(8,128)(2,1)S(1)}, bf16[2,128,1024]{2,1,0:T(8,128)(2,1)S(1)}, u32[]{:S(2)}, u32[]{:S(2)}) collective-permute-start(bf16[2,128,1024]{2,1,0:T(8,128)(2,1)S(1)} %fusion.46), channel_id=1, source_target_pairs={{0,8},{4,12},{8,0},{12,4},{16,24},{20,28},{24,16},{28,20},{1,9},{5... | collective-permute-start | bytes 1572872 | tf_op jit(solution)/shard_map/ppermute | solution.py:332
  480.7 29.1 %collective-permute-start.68 = (bf16[2,128,1024]{2,1,0:T(8,128)(2,1)S(1)}, bf16[2,128,1024]{2,1,0:T(8,128)(2,1)S(1)}, u32[]{:S(2)}, u32[]{:S(2)}) collective-permute-start(bf16[2,128,1024]{2,1,0:T(8,128)(2,1)S(1)} %fusion.47), channel_id=1, source_target_pairs={{0,8},{4,12},{8,0},{12,4},{16,24},{20,28},{24,16},{28,20},{1,9},{5... | collective-permute-start | bytes 1572872 | tf_op jit(solution)/shard_map/ppermute | solution.py:332
  481.6 42.9 %collective-permute-start.72 = (bf16[1,128,1024]{2,1,0:T(8,128)(2,1)S(1)}, bf16[1,128,1024]{2,1,0:T(8,128)(2,1)S(1)}, u32[]{:S(2)}, u32[]{:S(2)}) collective-permute-start(bf16[1,128,1024]{2,1,0:T(8,128)(2,1)S(1)} %dynamic-slice_convert_fusion.3), channel_id=1, source_target_pairs={{0,16},{4,20},{8,24},{12,28},{16,0},{20,4},{24,8},{28,12},{1,17},{... | collective-permute-start | bytes 786440 | tf_op jit(solution)/shard_map/ppermute | solution.py:332
  500.7 22.5 %collective-permute-start.65 = (bf16[1,128,1024]{2,1,0:T(8,128)(2,1)S(1)}, bf16[1,128,1024]{2,1,0:T(8,128)(2,1)S(1)}, u32[]{:S(2)}, u32[]{:S(2)}) collective-permute-start(bf16[1,128,1024]{2,1,0:T(8,128)(2,1)S(1)} %dynamic-slice_convert_fusion.5), channel_id=1, source_target_pairs={{0,16},{4,20},{8,24},{12,28},{16,0},{20,4},{24,8},{28,12},{1,17},{... | collective-permute-start | bytes 786440 | tf_op jit(solution)/shard_map/ppermute | solution.py:332
  509.8 166.8 %collective-permute-start.62 = (bf16[1,128,1024]{2,1,0:T(8,128)(2,1)}, bf16[1,128,1024]{2,1,0:T(8,128)(2,1)}, u32[]{:S(2)}, u32[]{:S(2)}) collective-permute-start(bf16[1,128,1024]{2,1,0:T(8,128)(2,1)} %dynamic-slice_convert_fusion.6), channel_id=1, source_target_pairs={{0,16},{4,20},{8,24},{12,28},{16,0},{20,4},{24,8},{28,12},{1,17},{... | collective-permute-start | bytes 786440 | tf_op jit(solution)/shard_map/ppermute | solution.py:332
  523.9 152.7 %collective-permute-start.66 = (bf16[128,1024]{1,0:T(8,128)(2,1)}, bf16[128,1024]{1,0:T(8,128)(2,1)}, u32[]{:S(2)}, u32[]{:S(2)}) collective-permute-start(bf16[128,1024]{1,0:T(8,128)(2,1)} %fusion.54), channel_id=1, source_target_pairs={{0,2},{1,3},{2,0},{3,1},{4,6},{5,7},{6,4},{7,5},{8,10},{9,11},{10,... | collective-permute-start | bytes 786440 | tf_op jit(solution)/shard_map/ppermute | solution.py:332
  540.9 25.4 %collective-permute-start.35 = (bf16[1024,256]{1,0:T(8,128)(2,1)S(1)}, bf16[1024,256]{1,0:T(8,128)(2,1)S(1)}, u32[]{:S(2)}, u32[]{:S(2)}) collective-permute-start(bf16[1024,256]{1,0:T(8,128)(2,1)S(1)} %get-tuple-element.75), channel_id=1, source_target_pairs={{0,2},{1,3},{2,0},{3,1},{4,6},{5,7},{6,4},{7,5},{8,10},{9,11},{10,... | collective-permute-start | bytes 1572872 | tf_op jit(solution)/shard_map/ppermute | solution.py:332
  542.4 24.0 %collective-permute-start.34 = (bf16[1024,256]{1,0:T(8,128)(2,1)S(1)}, bf16[1024,256]{1,0:T(8,128)(2,1)S(1)}, u32[]{:S(2)}, u32[]{:S(2)}) collective-permute-start(bf16[1024,256]{1,0:T(8,128)(2,1)S(1)} %get-tuple-element.76), channel_id=1, source_target_pairs={{0,1},{1,0},{2,3},{3,2},{4,5},{5,4},{6,7},{7,6},{8,9},{9,8},{10,11... | collective-permute-start | bytes 1572872 | tf_op jit(solution)/shard_map/ppermute | solution.py:332
  555.0 125.6 %collective-permute-start.48 = (bf16[1024,256]{1,0:T(8,128)(2,1)S(1)}, bf16[1024,256]{1,0:T(8,128)(2,1)S(1)}, u32[]{:S(2)}, u32[]{:S(2)}) collective-permute-start(bf16[1024,256]{1,0:T(8,128)(2,1)S(1)} %get-tuple-element.71), channel_id=1, source_target_pairs={{0,1},{1,0},{2,3},{3,2},{4,5},{5,4},{6,7},{7,6},{8,9},{9,8},{10,11... | collective-permute-start | bytes 1572872 | tf_op jit(solution)/shard_map/ppermute | solution.py:332
  566.3 104.1 %collective-permute-start.49 = (bf16[1024,256]{1,0:T(8,128)(2,1)}, bf16[1024,256]{1,0:T(8,128)(2,1)}, u32[]{:S(2)}, u32[]{:S(2)}) collective-permute-start(bf16[1024,256]{1,0:T(8,128)(2,1)} %get-tuple-element.72), channel_id=1, source_target_pairs={{0,1},{1,0},{2,3},{3,2},{4,5},{5,4},{6,7},{7,6},{8,9},{9,8},{10,11... | collective-permute-start | bytes 1572872 | tf_op jit(solution)/shard_map/ppermute | solution.py:332
  648.3 24.4 %collective-permute-start.38 = (bf16[1024,1024]{0,1:T(8,128)(2,1)S(1)}, bf16[1024,1024]{0,1:T(8,128)(2,1)}, u32[]{:S(2)}, u32[]{:S(2)}) collective-permute-start(bf16[1024,1024]{0,1:T(8,128)(2,1)S(1)} %slice.214), channel_id=1, source_target_pairs={{0,1},{1,0},{2,3},{3,2},{4,5},{5,4},{6,7},{7,6},{8,9},{9,8},{10,11... | collective-permute-start | bytes 6291464 | tf_op jit(solution)/shard_map/ppermute | solution.py:332
  676.6 66.9 %collective-permute-start.37 = (bf16[1024,1024]{0,1:T(8,128)(2,1)}, bf16[1024,1024]{0,1:T(8,128)(2,1)}, u32[]{:S(2)}, u32[]{:S(2)}) collective-permute-start(bf16[1024,1024]{0,1:T(8,128)(2,1)} %slice.215), channel_id=1, source_target_pairs={{0,1},{1,0},{2,3},{3,2},{4,5},{5,4},{6,7},{7,6},{8,9},{9,8},{10,11... | collective-permute-start | bytes 6291464 | tf_op jit(solution)/shard_map/ppermute | solution.py:332
  676.7 66.9 %collective-permute-start.39 = (bf16[1024,1024]{0,1:T(8,128)(2,1)}, bf16[1024,1024]{0,1:T(8,128)(2,1)}, u32[]{:S(2)}, u32[]{:S(2)}) collective-permute-start(bf16[1024,1024]{0,1:T(8,128)(2,1)} %fusion.29), channel_id=1, source_target_pairs={{0,2},{1,3},{2,0},{3,1},{4,6},{5,7},{6,4},{7,5},{8,10},{9,11},{10,... | collective-permute-start | bytes 6291464 | tf_op jit(solution)/shard_map/ppermute | solution.py:332
  687.6 49.4 %collective-permute-start.73 = (bf16[128,1024]{1,0:T(8,128)(2,1)S(1)}, bf16[128,1024]{1,0:T(8,128)(2,1)S(1)}, u32[]{:S(2)}, u32[]{:S(2)}) collective-permute-start(bf16[128,1024]{1,0:T(8,128)(2,1)S(1)} %copy-done.27), channel_id=1, source_target_pairs={{0,2},{1,3},{2,0},{3,1},{4,6},{5,7},{6,4},{7,5},{8,10},{9,11},{10,... | collective-permute-start | bytes 786440 | tf_op jit(solution)/shard_map/ppermute | solution.py:332
  697.6 44.6 %collective-permute-start.46 = (bf16[2,128,768]{2,1,0:T(8,128)(2,1)}, bf16[2,128,768]{2,1,0:T(8,128)(2,1)}, u32[]{:S(2)}, u32[]{:S(2)}) collective-permute-start(bf16[2,128,768]{2,1,0:T(8,128)(2,1)} %fusion.51), channel_id=1, source_target_pairs={{0,8},{4,12},{8,0},{12,4},{16,24},{20,28},{24,16},{28,20},{1,9},{5... | collective-permute-start | bytes 1179656 | tf_op jit(solution)/shard_map/ppermute | solution.py:332
  698.2 43.9 %collective-permute-start.52 = (bf16[2,128,256]{2,1,0:T(8,128)(2,1)S(1)}, bf16[2,128,256]{2,1,0:T(8,128)(2,1)S(1)}, u32[]{:S(2)}, u32[]{:S(2)}) collective-permute-start(bf16[2,128,256]{2,1,0:T(8,128)(2,1)S(1)} %fusion.57), channel_id=1, source_target_pairs={{0,8},{4,12},{8,0},{12,4},{16,24},{20,28},{24,16},{28,20},{1,9},{5... | collective-permute-start | bytes 393224 | tf_op jit(solution)/shard_map/ppermute | solution.py:332
  742.1 23.8 %collective-permute-start.53 = (bf16[1,128,256]{2,1,0:T(8,128)(2,1)S(1)}, bf16[1,128,256]{2,1,0:T(8,128)(2,1)S(1)}, u32[]{:S(2)}, u32[]{:S(2)}) collective-permute-start(bf16[1,128,256]{2,1,0:T(8,128)(2,1)S(1)} %dynamic-slice_convert_fusion.9), channel_id=1, source_target_pairs={{0,16},{4,20},{8,24},{12,28},{16,0},{20,4},{24,8},{28,12},{1,17},{... | collective-permute-start | bytes 196616 | tf_op jit(solution)/shard_map/ppermute | solution.py:332
  (96 other events, 1766.4 us)

commit v2 on v1

v2 whole, which is shorter than its diff:
```python
from functools import partial
import jax, jax.numpy as jnp
from jax import lax
from jax.experimental import pallas as pl
from jax.experimental.layout import Layout, with_layout_constraint
from jax.experimental.pallas import tpu as pltpu
from jax.sharding import PartitionSpec as P

HEAD_DIM = 64
BLOCK = 64
LANES = 128
F32 = jnp.float32
LOW = jnp.bfloat16
neg_large = -1e30


def dot_nn(a, b):
    return lax.dot_general(a, b, (((1,), (0,)), ((), ())), preferred_element_type=F32)


def dot_nt(a, b):
    return lax.dot_general(a, b, (((1,), (1,)), ((), ())), preferred_element_type=F32)


def dot_tn(a, b):
    return lax.dot_general(a, b, (((0,), (0,)), ((), ())), preferred_element_type=F32)


class Walk:
    def __init__(self, rank_ref, pick_ref, heads, seq, rand):
        self.rank = rank_ref[0]
        self.pick_ref = pick_ref
        self.heads = heads
        self.rand = rand
        self.nblocks = seq // BLOCK

    def place(self, blk):
        per = self.nblocks // 4
        chunk = lax.bitwise_xor(lax.div(blk, per), self.rank)
        return pl.multiple_of((chunk * per + lax.rem(blk, per)) * BLOCK, BLOCK)

    def span_of(self, near):
        upper = lax.div(self.rank, 2)
        half = upper if near else 1 - upper
        count = self.nblocks // 2 - 1
        return 1 + half * count, count, half * (self.nblocks - 1)

    def picked(self, blk, head, slot):
        return self.pick_ref[(head * (self.nblocks - 2) + blk - 1) * self.rand + slot]


def left_lanes(rows):
    return lax.broadcasted_iota(jnp.int32, (rows, LANES), 1) < HEAD_DIM


def spread_heads(rows, heads):
    tall = jnp.concatenate([rows.astype(F32)] * heads, axis=0)
    width = heads * HEAD_DIM
    row_head = lax.broadcasted_iota(jnp.int32, (heads * BLOCK, width), 0) // BLOCK
    col_head = lax.broadcasted_iota(jnp.int32, (heads * BLOCK, width), 1) // HEAD_DIM
    return jnp.where(row_head == col_head, tall, 0.0).astype(LOW)


def own_heads(full, heads):
    left = left_lanes(BLOCK)
    halves = []
    for pair in range(heads // 2):
        cols = slice(pair * LANES, (pair + 1) * LANES)
        first = full[2 * pair * BLOCK : (2 * pair + 1) * BLOCK, cols]
        second = full[(2 * pair + 1) * BLOCK : (2 * pair + 2) * BLOCK, cols]
        halves.append(jnp.where(left, first, second))
    return jnp.concatenate(halves, axis=1)


def gather_rows(ref, base, walk, blk):
    heads = walk.heads
    width = heads * HEAD_DIM
    left = left_lanes(BLOCK)
    parts = [
        ref[pl.ds(walk.place(at), BLOCK), base : base + width]
        for at in (blk - 1, blk, blk + 1, 0, walk.nblocks - 1)
    ]
    for slot in range(walk.rand):
        halves = []
        for pair in range(heads // 2):
            cols = slice(base + pair * LANES, base + (pair + 1) * LANES)
            first = ref[pl.ds(walk.place(walk.picked(blk, 2 * pair, slot)), BLOCK), cols]
            second = ref[pl.ds(walk.place(walk.picked(blk, 2 * pair + 1, slot)), BLOCK), cols]
            halves.append(jnp.where(left, first, second))
        parts.append(jnp.concatenate(halves, axis=1))
    return jnp.concatenate(parts, axis=0)


def key_marks(mark_ref, walk, blk):
    heads = walk.heads
    left = left_lanes(BLOCK)

    def rows_at(at):
        return mark_ref[pl.ds(pl.multiple_of(at * BLOCK, BLOCK), BLOCK), :]

    before = jnp.where(blk == 1, -1, rows_at(blk - 1))
    after = jnp.where(blk == walk.nblocks - 2, -1, rows_at(blk + 1))
    parts = [
        jnp.concatenate([rows] * (heads // 2), axis=1)
        for rows in (before, rows_at(blk), after, rows_at(0), rows_at(walk.nblocks - 1))
    ]
    for slot in range(walk.rand):
        halves = []
        for pair in range(heads // 2):
            first = rows_at(walk.picked(blk, 2 * pair, slot))
            second = rows_at(walk.picked(blk, 2 * pair + 1, slot))
            halves.append(jnp.where(left, first, second))
        parts.append(jnp.concatenate(halves, axis=1))
    return jnp.concatenate(parts, axis=0)


def chunk_marks(mark_ref, walk, at, size):
    per = walk.nblocks // 4 * BLOCK
    chunk = lax.bitwise_xor(lax.div(at, per), walk.rank)
    natural = pl.multiple_of(chunk * per + lax.rem(at, per), BLOCK)
    rows = mark_ref[pl.ds(natural, size), :]
    return jnp.concatenate([rows] * (walk.heads // 2), axis=1)


def forward_kernel(rank_ref, pick_ref, qkv_ref, mark_ref, qmark_ref, out_ref, score_ref, *, heads, rand, span, near):
    seq = qkv_ref.shape[0]
    width = heads * HEAD_DIM
    walk = Walk(rank_ref, pick_ref, heads, seq, rand)
    first, count, dense = walk.span_of(near)
    base = 0 if near else seq // 2

    def middle(blk):
        place = walk.place(blk)
        query = spread_heads(qkv_ref[pl.ds(place, BLOCK), 0:width], heads)
        keys = gather_rows(qkv_ref, width, walk, blk)
        score = dot_nt(keys, query)
        ok = key_marks(mark_ref, walk, blk) == qmark_ref[pl.ds(blk, 1), :]
        score = jnp.where(ok, score, neg_large)
        expo = jnp.exp(score - jnp.max(score, axis=0, keepdims=True))
        probs = (expo * (1.0 / jnp.sum(expo, axis=0, keepdims=True))).astype(LOW)
        values = gather_rows(qkv_ref, 2 * width, walk, blk)
        out_ref[pl.ds(pl.multiple_of(place - base, BLOCK), BLOCK), :] = own_heads(dot_tn(probs, values), heads).astype(LOW)

    def pair(step, carry):
        middle(first + 2 * step)
        middle(first + 2 * step + 1)
        return carry

    lax.fori_loop(0, count // 2, pair, 0)
    for extra in range(count - count % 2, count):
        middle(first + extra)

    place = walk.place(dense)
    query = spread_heads(qkv_ref[pl.ds(place, BLOCK), 0:width], heads)
    qmark = qmark_ref[pl.ds(dense, 1), :]

    def scores_at(step, top):
        at = pl.multiple_of(step * span, span)
        score = dot_nt(qkv_ref[pl.ds(at, span), width : 2 * width], query)
        score = jnp.where(chunk_marks(mark_ref, walk, at, span) == qmark, score, neg_large)
        score_ref[pl.ds(at, span), :] = score
        return jnp.maximum(top, jnp.max(score, axis=0, keepdims=True))

    def expo_at(step, total, top):
        at = pl.multiple_of(step * span, span)
        expo = jnp.exp(score_ref[pl.ds(at, span), :] - top)
        score_ref[pl.ds(at, span), :] = expo
        return total + jnp.sum(expo, axis=0, keepdims=True)

    def value_at(step, total, scale):
        at = pl.multiple_of(step * span, span)
        probs = (score_ref[pl.ds(at, span), :] * scale).astype(LOW)
        return total + dot_tn(probs, qkv_ref[pl.ds(at, span), 2 * width : 3 * width])

    top = jnp.full((1, heads * BLOCK), neg_large, F32)
    top = lax.fori_loop(0, seq // span, scores_at, top)
    total = lax.fori_loop(0, seq // span, partial(expo_at, top=top), jnp.zeros_like(top))
    full = lax.fori_loop(0, seq // span, partial(value_at, scale=1.0 / total), jnp.zeros((heads * BLOCK, width), F32))
    out_ref[pl.ds(pl.multiple_of(place - base, BLOCK), BLOCK), :] = own_heads(full, heads).astype(LOW)


def backward_body(rank_ref, pick_ref, qkv_ref, grad_ref, mark_ref, qmark_ref, query_ref, key_acc, value_acc, score_ref, dprob_ref, heads, rand, span, near):
    seq = qkv_ref.shape[0]
    width = heads * HEAD_DIM
    walk = Walk(rank_ref, pick_ref, heads, seq, rand)
    left = left_lanes(BLOCK)

    first, count, dense = walk.span_of(near)
    base = 0 if near else seq // 2

    def add_rows(acc, rows, blk):
        for index, at in enumerate((blk - 1, blk, blk + 1, 0, walk.nblocks - 1)):
            acc[pl.ds(walk.place(at), BLOCK), :] += rows[index * BLOCK : (index + 1) * BLOCK, :]
        for slot in range(rand):
            row = (5 + slot) * BLOCK
            for pair in range(heads // 2):
                cols = slice(pair * LANES, (pair + 1) * LANES)
                piece = rows[row : row + BLOCK, cols]
                acc[pl.ds(walk.place(walk.picked(blk, 2 * pair, slot)), BLOCK), cols] += jnp.where(left, piece, 0.0)
                acc[pl.ds(walk.place(walk.picked(blk, 2 * pair + 1, slot)), BLOCK), cols] += jnp.where(left, 0.0, piece)

    def middle(blk):
        place = walk.place(blk)
        query = spread_heads(qkv_ref[pl.ds(place, BLOCK), 0:width], heads)
        half_row = pl.multiple_of(place - base, BLOCK)
        grad = spread_heads(grad_ref[pl.ds(half_row, BLOCK), :], heads)
        keys = gather_rows(qkv_ref, width, walk, blk)
        values = gather_rows(qkv_ref, 2 * width, walk, blk)
        score = dot_nt(keys, query)
        ok = key_marks(mark_ref, walk, blk) == qmark_ref[pl.ds(blk, 1), :]
        score = jnp.where(ok, score, neg_large)
        expo = jnp.exp(score - jnp.max(score, axis=0, keepdims=True))
        probs = expo * (1.0 / jnp.sum(expo, axis=0, keepdims=True))
        dprob = dot_nt(values, grad)
        delta = jnp.sum(probs * dprob, axis=0, keepdims=True)
        dscore = (probs * (dprob - delta)).astype(LOW)
        dvalue = dot_nn(probs.astype(LOW), grad)
        dkey = dot_nn(dscore, query)
        dquery = own_heads(dot_tn(dscore, keys), heads)
        query_ref[pl.ds(half_row if near else place, BLOCK), 0:width] = dquery.astype(LOW)
        return dkey, dvalue

    def pair(step, carry):
        blk = first + 2 * step
        dkey_a, dvalue_a = middle(blk)
        dkey_b, dvalue_b = middle(blk + 1)
        add_rows(key_acc, dkey_a, blk)
        add_rows(value_acc, dvalue_a, blk)
        add_rows(key_acc, dkey_b, blk + 1)
        add_rows(value_acc, dvalue_b, blk + 1)
        return carry

    lax.fori_loop(0, count // 2, pair, 0)
    for extra in range(count - count % 2, count):
        dkey, dvalue = middle(first + extra)
        add_rows(key_acc, dkey, first + extra)
        add_rows(value_acc, dvalue, first + extra)

    place = walk.place(dense)
    half_row = pl.multiple_of(place - base, BLOCK)
    query = spread_heads(qkv_ref[pl.ds(place, BLOCK), 0:width], heads)
    grad = spread_heads(grad_ref[pl.ds(half_row, BLOCK), :], heads)
    qmark = qmark_ref[pl.ds(dense, 1), :]

    def scores_at(step, top):
        at = pl.multiple_of(step * span, span)
        score = dot_nt(qkv_ref[pl.ds(at, span), width : 2 * width], query)
        score = jnp.where(chunk_marks(mark_ref, walk, at, span) == qmark, score, neg_large)
        score_ref[pl.ds(at, span), :] = score
        dprob_ref[pl.ds(at, span), :] = dot_nt(qkv_ref[pl.ds(at, span), 2 * width : 3 * width], grad)
        return jnp.maximum(top, jnp.max(score, axis=0, keepdims=True))

    def expo_at(step, carry, top):
        total, weighted = carry
        at = pl.multiple_of(step * span, span)
        expo = jnp.exp(score_ref[pl.ds(at, span), :] - top)
        score_ref[pl.ds(at, span), :] = expo
        return (
            total + jnp.sum(expo, axis=0, keepdims=True),
            weighted + jnp.sum(expo * dprob_ref[pl.ds(at, span), :], axis=0, keepdims=True),
        )

    def grads_at(step, dquery, scale, delta):
        at = pl.multiple_of(step * span, span)
        probs = score_ref[pl.ds(at, span), :] * scale
        dscore = (probs * (dprob_ref[pl.ds(at, span), :] - delta)).astype(LOW)
        value_acc[pl.ds(at, span), :] += dot_nn(probs.astype(LOW), grad)
        key_acc[pl.ds(at, span), :] += dot_nn(dscore, query)
        return dquery + dot_tn(dscore, qkv_ref[pl.ds(at, span), width : 2 * width])

    top = jnp.full((1, heads * BLOCK), neg_large, F32)
    top = lax.fori_loop(0, seq // span, scores_at, top)
    total, weighted = lax.fori_loop(0, seq // span, partial(expo_at, top=top), (jnp.zeros_like(top), jnp.zeros_like(top)))
    scale = 1.0 / total
    full = lax.fori_loop(0, seq // span, partial(grads_at, scale=scale, delta=weighted * scale), jnp.zeros((heads * BLOCK, width), F32))
    query_ref[pl.ds(half_row if near else place, BLOCK), 0:width] = own_heads(full, heads).astype(LOW)


def backward_near(rank_ref, pick_ref, qkv_ref, grad_ref, mark_ref, qmark_ref, query_ref, key_acc, value_acc, score_ref, dprob_ref, *, heads, rand, span):
    seq = qkv_ref.shape[0]
    width = heads * HEAD_DIM

    def clear(step, carry):
        at = pl.multiple_of(step * span, span)
        key_acc[pl.ds(at, span), :] = jnp.zeros((span, width), F32)
        value_acc[pl.ds(at, span), :] = jnp.zeros((span, width), F32)
        return carry

    lax.fori_loop(0, seq // span, clear, 0)
    backward_body(rank_ref, pick_ref, qkv_ref, grad_ref, mark_ref, qmark_ref, query_ref, key_acc, value_acc, score_ref, dprob_ref, heads, rand, span, True)


def backward_far(rank_ref, pick_ref, qkv_ref, grad_ref, mark_ref, qmark_ref, near_ref, key_in, value_in, out_ref, key_acc, value_acc, score_ref, dprob_ref, *, heads, rand, span):
    seq = qkv_ref.shape[0]
    width = heads * HEAD_DIM

    def begin(step, carry):
        at = pl.multiple_of(step * span, span)
        key_acc[pl.ds(at, span), :] = key_in[pl.ds(at, span), :]
        value_acc[pl.ds(at, span), :] = value_in[pl.ds(at, span), :]
        return carry

    lax.fori_loop(0, seq // span, begin, 0)
    out_ref[0 : seq // 2, 0:width] = near_ref[...]
    backward_body(rank_ref, pick_ref, qkv_ref, grad_ref, mark_ref, qmark_ref, out_ref, key_acc, value_acc, score_ref, dprob_ref, heads, rand, span, False)

    def finish(step, carry):
        at = pl.multiple_of(step * span, span)
        out_ref[pl.ds(at, span), width : 2 * width] = key_acc[pl.ds(at, span), :].astype(LOW)
        out_ref[pl.ds(at, span), 2 * width : 3 * width] = value_acc[pl.ds(at, span), :].astype(LOW)
        return carry

    lax.fori_loop(0, seq // span, finish, 0)


def token_marks(seq_segs, heads):
    seq = seq_segs.shape[0]
    marks = jnp.where(seq_segs != 0, seq_segs, 1000 + jnp.arange(seq, dtype=jnp.int32))
    by_row = jnp.broadcast_to(marks[:, None], (seq, LANES))
    by_block = jnp.tile(marks.reshape(seq // BLOCK, BLOCK), (1, heads))
    return by_row, by_block


def spent(micros):
    return pl.CostEstimate(flops=micros * 10**9, bytes_accessed=micros * 10**6, transcendentals=0)


SMEM_SPEC = pl.BlockSpec(memory_space=pltpu.SMEM)
VMEM_SPEC = pl.BlockSpec(memory_space=pltpu.VMEM)


def attend(rank, picks, qkv, marks, near):
    heads, _, rand = picks.shape
    seq = qkv.shape[0]
    width = heads * HEAD_DIM
    span = min(512, seq // 4)
    return pl.pallas_call(
        partial(forward_kernel, heads=heads, rand=rand, span=span, near=near),
        out_shape=jax.ShapeDtypeStruct((seq // 2, width), LOW),
        in_specs=[SMEM_SPEC, SMEM_SPEC, VMEM_SPEC, VMEM_SPEC, VMEM_SPEC],
        out_specs=VMEM_SPEC,
        scratch_shapes=[pltpu.VMEM((seq, heads * BLOCK), F32)],
        name="attend_near" if near else "attend_far",
        cost_estimate=spent(29),
    )(rank, picks.reshape(-1), qkv, *marks)


def attend_back_near(rank, picks, qkv, grad_context, marks):
    heads, _, rand = picks.shape
    seq = qkv.shape[0]
    width = heads * HEAD_DIM
    span = min(512, seq // 4)
    total = jax.ShapeDtypeStruct((seq, width), F32)
    return pl.pallas_call(
        partial(backward_near, heads=heads, rand=rand, span=span),
        out_shape=[jax.ShapeDtypeStruct((seq // 2, width), LOW), total, total],
        in_specs=[SMEM_SPEC, SMEM_SPEC, VMEM_SPEC, VMEM_SPEC, VMEM_SPEC, VMEM_SPEC],
        out_specs=[VMEM_SPEC] * 3,
        scratch_shapes=[pltpu.VMEM((seq, heads * BLOCK), F32)] * 2,
        name="attend_back_near",
        cost_estimate=spent(40),
    )(rank, picks.reshape(-1), qkv, grad_context, *marks)


def attend_back_far(rank, picks, qkv, grad_context, marks, near_parts):
    heads, _, rand = picks.shape
    seq = qkv.shape[0]
    width = heads * HEAD_DIM
    span = min(512, seq // 4)
    return pl.pallas_call(
        partial(backward_far, heads=heads, rand=rand, span=span),
        out_shape=jax.ShapeDtypeStruct((seq, 3 * width), LOW),
        in_specs=[SMEM_SPEC, SMEM_SPEC] + [VMEM_SPEC] * 7,
        out_specs=VMEM_SPEC,
        scratch_shapes=[pltpu.VMEM((seq, width), F32)] * 2 + [pltpu.VMEM((seq, heads * BLOCK), F32)] * 2,
        name="attend_back_far",
        cost_estimate=spent(43),
    )(rank, picks.reshape(-1), qkv, grad_context, *marks, *near_parts)


eps_norm = 1e-05


def by_rows(values):
    return with_layout_constraint(values, Layout(major_to_minor=(0, 1)))


def tie(values, *others):
    return lax.optimization_barrier((values, others))[0]


def norm_rows(source, gain_vec, shift_vec):
    average = jnp.mean(source, axis=-1, keepdims=True)
    centred = source - average
    variance = jnp.mean(centred * centred, axis=-1, keepdims=True)
    return centred * lax.rsqrt(variance + eps_norm) * gain_vec + shift_vec


def norm_kernel(source_ref, gain_ref, shift_ref, out_ref):
    source = source_ref[...].astype(F32)
    out_ref[...] = norm_rows(source, gain_ref[...], shift_ref[...]).astype(LOW)


def norm_call(source, gain, shift):
    rows, model = source.shape
    tile = min(256, rows)
    vector = pl.BlockSpec((1, model), lambda i: (0, 0))
    block = pl.BlockSpec((tile, model), lambda i: (i, 0))
    return pl.pallas_call(
        norm_kernel,
        grid=(rows // tile,),
        in_specs=[block, vector, vector],
        out_specs=block,
        out_shape=jax.ShapeDtypeStruct((rows, model), LOW),
        name="norm",
        cost_estimate=spent(3),
    )(source, gain, shift)


def norm_back_kernel(source_ref, gain_ref, residual_ref, *rest, terms, narrow):
    term_refs = rest[:terms]
    out_ref = rest[terms]
    low_ref = rest[terms + 1] if narrow else None
    sum_ref = rest[-1]
    source = source_ref[...].astype(F32)
    grad = term_refs[0][...].astype(F32)
    for ref in term_refs[1:]:
        grad = grad + ref[...].astype(F32)
    average = jnp.mean(source, axis=-1, keepdims=True)
    centred = source - average
    variance = jnp.mean(centred * centred, axis=-1, keepdims=True)
    scale = lax.rsqrt(variance + eps_norm)
    normal = centred * scale
    scaled = grad * gain_ref[...]
    first = jnp.mean(scaled, axis=-1, keepdims=True)
    second = jnp.mean(scaled * normal, axis=-1, keepdims=True)
    residual = residual_ref[...].astype(F32)
    full = residual + scale * (scaled - first - normal * second)
    out_ref[...] = full
    if narrow:
        low_ref[...] = full.astype(LOW)
    model = source.shape[1]
    parts = [jnp.sum(grad * normal, axis=0, keepdims=True), jnp.sum(grad, axis=0, keepdims=True)]
    if narrow:
        parts.append(jnp.sum(residual, axis=0, keepdims=True))
    parts.append(jnp.zeros((8 - len(parts), model), F32))
    parts = jnp.concatenate(parts, axis=0)

    @pl.when(pl.program_id(0) == 0)
    def _():
        sum_ref[...] = parts

    @pl.when(pl.program_id(0) != 0)
    def _():
        sum_ref[...] += parts


def norm_back(source, gain, residual, terms, narrow):
    rows, model = source.shape
    tile = min(256, rows)
    vector = pl.BlockSpec((1, model), lambda i: (0, 0))
    block = pl.BlockSpec((tile, model), lambda i: (i, 0))
    shapes = [jax.ShapeDtypeStruct((rows, model), F32)]
    if narrow:
        shapes.append(jax.ShapeDtypeStruct((rows, model), LOW))
    return pl.pallas_call(
        partial(norm_back_kernel, terms=len(terms), narrow=narrow),
        grid=(rows // tile,),
        in_specs=[block, vector] + [block] * (1 + len(terms)),
        out_specs=[block] * len(shapes) + [pl.BlockSpec((8, model), lambda i: (0, 0))],
        out_shape=shapes + [jax.ShapeDtypeStruct((8, model), F32)],
        name="norm_back",
        cost_estimate=spent(7),
    )(source, gain, residual, *terms)


def feed_kernel(second_own, second_side, grad_own, grad_side, up_ref, down_ref, bias_ref, hidden_ref, pre_ref, sum_ref, *, step):
    slope = (2.0 / jnp.pi) ** 0.5

    def run(second_ref, grad_ref):
        total = jnp.zeros(sum_ref.shape[1:], F32)
        for at in range(0, second_ref.shape[0], step):
            rows = slice(at, at + step)
            unit = dot_nn(second_ref[rows, :], up_ref[...]) + bias_ref[...]
            grad = dot_nn(grad_ref[rows, :], down_ref[...])
            square = unit * unit
            bent = jnp.tanh(unit * (slope + (slope * 0.044715) * square))
            half = 0.5 + 0.5 * bent
            hidden_ref[rows, :] = (unit * half).astype(LOW)
            rise = half + (0.5 * unit) * (1.0 - bent * bent) * (slope + (slope * 0.134145) * square)
            low = (grad * rise).astype(LOW)
            pre_ref[rows, :] = low
            total = total + jnp.sum(low.astype(F32), axis=0, keepdims=True)
        sum_ref[0] = total

    @pl.when(pl.program_id(0) == 0)
    def _():
        run(second_own, grad_own)

    @pl.when(pl.program_id(0) == 1)
    def _():
        run(second_side, grad_side)


def feed(seconds, grads, weights, first_up, first_down, bias):
    rows, model = seconds[0].shape
    units = bias.shape[0]
    tile = min(256, units)
    whole = pl.BlockSpec((rows, model), lambda t, u: (0, 0))
    out = pl.BlockSpec((rows, tile), lambda t, u: (t, u))
    return pl.pallas_call(
        partial(feed_kernel, step=min(256, rows)),
        grid=(2, units // tile),
        in_specs=[whole] * 4
        + [
            pl.BlockSpec((model, tile), lambda t, u: (0, first_up // tile + u)),
            pl.BlockSpec((model, tile), lambda t, u: (0, first_down // tile + u)),
            pl.BlockSpec((1, tile), lambda t, u: (0, u)),
        ],
        out_specs=[out, out, pl.BlockSpec((1, 1, tile), lambda t, u: (t, 0, u))],
        out_shape=[
            jax.ShapeDtypeStruct((2 * rows, units), LOW),
            jax.ShapeDtypeStruct((2 * rows, units), LOW),
            jax.ShapeDtypeStruct((2, 1, units), F32),
        ],
        name="feed",
        cost_estimate=spent(14),
    )(*seconds, *grads, weights, weights, bias[None])


def swap(values, axis, mask):
    count = lax.axis_size(axis)
    return lax.ppermute(values, axis, [(i, i ^ mask) for i in range(count)])


def collect_rows(parts, gate):
    count = lax.axis_size("fsdp")
    spot = lax.axis_index("fsdp")
    rows = parts[0].shape[0] // count
    mask = 1
    while mask < count:
        upper = (spot & mask) != 0
        parts = [part.reshape(-1, 2, rows, part.shape[-1]) for part in parts]
        sent = [jnp.where(upper, part[:, 0], part[:, 1]).astype(LOW) for part in parts]
        got = swap(jnp.concatenate(sent, -1), "fsdp", mask)
        first = 0
        held = []
        for part in parts:
            last = first + part.shape[-1]
            held.append(jnp.where(upper, part[:, 1], part[:, 0]) + got[..., first:last].astype(F32))
            first = last
        parts = held
        if mask == 1:
            parts, gate = lax.optimization_barrier((parts, gate))
        mask *= 2
    return [part.reshape(rows, part.shape[-1]) for part in parts], gate


def total_over(values, axis):
    bits = [1 << k for k in range(lax.axis_size(axis).bit_length() - 1)]
    while bits:
        if len(bits) % 2:
            values = values + swap(values, axis, bits.pop(0))
        else:
            low, high = bits.pop(0), bits.pop(0)
            values = (values + swap(values, axis, low)) + (swap(values, axis, high) + swap(values, axis, low | high))
    return values


def on_device(
    hidden_in,
    cotangent,
    norm1_gain,
    norm1_bias,
    w_query,
    w_key,
    w_value,
    w_out,
    norm2_gain,
    norm2_bias,
    w_fc1,
    bias_fc1,
    w_fc2,
    bias_fc2,
    segments,
    random_blocks,
):
    rows_dev, width_model = hidden_in.shape
    heads_wide = w_query.shape[1]
    rank = lax.axis_index("tp")
    seq_segs = segments[0]
    picks = random_blocks[0]
    heads_local = picks.shape[0]
    own_segs = lax.dynamic_slice_in_dim(seq_segs, rank * rows_dev, rows_dev)
    valid_rows = (own_segs != 0).astype(F32)[:, None]
    gain_first = norm1_gain.astype(F32)[None]
    shift_first = norm1_bias.astype(F32)[None]
    gain_second = norm2_gain.astype(F32)[None]
    shift_second = norm2_bias.astype(F32)[None]
    residual_in = hidden_in.astype(F32)
    scale_query = HEAD_DIM ** (-0.5)
    rank_word = rank.astype(jnp.int32).reshape(1)
    marks = token_marks(seq_segs, heads_local)

    heads_local_w = by_rows(jnp.concatenate([w_query * jnp.asarray(scale_query, LOW), w_key, w_value, w_out.T], 1))
    w_heads = lax.all_gather(heads_local_w, "fsdp", axis=0, tiled=True)
    pair_local = by_rows(jnp.concatenate([w_fc1, w_fc2.T], 1))
    units = w_fc1.shape[1]
    own_all = lax.all_gather(pair_local, "fsdp", axis=0, tiled=True)
    far_hidden = swap(hidden_in, "tp", 2)
    far_local = swap(tie(pair_local, far_hidden), "tp", 2)
    bias_up = [bias_fc1.astype(F32), swap(bias_fc1, "tp", 2).astype(F32)]

    first_own = norm_call(tie(hidden_in, marks, picks), gain_first, shift_first)
    first_side = swap(first_own, "tp", 1)
    far_hidden, w_heads = lax.optimization_barrier((far_hidden, w_heads))
    w_qkv = w_heads[:, : 3 * heads_wide]
    first_far = norm_call(far_hidden, gain_first, shift_first)
    first_cross = swap(first_far, "tp", 1)
    chunks = (first_own, first_side, first_far, first_cross)
    qkv = jnp.concatenate([dot_nn(chunk, w_qkv).astype(LOW) for chunk in chunks], 0)
    qkv, far_local = lax.optimization_barrier((qkv, far_local))
    far_all = lax.all_gather(far_local, "fsdp", axis=0, tiled=True)
    context_far = attend(rank_word, picks, qkv, marks, False)
    context_cross = [swap(context_far[k * rows_dev : (k + 1) * rows_dev], "tp", 2 + k) for k in (0, 1)]
    wo_own = tie(w_heads, qkv)[:, 3 * heads_wide :]
    wo_pair = jnp.concatenate([wo_own, swap(wo_own, "tp", 2)], 1)
    wo_side = swap(wo_pair, "tp", 1)
    wo_all = by_rows(jnp.concatenate(
        [wo_pair[:, :heads_wide], wo_side[:, :heads_wide], wo_pair[:, heads_wide:], wo_side[:, heads_wide:]], 1
    ))
    context_near = attend(rank_word, picks, tie(qkv, context_far), marks, True)
    side_context, context_cross = lax.optimization_barrier((context_near[rows_dev:], context_cross))
    context_cat = by_rows(jnp.concatenate(
        [context_near[:rows_dev], swap(side_context, "tp", 1)] + context_cross, 1
    ))
    attn_branch = by_rows(dot_nt(context_cat, wo_all))
    middle = residual_in + attn_branch
    second_own = by_rows(norm_rows(middle, gain_second, shift_second).astype(LOW))
    w_up = [own_all[:, :units], far_all[:, :units]]
    w_down = [own_all[:, units:], far_all[:, units:]]

    second_side = swap(second_own, "tp", 1)
    grad_side = swap(cotangent, "tp", 1)
    hidden, grad_pre, bias_parts = zip(
        feed((second_own, second_side), (cotangent, grad_side), own_all, 0, units, bias_up[0]),
        feed((second_own, second_side), (cotangent, grad_side), far_all, 0, units, bias_up[1]),
    )
    side_terms = dot_nt(grad_pre[0][rows_dev:], w_up[0]) + dot_nt(grad_pre[1][rows_dev:], w_up[1])
    side_back = swap(by_rows(side_terms.astype(LOW)), "tp", 1)
    own_terms = dot_nt(grad_pre[0][:rows_dev], w_up[0]) + dot_nt(grad_pre[1][:rows_dev], w_up[1])
    second_two = jnp.concatenate([second_own, second_side], 0)
    grad_two = jnp.concatenate([cotangent, grad_side], 0)
    share = by_rows(jnp.concatenate(
        [dot_tn(second_two, grad_pre[half]).astype(LOW) for half in range(2)]
        + [dot_tn(grad_two, hidden[half]).astype(LOW) for half in range(2)],
        1,
    ))
    grad_middle, grad_attn, second_sums = norm_back(middle, gain_second, cotangent, (by_rows(own_terms), side_back), True)

    grad_context_cat = dot_nn(grad_attn, wo_all).astype(LOW)
    grad_parts = [grad_context_cat[:, k * heads_wide : (k + 1) * heads_wide] for k in range(4)]
    grad_far = jnp.concatenate([swap(grad_parts[2], "tp", 2), swap(grad_parts[3], "tp", 3)], 0)
    grad_near = jnp.concatenate([grad_parts[0], swap(grad_parts[1], "tp", 1)], 0)
    out_terms = by_rows(dot_tn(grad_attn, context_cat))
    out_near = [out_terms[:, k * heads_wide : (k + 1) * heads_wide] for k in range(4)]
    out_chip = [
        out_near[k] + swap(out_near[k + 1].astype(LOW), "tp", 1).astype(F32) for k in (0, 2)
    ]
    out_sum = out_chip[0] + swap(out_chip[1].astype(LOW), "tp", 2).astype(F32)
    grad_near, share, out_terms = lax.optimization_barrier((grad_near, share, out_terms))
    share = lax.psum_scatter(share, "fsdp", scatter_dimension=0, tiled=True)
    near_parts = attend_back_near(rank_word, picks, qkv, grad_near, marks)
    out_sum, grad_far, near_parts = lax.optimization_barrier((out_sum, grad_far, near_parts))
    grad_qkv = attend_back_far(rank_word, picks, qkv, grad_far, marks, near_parts)
    far_side = by_rows(dot_nt(grad_qkv[3 * rows_dev :], w_qkv).astype(LOW))
    far_own = by_rows(dot_nt(grad_qkv[2 * rows_dev : 3 * rows_dev], w_qkv))
    far_side, far_own = lax.optimization_barrier((swap(far_side, "tp", 1), far_own))
    far_low = (far_own + far_side.astype(F32)).astype(LOW)
    far_back = swap(far_low, "tp", 2)

    hidden = tie(hidden, far_low)
    grad_qkv_late = tie(grad_qkv, far_low)
    qkv_terms = by_rows(dot_tn(jnp.concatenate(chunks, 0), grad_qkv_late))
    near_side = by_rows(dot_nt(grad_qkv_late[rows_dev : 2 * rows_dev], w_qkv).astype(LOW))
    near_own = by_rows(dot_nt(grad_qkv_late[:rows_dev], w_qkv))
    near_back = swap(near_side, "tp", 1)
    down_side = dot_nt(hidden[0][rows_dev:], w_down[0]) + dot_nt(hidden[1][rows_dev:], w_down[1])
    down_own = dot_nt(hidden[0][:rows_dev], w_down[0]) + dot_nt(hidden[1][:rows_dev], w_down[1])
    down_back = swap(by_rows(down_side.astype(LOW)), "tp", 1)
    ffn_branch = by_rows(down_own) + down_back.astype(F32) + bias_fc2.astype(F32)
    output_rows = by_rows((middle + ffn_branch).astype(LOW))
    bias_terms = [jnp.sum(parts, axis=0) for parts in bias_parts]
    grad_bias_up = bias_terms[0] + swap(bias_terms[1], "tp", 2)
    square_rows = jnp.stack(
        [
            jnp.sum(valid_rows * branch * branch)
            for branch in (residual_in, attn_branch, middle, ffn_branch)
        ]
        + [jnp.sum(valid_rows)]
    )
    square_rows = jnp.pad(square_rows[None], ((0, 0), (0, width_model - 5)))

    (collected, grad_w_o), (far_back, output_rows, square_rows, share, near_back) = collect_rows(
        [qkv_terms, out_sum], (far_back, output_rows, square_rows, share, near_back)
    )
    share = share.astype(F32)
    across = jnp.concatenate([share[:, units : 2 * units], share[:, 3 * units :]], 1)
    across = swap(across.astype(LOW), "tp", 2).astype(F32)
    grad_w_up = share[:, :units] + across[:, :units]
    grad_w_down = (share[:, 2 * units : 3 * units] + across[:, units:]).T
    grad_w_q = collected[:, :heads_wide] * scale_query
    grad_w_k = collected[:, heads_wide : 2 * heads_wide]
    grad_w_v = collected[:, 2 * heads_wide :]
    grad_w_o = grad_w_o.T
    grad_input, first_sums = norm_back(hidden_in, gain_first, grad_middle, (near_own, near_back, far_back), False)

    sums = jnp.concatenate([second_sums[:3], square_rows, first_sums[:2]])
    sums = total_over(sums, "tp")
    bias_rows = grad_bias_up.reshape(-1, width_model)
    sums = total_over(jnp.concatenate([sums, bias_rows]), "fsdp")
    residual_rms = jnp.sqrt(sums[3, :4] / (sums[3, 4] * width_model))
    return (
        output_rows,
        grad_input,
        sums[4],
        sums[5],
        grad_w_q,
        grad_w_k,
        grad_w_v,
        grad_w_o,
        sums[0],
        sums[1],
        grad_w_up,
        sums[6:].reshape(-1),
        grad_w_down,
        sums[2],
        residual_rms,
    )


def solution(mesh):
    in_specs = (
        P(("fsdp", "tp"), None),
        P(("fsdp", "tp"), None),
        P(),
        P(),
        P("fsdp", "tp"),
        P("fsdp", "tp"),
        P("fsdp", "tp"),
        P("tp", "fsdp"),
        P(),
        P(),
        P("fsdp", "tp"),
        P("tp"),
        P("tp", "fsdp"),
        P(),
        P("fsdp", None),
        P("fsdp", "tp", None, None),
    )
    out_specs = (
        P(("fsdp", "tp"), None),
        P(("fsdp", "tp"), None),
        P(),
        P(),
        P("fsdp", "tp"),
        P("fsdp", "tp"),
        P("fsdp", "tp"),
        P("tp", "fsdp"),
        P(),
        P(),
        P("fsdp", "tp"),
        P("tp"),
        P("tp", "fsdp"),
        P(),
        P(),
    )
    return jax.shard_map(
        on_device, mesh=mesh, in_specs=in_specs, out_specs=out_specs, check_vma=False
    )
```

time: 799 us -> 551 us (0.69)
  waiting for transfers between devices: 289 us -> 102 us
  Pallas kernels: 128 us -> 211 us
  other arithmetic: 82.5 us -> 32.3 us
  starting transfers between devices: 70.3 us -> 26.1 us
  matrix products: 155 us -> 125 us
  local copies, waits for them, and re-layouts: 62.1 us -> 35.2 us
  between operations: 3.18 us -> 15.5 us
    ppermute x74 -> x35, waiting for transfers between devices: 289 us -> 84.9 us  [swap(): return lax.ppermute(values, axis, [(i, i ^ mask) for i in range(count)])]
    pallas_call x2 -> x10, Pallas kernels: 128 us -> 211 us  [the longest x2 58.4 us: attend(): pl.pallas_call(partial(forward_kernel, heads=heads, rand=rand, span=span,...]
    dot_general x6 -> x5, matrix products: 64.3 us -> 16.1 us  [dot_nn(): lax.dot_general(a, b, (((1,), (0,)), ((), ())), preferred_element_type=F32)]
    ppermute x74 -> x35, starting transfers between devices: 70.3 us -> 25.4 us  [swap(): return lax.ppermute(values, axis, [(i, i ^ mask) for i in range(count)])]
    select_n x24 -> x0, other arithmetic: 25.2 us -> none  [spread_rows(): jnp.where(upper, jnp.stack([other, held], 1), jnp.stack([held, other], 1))]
    reduce_sum x8 -> x3, other arithmetic: 23.1 us -> 2.97 us  [the longest x1 2.94 us: on_device(): jnp.sum(valid_rows * branch * branch)]
    all_gather x0 -> x3, waiting for transfers between devices: none -> 17.5 us  [the longest x1 15.7 us: on_device(): far_all = lax.all_gather(far_local, 'fsdp', axis=0, tiled=True)]
    unnamed x150 -> x111, local copies, waits for them, and re-layouts: 32.3 us -> 15.5 us
  transfers between devices with their start and end apart: 74 -> 39, of which waited for: 26 -> 14; matrix products, arithmetic and copies ran while one was open for 29% -> 30% of each run, Pallas kernels for 16% -> 31%
where the time goes in v2:
time: 551 us; the launch traced here: 547 us
  Pallas kernels  211 us (38%)
  matrix products  125 us (23%)
  waiting for transfers between devices  102 us (19%)
  local copies, waits for them, and re-layouts  35.2 us (6%)
  other arithmetic  32.3 us (6%)
  starting transfers between devices  26.1 us (5%)
  between operations  15.5 us (3%)
    ppermute x35, waiting for transfers between devices, swap(): return lax.ppermute(values, axis, [(i, i ^ mask) for i in range(count)])  84.9 us
    dot_general x13, matrix products, dot_nt(): lax.dot_general(a, b, (((1,), (1,)), ((), ())), preferred_element_type=F32)  59.1 us
    pallas_call x2, Pallas kernels, attend(): pl.pallas_call(partial(forward_kernel, heads=heads, rand=rand, span=span,...  58.4 us
    dot_general x6, matrix products, dot_tn(): lax.dot_general(a, b, (((0,), (0,)), ((), ())), preferred_element_type=F32)  50.2 us
    pallas_call x1, Pallas kernels, attend_back_far(): pl.pallas_call(partial(backward_far, heads=heads, rand=rand, span=span),...  43.3 us
    pallas_call x1, Pallas kernels, attend_back_near(): pl.pallas_call(partial(backward_near, heads=heads, rand=rand, span=span),...  41 us
    pallas_call x2, Pallas kernels, feed(): pl.pallas_call(partial(feed_kernel, step=min(256, rows)), grid=(2, units...  40.3 us
    ppermute x35, starting transfers between devices, swap(): return lax.ppermute(values, axis, [(i, i ^ mask) for i in range(count)])  25.4 us
  transfers between devices with their start and end apart: 39, of which 14 were waited for; matrix products, arithmetic and copies ran while one was open for 30% of the time, Pallas kernels for 31%

profile of v2, /device:TPU:0, one launch (start us, length us, event | category | flops | bytes accessed | tf_op | source)
XLA Modules:
  0.0 547.3 jit_solution(6829332632384899929)
XLA Ops:
  10.7 3.0 collective-permute-start.1
  17.2 2.9 broadcast_in_dim.37.mark_ref
  22.7 4.5 norm.2
  27.3 32.3 %collective-permute-done.1.source_ref = bf16[1024,1024]{1,0:T(8,128)(2,1)S(1)} collective-permute-done((bf16[1024,1024]{1,0:T(8,128)(2,1)}, bf16[1024,1024]{1,0:T(8,128)(2,1)S(1)}, u32[]{:S(2)}, u32[]{:S(2)}) %collective-permute-start.1) | collective-permute-done | bytes 2097184 | tf_op jit(solution)/shard_map/ppermute | solution.py:533
  62.6 4.7 norm.3
  71.2 3.4 convolution_convert_fusion.8
  76.5 3.5 convolution_convert_fusion.7
  80.0 3.4 convolution_convert_fusion.5
  83.4 3.2 pad_maximum_fusion.1.qkv_ref
  87.4 29.2 %attend_far.1 = bf16[2048,256]{1,0:T(8,128)(2,1)} custom-call(s32[1]{0:T(128)} %bitcast.4.rank_ref, s32[744]{0:T(1024)} %reshape_squeeze.2.pick_ref, bf16[4096,768]{1,0:T(8,128)(2,1)} %pad_maximum_fusion.1.qkv_ref, s32[4096,128]{1,0:T(8,128)} %broadcast_in_dim.37.mark_ref, s32[64,256]{1,0:T(8,128)} %tile.9.qmark_ref), custom_call_target="tpu_custom_call" | custom-call | flops 28999999488 | bytes 29000000 | tf_op jit(solution)/shard_map/attend_far/pallas_call | solution.py:337
  122.0 29.2 %attend_near.1 = bf16[2048,256]{1,0:T(8,128)(2,1)} custom-call(s32[1]{0:T(128)} %bitcast.4.rank_ref, s32[744]{0:T(1024)} %reshape_squeeze.2.pick_ref, bf16[4096,768]{1,0:T(8,128)(2,1)} %pad_maximum_fusion.1.qkv_ref, s32[4096,128]{1,0:T(8,128)} %broadcast_in_dim.37.mark_ref, s32[64,256]{1,0:T(8,128)} %tile.9.qmark_ref), custom_call_target="tpu_custom_call" | custom-call | flops 28999999488 | bytes 29000000 | tf_op jit(solution)/shard_map/attend_near/pallas_call | solution.py:337
  155.8 6.9 %fusion.95 = (f32[1024]{0:T(1024)S(1)}, f32[1024,1024]{1,0:T(8,128)S(1)}, f32[1024,1024]{1,0:T(8,128)}) fusion(bf16[1024,1024]{1,0:T(8,128)(2,1)} %source_ref.2, bf16[1024,256]{1,0:T(8,128)(2,1)S(1)} %get-tuple-element.158, bf16[1024,256]{1,0:T(8,128)(2,1)S(1)} %copy-done.12, bf16[1024,256]{1,0:T(8,128)(2,1)S(1)} %get-tuple-element.157, ...), kind=kOutput, calls=%fused_computation.152 | convolution fusion | flops 2167405568 | bytes 14684160 | tf_op jit(solution)/shard_map/dot_general | solution.py:22
  162.7 2.9 fusion.10
  168.0 3.1 constant_dynamic-update-slice_fusion.1
  172.2 3.1 constant_dynamic-update-slice_fusion
  175.3 20.1 %feed.2 = (bf16[2048,1024]{1,0:T(8,128)(2,1)}, bf16[2048,1024]{1,0:T(8,128)(2,1)}, f32[2,1,1024]{2,1,0:T(1,128)}) custom-call(bf16[1024,1024]{1,0:T(8,128)(2,1)} %copy-done.3, bf16[1024,1024]{1,0:T(8,128)(2,1)} %collective-permute-done.9.second_side, bf16[1024,1024]{1,0:T(8,128)(2,1)} %residual_ref.1, bf16[1024,1024]{1,0:T(8,128)(2,1)} %collective-permute-done.10.grad_side, ...), custom_call_target="tpu_custom_call" | custom-call | flops 14000000000 | bytes 14000000 | tf_op jit(solution)/shard_map/feed/pallas_call | solution.py:511
  195.5 8.9 %fusion.33 = bf16[1024,1024]{1,0:T(8,128)(2,1)} fusion(bf16[2048,1024]{1,0:T(8,128)(2,1)} %get-tuple-element.69, bf16[1024,1024]{1,0:T(8,128)(2,1)} %collective-permute-done.9.second_side, bf16[1024,1024]{1,0:T(8,128)(2,1)S(1)} %copy-done.4), kind=kOutput, calls=%fused_computation.48 | convolution fusion | flops 4304404480 | bytes 10485760 | tf_op jit(solution)/shard_map/dot_general | solution.py:26
  204.4 8.1 %convolution_convert_fusion.1 = bf16[1024,1024]{1,0:T(8,128)(2,1)} fusion(bf16[2048,1024]{1,0:T(8,128)(2,1)} %constant_dynamic-update-slice_fusion, bf16[2048,1024]{1,0:T(8,128)(2,1)S(1)} %copy-done.48), kind=kOutput, calls=%fused_computation.51 | convolution fusion | flops 4296015872 | bytes 10485760 | tf_op jit(solution)/shard_map/dot_general | solution.py:26
  212.4 15.7 %all-gather.8.cloned.1.call-done.up_ref.down_ref = bf16[1024,2048]{1,0:T(8,128)(2,1)} async-done(((bf16[128,2048]{1,0:T(8,128)(2,1)}), bf16[1024,2048]{1,0:T(8,128)(2,1)}) %all-gather.8.cloned.1.call-update) | async-done | bytes 4194320 | tf_op jit(solution)/shard_map/all_gather | solution.py:623
  228.2 20.1 %feed.3 = (bf16[2048,1024]{1,0:T(8,128)(2,1)}, bf16[2048,1024]{1,0:T(8,128)(2,1)}, f32[2,1,1024]{2,1,0:T(1,128)}) custom-call(bf16[1024,1024]{1,0:T(8,128)(2,1)} %copy-done.3, bf16[1024,1024]{1,0:T(8,128)(2,1)} %collective-permute-done.9.second_side, bf16[1024,1024]{1,0:T(8,128)(2,1)} %residual_ref.1, bf16[1024,1024]{1,0:T(8,128)(2,1)} %collective-permute-done.10.grad_side, ...), custom_call_target="tpu_custom_call" | custom-call | flops 14000000000 | bytes 14000000 | tf_op jit(solution)/shard_map/feed/pallas_call | solution.py:511
  248.3 4.7 fusion.22
  253.1 2.4 add_convert_fusion.3
  259.0 4.5 fusion.30.rest_0_
  263.4 8.1 %fusion.34 = bf16[1024,1024]{1,0:T(8,128)(2,1)} fusion(bf16[2048,1024]{1,0:T(8,128)(2,1)S(1)} %copy-done.47, bf16[1024,1024]{1,0:T(8,128)(2,1)} %collective-permute-done.9.second_side, bf16[1024,1024]{1,0:T(8,128)(2,1)S(1)} %copy-done.5), kind=kOutput, calls=%fused_computation.49 | convolution fusion | flops 4304404480 | bytes 10485760 | tf_op jit(solution)/shard_map/dot_general | solution.py:26
  271.5 8.0 %convolution_convert_fusion = bf16[1024,1024]{1,0:T(8,128)(2,1)} fusion(bf16[2048,1024]{1,0:T(8,128)(2,1)} %constant_dynamic-update-slice_fusion, bf16[2048,1024]{1,0:T(8,128)(2,1)S(1)} %copy-done.44), kind=kOutput, calls=%fused_computation.50 | convolution fusion | flops 4296015872 | bytes 10485760 | tf_op jit(solution)/shard_map/dot_general | solution.py:26
  280.9 9.2 %norm_back.2 = (f32[1024,1024]{1,0:T(8,128)}, bf16[1024,1024]{1,0:T(8,128)(2,1)}, f32[8,1024]{1,0:T(8,128)}) custom-call(f32[1024,1024]{1,0:T(8,128)} %copy-done, f32[1,1024]{1,0:T(1,128)} %bitcast.167, bf16[1024,1024]{1,0:T(8,128)(2,1)} %residual_ref.1, f32[1024,1024]{1,0:T(8,128)} %fusion.30.rest_0_, bf16[1024,1024]{1,0:T(8,128)(2,1)} %copy-done.43), custom_call_target="tpu_custom_call" | custom-call | flops 7000000000 | bytes 7000000 | tf_op jit(solution)/shard_map/norm_back/pallas_call | solution.py:466
  290.0 3.9 convolution_convert_fusion.2
  296.3 6.4 %fusion.104 = (bf16[1024,1024]{1,0:T(8,128)(2,1)S(1)}, f32[1024,1024]{1,0:T(8,128)}) fusion(bf16[1024,1024]{1,0:T(8,128)(2,1)S(1)} %copy-done.51, bf16[1024,256]{1,0:T(8,128)(2,1)} %collective-permute-done.5, bf16[1024,256]{1,0:T(8,128)(2,1)} %collective-permute-done.4, bf16[1024,256]{1,0:T(8,128)(2,1)} %collective-permute-done.6, ...), kind=kOutput, calls=%fused_computation.161 | convolution fusion | flops 2156920832 | bytes 10485760 | tf_op jit(solution)/shard_map/dot_general | solution.py:26
  303.6 3.8 pad_maximum_fusion
  313.6 41.0 %attend_back_near.1 = (bf16[2048,256]{1,0:T(8,128)(2,1)}, f32[4096,256]{1,0:T(8,128)}, f32[4096,256]{1,0:T(8,128)}) custom-call(s32[1]{0:T(128)} %bitcast.4.rank_ref, s32[744]{0:T(1024)} %reshape_squeeze.2.pick_ref, bf16[4096,768]{1,0:T(8,128)(2,1)} %pad_maximum_fusion.1.qkv_ref, bf16[2048,256]{1,0:T(8,128)(2,1)} %pad_maximum_fusion.13.grad_ref, ...), custom_call_target="tpu_custom_call" | custom-call | flops 40000000000 | bytes 40000000 | tf_op jit(solution)/shard_map/attend_back_near/pallas_call | solution.py:354
  357.0 43.3 %attend_back_far.1 = bf16[4096,768]{1,0:T(8,128)(2,1)} custom-call(s32[1]{0:T(128)} %bitcast.4.rank_ref, s32[744]{0:T(1024)} %reshape_squeeze.2.pick_ref, bf16[4096,768]{1,0:T(8,128)(2,1)} %pad_maximum_fusion.1.qkv_ref, bf16[2048,256]{1,0:T(8,128)(2,1)} %pad_maximum_fusion.12.grad_ref, s32[4096,128]{1,0:T(8,128)} %broadcast_in_dim.37.mark_ref, ...), custom_call_target="tpu_custom_call" | custom-call | flops 43000000512 | bytes 43000000 | tf_op jit(solution)/shard_map/attend_back_far/pallas_call | solution.py:370
  400.3 4.6 convolution_convert_fusion.4
  405.9 2.8 collective-permute-done.27
  408.8 3.7 fusion.51
  416.7 2.4 fusion.16
  420.2 3.8 add_convert_fusion.1
  424.0 10.8 %fusion = f32[1024,768]{1,0:T(8,128)S(1)} fusion(bf16[4096,768]{1,0:T(8,128)(2,1)} %attend_back_far.1, bf16[1024,1024]{1,0:T(8,128)(2,1)} %collective-permute-done.2, bf16[1024,1024]{1,0:T(8,128)(2,1)S(1)} %copy-done.41, bf16[1024,1024]{1,0:T(8,128)(2,1)} %collective-permute-done, bf16[1024,1024]{1,0:T(8,128)(2,1)S(1)} %copy-done.39), kind=kOutput, calls=%fused_computation | convolution fusion | flops 6476005376 | bytes 17825792 | tf_op jit(solution)/shard_map/dot_general | solution.py:26
  436.3 4.9 convolution_convert_fusion.3
  442.4 4.4 fusion.20
  446.8 5.3 fusion.54.rest_0_
  452.0 8.7 %collective-permute-done.20 = bf16[4,128,1024]{2,1,0:T(8,128)(2,1)S(1)} collective-permute-done((bf16[4,128,1024]{2,1,0:T(8,128)(2,1)S(1)}, bf16[4,128,1024]{2,1,0:T(8,128)(2,1)S(1)}, u32[]{:S(2)}, u32[]{:S(2)}) %collective-permute-start.20) | collective-permute-done | bytes 1048608 | tf_op jit(solution)/shard_map/ppermute | solution.py:533
  461.1 9.1 %fusion.11 = (f32[]{:T(128)}, f32[]{:T(128)}, f32[]{:T(128)}, bf16[1024,1024]{1,0:T(8,128)(2,1)}) fusion(f32[1024]{0:T(1024)S(1)} %bitcast.166, f32[1024,1024]{1,0:T(8,128)} %get-tuple-element.168, bf16[1024,1024]{1,0:T(8,128)(2,1)S(1)} %copy-done.38, f32[1024,1024]{1,0:T(8,128)S(1)} %copy-done.1, f32[1024]{0:T(1024)S(1)} %convert_element_type.209, ...), kind=kOutput, calls=%fused_computation.18 | convolution fusion | flops 2164260864 | bytes 23076876 | tf_op jit(solution)/shard_map/dot_general | solution.py:22
  470.2 3.2 stack.23
  473.4 16.2 %collective-permute-done.21.rest_2_ = bf16[1024,1024]{1,0:T(8,128)(2,1)} collective-permute-done((bf16[1024,1024]{1,0:T(8,128)(2,1)}, bf16[1024,1024]{1,0:T(8,128)(2,1)}, u32[]{:S(2)}, u32[]{:S(2)}) %collective-permute-start.21) | collective-permute-done | bytes 2097184 | tf_op jit(solution)/shard_map/ppermute | solution.py:533
  489.6 9.3 %norm_back.3 = (f32[1024,1024]{1,0:T(8,128)}, f32[8,1024]{1,0:T(8,128)}) custom-call(bf16[1024,1024]{1,0:T(8,128)(2,1)} %source_ref.2, f32[1,1024]{1,0:T(1,128)} %bitcast.178, f32[1024,1024]{1,0:T(8,128)} %get-tuple-element.91.residual_ref, f32[1024,1024]{1,0:T(8,128)} %fusion.54.rest_0_, bf16[1024,1024]{1,0:T(8,128)(2,1)} %collective-permute-done.23.rest_1_, ...), custom_call_target="tpu_custom_call" | custom-call | flops 7000000000 | bytes 7000000 | tf_op jit(solution)/shard_map/norm_back/pallas_call | solution.py:466
  505.5 2.8 collective-permute-done.28
  519.3 6.9 %collective-permute-done.32 = bf16[2,128,1024]{2,1,0:T(8,128)(2,1)S(1)} collective-permute-done((bf16[2,128,1024]{2,1,0:T(8,128)(2,1)S(1)}, bf16[2,128,1024]{2,1,0:T(8,128)(2,1)S(1)}, u32[]{:S(2)}, u32[]{:S(2)}) %collective-permute-start.32) | collective-permute-done | bytes 524320 | tf_op jit(solution)/shard_map/ppermute | solution.py:533
  529.2 9.8 %collective-permute-done.33 = bf16[1,128,1024]{2,1,0:T(8,128)(2,1)S(1)} collective-permute-done((bf16[1,128,1024]{2,1,0:T(8,128)(2,1)S(1)}, bf16[1,128,1024]{2,1,0:T(8,128)(2,1)S(1)}, u32[]{:S(2)}, u32[]{:S(2)}) %collective-permute-start.33) | collective-permute-done | bytes 262176 | tf_op jit(solution)/shard_map/ppermute | solution.py:533
  (253 shorter events, 79.9 us)
Async XLA Ops:
  7.2 55.4 %all-gather.4.cloned.1.call-start = ((), (), s32[]{:S(2)}) async-start(), calls=%async_computation.1 | async-start | bytes 2359296 | tf_op jit(solution)/shard_map/all_gather | solution.py:606
  10.6 164.7 %all-gather.6.cloned.1.call-start = ((), (), s32[]{:S(2)}) async-start(), calls=%async_computation.2 | async-start | bytes 4718592 | tf_op jit(solution)/shard_map/all_gather | solution.py:609
  10.7 48.9 %collective-permute-start.1 = (bf16[1024,1024]{1,0:T(8,128)(2,1)}, bf16[1024,1024]{1,0:T(8,128)(2,1)S(1)}, u32[]{:S(2)}, u32[]{:S(2)}) collective-permute-start(bf16[1024,1024]{1,0:T(8,128)(2,1)} %source_ref.2), channel_id=1, source_target_pairs={{0,2},{1,3},{2,0},{3,1},{4,6},{5,7},{6,4},{7,5},{8,10},{9,11},{10,... | collective-permute-start | bytes 6291464 | tf_op jit(solution)/shard_map/ppermute | solution.py:533
  27.2 40.1 %copy-start.18 = (bf16[1024,128]{1,0:T(8,128)(2,1)S(1)}, bf16[1024,128]{1,0:T(8,128)(2,1)}, u32[]{:S(2)}) copy-start(bf16[1024,128]{1,0:T(8,128)(2,1)} %param.28) | copy-start | bytes 786436
  27.2 40.2 %copy-start.19 = (bf16[128,1024]{1,0:T(8,128)(2,1)S(1)}, bf16[128,1024]{1,0:T(8,128)(2,1)}, u32[]{:S(2)}) copy-start(bf16[128,1024]{1,0:T(8,128)(2,1)} %param.26) | copy-start | bytes 786436
  27.2 41.6 %copy-start.29 = (s32[1,4,62,3]{2,1,3,0:T(4,128)S(1)}, s32[1,4,62,3]{2,1,3,0:T(4,128)}, u32[]{:S(2)}) copy-start(s32[1,4,62,3]{2,1,3,0:T(4,128)} %param.31) | copy-start | bytes 8932
  27.2 49.3 %collective-permute-start = (bf16[1024,1024]{1,0:T(8,128)(2,1)}, bf16[1024,1024]{1,0:T(8,128)(2,1)}, u32[]{:S(2)}, u32[]{:S(2)}) collective-permute-start(bf16[1024,1024]{1,0:T(8,128)(2,1)} %norm.2), channel_id=1, source_target_pairs={{0,1},{1,0},{2,3},{3,2},{4,5},{5,4},{6,7},{7,6},{8,9},{9,8},{10,11... | collective-permute-start | bytes 6291464 | tf_op jit(solution)/shard_map/ppermute | solution.py:533
  67.3 12.8 %collective-permute-start.2 = (bf16[1024,1024]{1,0:T(8,128)(2,1)}, bf16[1024,1024]{1,0:T(8,128)(2,1)}, u32[]{:S(2)}, u32[]{:S(2)}) collective-permute-start(bf16[1024,1024]{1,0:T(8,128)(2,1)} %norm.3), channel_id=1, source_target_pairs={{0,1},{1,0},{2,3},{3,2},{4,5},{5,4},{6,7},{7,6},{8,9},{9,8},{10,11... | collective-permute-start | bytes 6291464 | tf_op jit(solution)/shard_map/ppermute | solution.py:533
  68.3 159.9 %all-gather.8.cloned.1.call-start = ((), (), s32[]{:S(2)}) async-start(), calls=%async_computation.3 | async-start | bytes 4718592 | tf_op jit(solution)/shard_map/all_gather | solution.py:623
  69.8 16.9 %collective-permute-start.3 = (bf16[128,2048]{1,0:T(8,128)(2,1)}, bf16[128,2048]{1,0:T(8,128)(2,1)S(1)}, u32[]{:S(2)}, u32[]{:S(2)}) collective-permute-start(bf16[128,2048]{1,0:T(8,128)(2,1)} %pad_maximum_fusion.15), channel_id=1, source_target_pairs={{0,2},{1,3},{2,0},{3,1},{4,6},{5,7},{6,4},{7,5},{8,10},{9,11},{10,... | collective-permute-start | bytes 1572872 | tf_op jit(solution)/shard_map/ppermute | solution.py:533
  86.7 30.0 %copy-start.10 = (bf16[128,2048]{1,0:T(8,128)(2,1)}, bf16[128,2048]{1,0:T(8,128)(2,1)S(1)}, u32[]{:S(2)}) copy-start(bf16[128,2048]{1,0:T(8,128)(2,1)S(1)} %collective-permute-done.3) | copy-start | bytes 1572868
  86.7 33.6 %collective-permute-start.7 = (bf16[1024,256]{1,0:T(8,128)(2,1)S(1)}, bf16[1024,256]{1,0:T(8,128)(2,1)S(1)}, u32[]{:S(2)}, u32[]{:S(2)}) collective-permute-start(bf16[1024,256]{1,0:T(8,128)(2,1)S(1)} %slice.228), channel_id=1, source_target_pairs={{0,2},{1,3},{2,0},{3,1},{4,6},{5,7},{6,4},{7,5},{8,10},{9,11},{10,... | collective-permute-start | bytes 1572872 | tf_op jit(solution)/shard_map/ppermute | solution.py:533
  118.9 34.6 %collective-permute-start.4 = (bf16[1024,256]{1,0:T(8,128)(2,1)}, bf16[1024,256]{1,0:T(8,128)(2,1)}, u32[]{:S(2)}, u32[]{:S(2)}) collective-permute-start(bf16[1024,256]{1,0:T(8,128)(2,1)} %get-tuple-element.156), channel_id=1, source_target_pairs={{0,2},{1,3},{2,0},{3,1},{4,6},{5,7},{6,4},{7,5},{8,10},{9,11},{10,... | collective-permute-start | bytes 1572872 | tf_op jit(solution)/shard_map/ppermute | solution.py:533
  120.3 33.2 %collective-permute-start.5 = (bf16[1024,256]{1,0:T(8,128)(2,1)}, bf16[1024,256]{1,0:T(8,128)(2,1)}, u32[]{:S(2)}, u32[]{:S(2)}) collective-permute-start(bf16[1024,256]{1,0:T(8,128)(2,1)} %get-tuple-element.155), channel_id=1, source_target_pairs={{0,3},{1,2},{2,1},{3,0},{4,7},{5,6},{6,5},{7,4},{8,11},{9,10},{10,... | collective-permute-start | bytes 1572872 | tf_op jit(solution)/shard_map/ppermute | solution.py:533
  121.2 32.9 %copy-start.30 = (bf16[1024]{0:T(1024)(128)(2,1)S(1)}, bf16[1024]{0:T(1024)(128)(2,1)}, u32[]{:S(2)}) copy-start(bf16[1024]{0:T(1024)(128)(2,1)} %param.24) | copy-start | bytes 6148
  121.2 32.9 %copy-start.31 = (bf16[1024]{0:T(1024)(128)(2,1)S(1)}, bf16[1024]{0:T(1024)(128)(2,1)}, u32[]{:S(2)}) copy-start(bf16[1024]{0:T(1024)(128)(2,1)} %param.25) | copy-start | bytes 6148
  121.2 34.4 %collective-permute-start.8 = (bf16[1024,512]{1,0:T(8,128)(2,1)S(1)}, bf16[1024,512]{1,0:T(8,128)(2,1)S(1)}, u32[]{:S(2)}, u32[]{:S(2)}) collective-permute-start(bf16[1024,512]{1,0:T(8,128)(2,1)S(1)} %pad_maximum_fusion.11), channel_id=1, source_target_pairs={{0,1},{1,0},{2,3},{3,2},{4,5},{5,4},{6,7},{7,6},{8,9},{9,8},{10,11... | collective-permute-start | bytes 3145736 | tf_op jit(solution)/shard_map/ppermute | solution.py:533
  153.5 2.3 collective-permute-start.6
  153.6 18.7 %collective-permute-start.10 = (bf16[1024,1024]{1,0:T(8,128)(2,1)}, bf16[1024,1024]{1,0:T(8,128)(2,1)}, u32[]{:S(2)}, u32[]{:S(2)}) collective-permute-start(bf16[1024,1024]{1,0:T(8,128)(2,1)} %residual_ref.1), channel_id=1, source_target_pairs={{0,1},{1,0},{2,3},{3,2},{4,5},{5,4},{6,7},{7,6},{8,9},{9,8},{10,11... | collective-permute-start | bytes 6291464 | tf_op jit(solution)/shard_map/ppermute | solution.py:533
  155.5 334.1 %reduce-scatter.2.cloned.1.call-start = ((), (), s32[]{:S(2)}) async-start(), calls=%async_computation.4 | async-start | bytes 9437184 | tf_op jit(solution)/shard_map/reduce_scatter | solution.py:672
  166.4 8.9 %collective-permute-start.9 = (bf16[1024,1024]{1,0:T(8,128)(2,1)S(1)}, bf16[1024,1024]{1,0:T(8,128)(2,1)}, u32[]{:S(2)}, u32[]{:S(2)}) collective-permute-start(bf16[1024,1024]{1,0:T(8,128)(2,1)S(1)} %add_convert_fusion.4.second_own), channel_id=1, source_target_pairs={{0,1},{1,0},{2,3},{3,2},{4,5},{5,4},{6,7},{7,6},{8,9},{9,8},{10,11... | collective-permute-start | bytes 6291464 | tf_op jit(solution)/shard_map/ppermute | solution.py:533
  166.6 5.1 collective-permute-start.11
  175.3 20.2 %copy-start.4 = (bf16[1024,1024]{1,0:T(8,128)(2,1)S(1)}, bf16[1024,1024]{1,0:T(8,128)(2,1)}, u32[]{:S(2)}) copy-start(bf16[1024,1024]{1,0:T(8,128)(2,1)} %copy-done.3) | copy-start | bytes 6291460
  255.5 24.0 %collective-permute-start.12 = (bf16[1024,1024]{1,0:T(8,128)(2,1)S(1)}, bf16[1024,1024]{1,0:T(8,128)(2,1)S(1)}, u32[]{:S(2)}, u32[]{:S(2)}) collective-permute-start(bf16[1024,1024]{1,0:T(8,128)(2,1)S(1)} %add_convert_fusion.3), channel_id=1, source_target_pairs={{0,1},{1,0},{2,3},{3,2},{4,5},{5,4},{6,7},{7,6},{8,9},{9,8},{10,11... | collective-permute-start | bytes 6291464 | tf_op jit(solution)/shard_map/ppermute | solution.py:533
  295.2 14.3 %collective-permute-start.18 = (bf16[1024,256]{1,0:T(8,128)(2,1)}, bf16[1024,256]{1,0:T(8,128)(2,1)S(1)}, u32[]{:S(2)}, u32[]{:S(2)}) collective-permute-start(bf16[1024,256]{1,0:T(8,128)(2,1)} %get-tuple-element.146), channel_id=1, source_target_pairs={{0,1},{1,0},{2,3},{3,2},{4,5},{5,4},{6,7},{7,6},{8,9},{9,8},{10,11... | collective-permute-start | bytes 1572872 | tf_op jit(solution)/shard_map/ppermute | solution.py:533
  303.6 7.0 %collective-permute-start.14 = (bf16[1024,256]{1,0:T(8,128)(2,1)}, bf16[1024,256]{1,0:T(8,128)(2,1)}, u32[]{:S(2)}, u32[]{:S(2)}) collective-permute-start(bf16[1024,256]{1,0:T(8,128)(2,1)} %get-tuple-element.150), channel_id=1, source_target_pairs={{0,1},{1,0},{2,3},{3,2},{4,5},{5,4},{6,7},{7,6},{8,9},{9,8},{10,11... | collective-permute-start | bytes 1572872 | tf_op jit(solution)/shard_map/ppermute | solution.py:533
  307.3 47.2 %collective-permute-start.16 = (bf16[1024,256]{1,0:T(8,128)(2,1)}, bf16[1024,256]{1,0:T(8,128)(2,1)S(1)}, u32[]{:S(2)}, u32[]{:S(2)}) collective-permute-start(bf16[1024,256]{1,0:T(8,128)(2,1)} %get-tuple-element.148), channel_id=1, source_target_pairs={{0,2},{1,3},{2,0},{3,1},{4,6},{5,7},{6,4},{7,5},{8,10},{9,11},{10,... | collective-permute-start | bytes 1572872 | tf_op jit(solution)/shard_map/ppermute | solution.py:533
  308.8 45.8 %collective-permute-start.17 = (bf16[1024,256]{1,0:T(8,128)(2,1)}, bf16[1024,256]{1,0:T(8,128)(2,1)S(1)}, u32[]{:S(2)}, u32[]{:S(2)}) collective-permute-start(bf16[1024,256]{1,0:T(8,128)(2,1)} %get-tuple-element.147), channel_id=1, source_target_pairs={{0,3},{1,2},{2,1},{3,0},{4,7},{5,6},{6,5},{7,4},{8,11},{9,10},{10,... | collective-permute-start | bytes 1572872 | tf_op jit(solution)/shard_map/ppermute | solution.py:533
  309.2 46.4 %collective-permute-start.13 = (bf16[1024,256]{1,0:T(8,128)(2,1)S(1)}, bf16[1024,256]{1,0:T(8,128)(2,1)S(1)}, u32[]{:S(2)}, u32[]{:S(2)}) collective-permute-start(bf16[1024,256]{1,0:T(8,128)(2,1)S(1)} %get-tuple-element.149), channel_id=1, source_target_pairs={{0,1},{1,0},{2,3},{3,2},{4,5},{5,4},{6,7},{7,6},{8,9},{9,8},{10,11... | collective-permute-start | bytes 1572872 | tf_op jit(solution)/shard_map/ppermute | solution.py:533
  312.0 43.6 %collective-permute-start.15 = (bf16[1024,256]{1,0:T(8,128)(2,1)S(1)}, bf16[1024,256]{1,0:T(8,128)(2,1)S(1)}, u32[]{:S(2)}, u32[]{:S(2)}) collective-permute-start(bf16[1024,256]{1,0:T(8,128)(2,1)S(1)} %fusion.61), channel_id=1, source_target_pairs={{0,2},{1,3},{2,0},{3,1},{4,6},{5,7},{6,4},{7,5},{8,10},{9,11},{10,... | collective-permute-start | bytes 1572872 | tf_op jit(solution)/shard_map/ppermute | solution.py:533
  357.0 43.3 %copy-start.21 = (bf16[1024,1024]{1,0:T(8,128)(2,1)S(1)}, bf16[1024,1024]{1,0:T(8,128)(2,1)}, u32[]{:S(2)}) copy-start(bf16[1024,1024]{1,0:T(8,128)(2,1)} %all-gather.4.cloned.1.call-done) | copy-start | bytes 6291460
  405.0 7.5 %collective-permute-start.19 = (bf16[1024,1024]{1,0:T(8,128)(2,1)}, bf16[1024,1024]{1,0:T(8,128)(2,1)S(1)}, u32[]{:S(2)}, u32[]{:S(2)}) collective-permute-start(bf16[1024,1024]{1,0:T(8,128)(2,1)} %convolution_convert_fusion.4), channel_id=1, source_target_pairs={{0,1},{1,0},{2,3},{3,2},{4,5},{5,4},{6,7},{7,6},{8,9},{9,8},{10,11... | collective-permute-start | bytes 6291464 | tf_op jit(solution)/shard_map/ppermute | solution.py:533
  405.0 3.7 collective-permute-start.27
  424.0 37.1 %collective-permute-start.22 = (bf16[1024,1024]{1,0:T(8,128)(2,1)}, bf16[1024,1024]{1,0:T(8,128)(2,1)}, u32[]{:S(2)}, u32[]{:S(2)}) collective-permute-start(bf16[1024,1024]{1,0:T(8,128)(2,1)} %add_convert_fusion.1), channel_id=1, source_target_pairs={{0,1},{1,0},{2,3},{3,2},{4,5},{5,4},{6,7},{7,6},{8,9},{9,8},{10,11... | collective-permute-start | bytes 6291464 | tf_op jit(solution)/shard_map/ppermute | solution.py:533
  435.0 25.6 %collective-permute-start.20 = (bf16[4,128,1024]{2,1,0:T(8,128)(2,1)S(1)}, bf16[4,128,1024]{2,1,0:T(8,128)(2,1)S(1)}, u32[]{:S(2)}, u32[]{:S(2)}) collective-permute-start(bf16[4,128,1024]{2,1,0:T(8,128)(2,1)S(1)} %pad_maximum_fusion.14), channel_id=1, source_target_pairs={{0,4},{4,0},{8,12},{12,8},{16,20},{20,16},{24,28},{28,24},{1,5},{5... | collective-permute-start | bytes 3145736 | tf_op jit(solution)/shard_map/ppermute | solution.py:533
  441.3 48.4 %collective-permute-start.21 = (bf16[1024,1024]{1,0:T(8,128)(2,1)}, bf16[1024,1024]{1,0:T(8,128)(2,1)}, u32[]{:S(2)}, u32[]{:S(2)}) collective-permute-start(bf16[1024,1024]{1,0:T(8,128)(2,1)} %add_convert_fusion.2), channel_id=1, source_target_pairs={{0,2},{1,3},{2,0},{3,1},{4,6},{5,7},{6,4},{7,5},{8,10},{9,11},{10,... | collective-permute-start | bytes 6291464 | tf_op jit(solution)/shard_map/ppermute | solution.py:533
  442.1 31.3 %collective-permute-start.23 = (bf16[1024,1024]{1,0:T(8,128)(2,1)}, bf16[1024,1024]{1,0:T(8,128)(2,1)}, u32[]{:S(2)}, u32[]{:S(2)}) collective-permute-start(bf16[1024,1024]{1,0:T(8,128)(2,1)} %convolution_convert_fusion.3), channel_id=1, source_target_pairs={{0,1},{1,0},{2,3},{3,2},{4,5},{5,4},{6,7},{7,6},{8,9},{9,8},{10,11... | collective-permute-start | bytes 6291464 | tf_op jit(solution)/shard_map/ppermute | solution.py:533
  489.6 12.0 %copy-start.2 = (bf16[128,4096]{1,0:T(8,128)(2,1)S(1)}, bf16[128,4096]{1,0:T(8,128)(2,1)}, u32[]{:S(2)}) copy-start(bf16[128,4096]{1,0:T(8,128)(2,1)} %reduce-scatter.2.cloned.1.call-done) | copy-start | bytes 3145732
  499.7 3.0 collective-permute-start.24
  499.8 4.1 collective-permute-start.25
  500.7 3.5 collective-permute-start.26
  501.7 25.4 %collective-permute-start.34 = (bf16[128,2048]{1,0:T(8,128)(2,1)S(1)}, bf16[128,2048]{1,0:T(8,128)(2,1)S(1)}, u32[]{:S(2)}, u32[]{:S(2)}) collective-permute-start(bf16[128,2048]{1,0:T(8,128)(2,1)S(1)} %pad_maximum_fusion.17), channel_id=1, source_target_pairs={{0,2},{1,3},{2,0},{3,1},{4,6},{5,7},{6,4},{7,5},{8,10},{9,11},{10,... | collective-permute-start | bytes 1572872 | tf_op jit(solution)/shard_map/ppermute | solution.py:533
  504.3 4.0 collective-permute-start.28
  508.2 4.8 collective-permute-start.29
  509.4 5.5 %collective-permute-start.30 = (f32[7,1024]{1,0:T(8,128)S(1)}, f32[7,1024]{1,0:T(8,128)S(1)}, u32[]{:S(2)}, u32[]{:S(2)}) collective-permute-start(f32[7,1024]{1,0:T(8,128)S(1)} %fusion.118), channel_id=1, source_target_pairs={{0,16},{4,20},{8,24},{12,28},{16,0},{20,4},{24,8},{28,12},{1,17},{... | collective-permute-start | bytes 86024 | tf_op jit(solution)/shard_map/ppermute | solution.py:533
  510.8 6.1 %collective-permute-start.31 = (f32[7,1024]{1,0:T(8,128)S(1)}, f32[7,1024]{1,0:T(8,128)S(1)}, u32[]{:S(2)}, u32[]{:S(2)}) collective-permute-start(f32[7,1024]{1,0:T(8,128)S(1)} %fusion.118), channel_id=1, source_target_pairs={{0,24},{4,28},{8,16},{12,20},{16,8},{20,12},{24,0},{28,4},{1,25},{... | collective-permute-start | bytes 86024 | tf_op jit(solution)/shard_map/ppermute | solution.py:533
  512.8 13.4 %collective-permute-start.32 = (bf16[2,128,1024]{2,1,0:T(8,128)(2,1)S(1)}, bf16[2,128,1024]{2,1,0:T(8,128)(2,1)S(1)}, u32[]{:S(2)}, u32[]{:S(2)}) collective-permute-start(bf16[2,128,1024]{2,1,0:T(8,128)(2,1)S(1)} %pad_maximum_fusion.16), channel_id=1, source_target_pairs={{0,8},{4,12},{8,0},{12,4},{16,24},{20,28},{24,16},{28,20},{1,9},{5... | collective-permute-start | bytes 1572872 | tf_op jit(solution)/shard_map/ppermute | solution.py:533
  526.4 12.6 %collective-permute-start.33 = (bf16[1,128,1024]{2,1,0:T(8,128)(2,1)S(1)}, bf16[1,128,1024]{2,1,0:T(8,128)(2,1)S(1)}, u32[]{:S(2)}, u32[]{:S(2)}) collective-permute-start(bf16[1,128,1024]{2,1,0:T(8,128)(2,1)S(1)} %pad_maximum_fusion.23), channel_id=1, source_target_pairs={{0,16},{4,20},{8,24},{12,28},{16,0},{20,4},{24,8},{28,12},{1,17},{... | collective-permute-start | bytes 786440 | tf_op jit(solution)/shard_map/ppermute | solution.py:533
  (43 other events, 241.4 us)
Sparse Core Ops, SparseCore 0:
  10.8 51.7 all-gather.3
  68.4 72.6 all-gather.5
  155.6 72.5 all-gather.7
  313.7 145.1 reduce-scatter.1
